TPU v7x, 32 devices: a whole 2x2x4 slice. The times are simulated.
32 devices in a mesh: wide: 16 (over z, y, x), narrow: 2 (over core).
Axes of the slice: x: 2, y: 2, z: 4, core: 2. Of those that a mesh axis runs over, the one named last changes fastest.
Arguments:
- tokens: bfloat16 [16384, 768], P(('wide', 'narrow')), may hold values from -6 to 6
- plot_slot: int32 [16384], P('wide'), may hold values from 0 to 1, as said below
- patch_mask: int32 [16384], P('wide'), may hold values from 0 to 1, as said below
- cotangent: bfloat16 [16384, 768], P(('wide', 'narrow')), may hold values from -6 to 6
- gain_attn: float32 [768], replicated, may hold values from 0.5 to 1.5
- w_qkv: bfloat16 [3, 768, 768], P(None, None, 'narrow'), may hold values from -0.21875 to 0.21875
- w_out: bfloat16 [768, 768], P('narrow'), may hold values from -2.5 to 2.5
- gain_mlp: float32 [768], replicated, may hold values from 0.5 to 1.5
- w_gu: bfloat16 [2, 768, 2048], P(None, None, 'narrow'), may hold values from -0.21875 to 0.21875
- w_down: bfloat16 [2048, 768], P('narrow'), may hold values from -0.125 to 0.125
- qkv_rows: float32 [3, 768], replicated, may hold values from 16.384 to 1638.4
- qkv_cols: float32 [3, 768], P(None, 'narrow'), may hold values from 16.384 to 1638.4
- out_rows: float32 [768], P('narrow'), may hold values from 16.384 to 1638.4
- out_cols: float32 [768], replicated, may hold values from 16.384 to 1638.4
- gu_rows: float32 [2, 768], replicated, may hold values from 16.384 to 1638.4
- gu_cols: float32 [2, 2048], P(None, 'narrow'), may hold values from 16.384 to 1638.4
- down_rows: float32 [2048], P('narrow'), may hold values from 16.384 to 1638.4
- down_cols: float32 [768], replicated, may hold values from 16.384 to 1638.4
- step_count: int32 [], replicated, may hold values from 4 to 399
- learn_rate: float32 [], replicated, may hold values from 0.02 to 0.2
Outputs:
- mixed_out: bfloat16 [16384, 768], P(('wide', 'narrow'))
- tokens_grad: float32 [16384, 768], P(('wide', 'narrow'))
- gain_attn_grad: float32 [768], P('wide')
- qkv_grad: float32 [3, 768, 768], P(None, 'wide', 'narrow')
- out_grad: float32 [768, 768], P('narrow', 'wide')
- gain_mlp_grad: float32 [768], P('wide')
- gu_grad: float32 [2, 768, 2048], P(None, 'wide', 'narrow')
- down_grad: float32 [2048, 768], P('narrow', 'wide')
- qkv_new: bfloat16 [3, 768, 768], P(None, 'wide', 'narrow')
- out_new: bfloat16 [768, 768], P('narrow', 'wide')
- gu_new: bfloat16 [2, 768, 2048], P(None, 'wide', 'narrow')
- down_new: bfloat16 [2048, 768], P('narrow', 'wide')
- qkv_rows_new: float32 [3, 768], P(None, 'wide')
- qkv_cols_new: float32 [3, 768], P(None, 'narrow')
- out_rows_new: float32 [768], P('narrow')
- out_cols_new: float32 [768], P('wide')
- gu_rows_new: float32 [2, 768], P(None, 'wide')
- gu_cols_new: float32 [2, 2048], P(None, 'narrow')
- down_rows_new: float32 [2048], P('narrow')
- down_cols_new: float32 [768], P('wide')
Inputs may be any that keep to these rules, and one draw needn't show every extreme that they name: `plot_slot`: within each aligned block of 1024 tokens, plots are numbered from 0 in order; each plot holds 512 or 1024 consecutive tokens and starts at a multiple of 256; some block holds one plot of 1024 tokens and some block holds two plots. `patch_mask`: in each plot the ones form a prefix of at least half of the plot's tokens; the rest of the plot is zero.
All inputs are finite; a program needn't handle non-finite values.
Results may differ from a plain program's by a relative error of at most 0.019.
Values may be sent and summed in bfloat16 or wider, within the bound.
No kernel may reach another device: no remote copies, remote signals or barrier semaphores. Data moves between devices by JAX's collectives and lax.ppermute only.
A program may use at most 128 MiB of HBM per device.

v0:
```python
import math

import jax
import jax.numpy as jnp
from jax import lax
from jax.sharding import PartitionSpec as P

D = 768
DH = 64
FF = 2048
HD = 768
U = 256


EPSILON = 1e-06
TINIEST = 1e-30
NEGATIVE = -1e30


def normed(rows_in, gain_row):
    return (
        rows_in
        * lax.rsqrt(jnp.mean(rows_in * rows_in, axis=-1, keepdims=True) + EPSILON)
        * gain_row
    )


def gelu_gate(paired):
    return jax.nn.gelu(paired[0], approximate=True) * paired[1]


def block_bounds(plot_slot):
    leaders = plot_slot.reshape(-1, U)[:, 0]
    before = jnp.sum((leaders[None, :] < leaders[:, None]).astype(jnp.int32), axis=1)
    through = jnp.sum((leaders[None, :] <= leaders[:, None]).astype(jnp.int32), axis=1)
    return (before, through)


def scores_of(query_rows, key_rows, live_keys):
    head_scale = 1.0 / math.sqrt(query_rows.shape[-1])
    scores = (
        jnp.einsum("qhd,khd->hqk", query_rows, key_rows, preferred_element_type=jnp.float32)
        * head_scale
    )
    return jnp.where(live_keys[None, None, :], scores, NEGATIVE)


def key_slices(key_index, key_all, value_all, key_live):
    offset = key_index * U
    return (
        lax.dynamic_slice_in_dim(key_all, offset, U, 0),
        lax.dynamic_slice_in_dim(value_all, offset, U, 0),
        lax.dynamic_slice_in_dim(key_live, offset, U, 0),
    )


def attention(query_all, key_all, value_all, key_live, before, through):
    block_count = query_all.shape[0] // U
    head_count = query_all.shape[1]

    def per_block(query_index):
        query_rows = lax.dynamic_slice_in_dim(query_all, query_index * U, U, 0)

        def measure(key_index, running):
            running_max, running_sum = running
            key_rows, value_rows, live_keys = key_slices(key_index, key_all, value_all, key_live)
            scores = scores_of(query_rows, key_rows, live_keys)
            new_max = jnp.maximum(running_max, jnp.max(scores, axis=-1))
            running_sum = running_sum * jnp.exp(running_max - new_max) + jnp.sum(
                jnp.exp(scores - new_max[..., None]), axis=-1
            )
            return (new_max, running_sum)

        start_state = (
            jnp.full((head_count, U), NEGATIVE, jnp.float32),
            jnp.zeros((head_count, U), jnp.float32),
        )
        running_max, running_sum = lax.fori_loop(
            before[query_index], through[query_index], measure, start_state
        )
        log_total = running_max + jnp.log(running_sum)

        def weigh(key_index, gathered):
            key_rows, value_rows, live_keys = key_slices(key_index, key_all, value_all, key_live)
            softmax_low = jnp.exp(
                scores_of(query_rows, key_rows, live_keys) - log_total[..., None]
            ).astype(jnp.bfloat16)
            return gathered + jnp.einsum(
                "hqk,khd->qhd", softmax_low, value_rows, preferred_element_type=jnp.float32
            )

        mixed_rows = lax.fori_loop(
            before[query_index],
            through[query_index],
            weigh,
            jnp.zeros((U, head_count, query_all.shape[2]), jnp.float32),
        )
        return (mixed_rows.astype(jnp.bfloat16), log_total)

    outputs, log_totals = lax.map(per_block, jnp.arange(block_count))
    return (outputs.reshape(query_all.shape[0], -1), log_totals)


def attention_back(query_all, key_all, value_all, grad_all, key_live, before, through, log_totals):
    block_count = query_all.shape[0] // U
    head_count = query_all.shape[1]
    head_scale = 1.0 / math.sqrt(query_all.shape[2])
    zeros_all = jnp.zeros(query_all.shape, jnp.float32)

    def per_block(query_index, grad_state):
        query_grad, key_grad, value_grad = grad_state
        query_rows = lax.dynamic_slice_in_dim(query_all, query_index * U, U, 0)
        grad_rows = lax.dynamic_slice_in_dim(grad_all, query_index * U, U, 0)
        log_total = log_totals[query_index]

        def recompute(key_index):
            key_rows, value_rows, live_keys = key_slices(key_index, key_all, value_all, key_live)
            softmax_rows = jnp.exp(
                scores_of(query_rows, key_rows, live_keys) - log_total[..., None]
            )
            prob_grads = jnp.einsum(
                "qhd,khd->hqk", grad_rows, value_rows, preferred_element_type=jnp.float32
            )
            return (key_rows, softmax_rows, prob_grads)

        def collect(key_index, row_dots):
            key_rows, softmax_rows, prob_grads = recompute(key_index)
            return row_dots + jnp.sum(softmax_rows * prob_grads, axis=-1)

        row_dots = lax.fori_loop(
            before[query_index],
            through[query_index],
            collect,
            jnp.zeros((head_count, U), jnp.float32),
        )

        def spread(key_index, inner_state):
            block_grad, key_total, value_total = inner_state
            key_rows, softmax_rows, prob_grads = recompute(key_index)
            score_grads = (softmax_rows * (prob_grads - row_dots[..., None])).astype(jnp.bfloat16)
            block_grad = (
                block_grad
                + jnp.einsum(
                    "hqk,khd->qhd", score_grads, key_rows, preferred_element_type=jnp.float32
                )
                * head_scale
            )
            offset = key_index * U
            key_part = (
                jnp.einsum(
                    "hqk,qhd->khd", score_grads, query_rows, preferred_element_type=jnp.float32
                )
                * head_scale
            )
            value_part = jnp.einsum(
                "hqk,qhd->khd",
                softmax_rows.astype(jnp.bfloat16),
                grad_rows,
                preferred_element_type=jnp.float32,
            )
            key_total = lax.dynamic_update_slice_in_dim(
                key_total, lax.dynamic_slice_in_dim(key_total, offset, U, 0) + key_part, offset, 0
            )
            value_total = lax.dynamic_update_slice_in_dim(
                value_total,
                lax.dynamic_slice_in_dim(value_total, offset, U, 0) + value_part,
                offset,
                0,
            )
            return (block_grad, key_total, value_total)

        block_start = jnp.zeros((U, head_count, query_all.shape[2]), jnp.float32)
        block_grad, key_grad, value_grad = lax.fori_loop(
            before[query_index], through[query_index], spread, (block_start, key_grad, value_grad)
        )
        query_grad = lax.dynamic_update_slice_in_dim(query_grad, block_grad, query_index * U, 0)
        return (query_grad, key_grad, value_grad)

    return lax.fori_loop(0, block_count, per_block, (zeros_all, zeros_all, zeros_all))


def stat_parts(gradient):
    squares = gradient * gradient
    return (jnp.sum(squares, axis=2), jnp.sum(squares, axis=1), jnp.sum(squares, axis=(1, 2)))


def square_sums(values_in):
    values_f32 = values_in.astype(jnp.float32)
    return jnp.sum(values_f32 * values_f32, axis=(1, 2))


def new_stats(
    decay_beta,
    row_prior,
    col_prior,
    row_square,
    col_square,
    total_square,
    prior_sum,
    row_total,
    col_total,
):
    row_new = decay_beta * row_prior + (1.0 - decay_beta) * (row_square / col_total + TINIEST)
    col_new = decay_beta * col_prior + (1.0 - decay_beta) * (col_square / row_total + TINIEST)
    row_mean = decay_beta * prior_sum / row_total + (1.0 - decay_beta) * (
        total_square / (row_total * col_total) + TINIEST
    )
    return (row_new, col_new, row_mean)


def scaled(gradient, row_new, col_new, row_mean):
    return gradient * lax.rsqrt(row_new[:, :, None] * col_new[:, None, :] / row_mean[:, None, None])


def applied(weight_own, scaled_rows, weight_square, learn_rate, entry_count):
    step_size = learn_rate * jnp.sqrt(weight_square / entry_count)
    return (weight_own.astype(jnp.float32) - step_size[:, None, None] * scaled_rows).astype(
        jnp.bfloat16
    )


def narrow_sums(
    qkv_row_sq,
    gu_row_sq,
    out_col_sq,
    down_col_sq,
    totals,
    weight_square,
    prior_sums,
    attn_gain,
    mlp_gain,
):
    return lax.psum(
        (
            qkv_row_sq,
            gu_row_sq,
            out_col_sq,
            down_col_sq,
            totals,
            weight_square,
            prior_sums,
            attn_gain,
            mlp_gain,
        ),
        "narrow",
    )


def body(
    tokens,
    plot_slot,
    patch_mask,
    cotangent,
    gain_attn,
    w_qkv,
    w_out,
    gain_mlp,
    w_gu,
    w_down,
    qkv_rows,
    qkv_cols,
    out_rows,
    out_cols,
    gu_rows,
    gu_cols,
    down_rows,
    down_cols,
    step_count,
    learn_rate,
):
    own_count = tokens.shape[0]
    own_offset = lax.axis_index("narrow") * own_count
    key_live = patch_mask > 0
    own_live = lax.dynamic_slice_in_dim(patch_mask, own_offset, own_count, 0).astype(jnp.float32)
    before, through = block_bounds(plot_slot)
    rows_in = tokens.astype(jnp.float32)
    attn_normed = lax.all_gather(
        normed(rows_in, gain_attn).astype(jnp.bfloat16), "narrow", axis=0, tiled=True
    )
    length = attn_normed.shape[0]
    projected = jnp.einsum(
        "td,kde->kte", attn_normed, w_qkv, preferred_element_type=jnp.float32
    ).astype(jnp.bfloat16)
    head_count = projected.shape[2] // DH
    query_all = projected[0].reshape(length, head_count, DH)
    key_all = projected[1].reshape(length, head_count, DH)
    value_all = projected[2].reshape(length, head_count, DH)
    attn_mixed, log_totals = attention(query_all, key_all, value_all, key_live, before, through)
    middle = rows_in + lax.psum_scatter(
        jnp.dot(attn_mixed, w_out, preferred_element_type=jnp.float32).astype(jnp.bfloat16),
        "narrow",
        scatter_dimension=0,
        tiled=True,
    ).astype(jnp.float32)
    mlp_normed = lax.all_gather(
        normed(middle, gain_mlp).astype(jnp.bfloat16), "narrow", axis=0, tiled=True
    )
    paired = jnp.einsum("td,kdf->ktf", mlp_normed, w_gu, preferred_element_type=jnp.float32)
    hidden = gelu_gate(paired).astype(jnp.bfloat16)
    mixed_out = (
        middle
        + lax.psum_scatter(
            jnp.dot(hidden, w_down, preferred_element_type=jnp.float32).astype(jnp.bfloat16),
            "narrow",
            scatter_dimension=0,
            tiled=True,
        ).astype(jnp.float32)
    ).astype(jnp.bfloat16)
    out_seed = cotangent.astype(jnp.float32) * own_live[:, None]
    mlp_seed = lax.all_gather(out_seed.astype(jnp.bfloat16), "narrow", axis=0, tiled=True)
    hidden_grad = jnp.einsum("td,fd->tf", mlp_seed, w_down, preferred_element_type=jnp.float32)
    paired_grad = jax.vjp(gelu_gate, paired)[1](hidden_grad)[0].astype(jnp.bfloat16)
    down_part = jnp.einsum("tf,td->fd", hidden, mlp_seed, preferred_element_type=jnp.float32)
    gu_part = jnp.einsum("td,ktf->kdf", mlp_normed, paired_grad, preferred_element_type=jnp.float32)
    mlp_normed_grad = lax.psum_scatter(
        jnp.einsum("ktf,kdf->td", paired_grad, w_gu, preferred_element_type=jnp.float32).astype(
            jnp.bfloat16
        ),
        "narrow",
        scatter_dimension=0,
        tiled=True,
    ).astype(jnp.float32)
    middle_back, mlp_gain_part = jax.vjp(normed, middle, gain_mlp)[1](mlp_normed_grad)
    middle_grad = out_seed + middle_back
    attn_seed = lax.all_gather(middle_grad.astype(jnp.bfloat16), "narrow", axis=0, tiled=True)
    out_part = jnp.einsum("te,td->ed", attn_mixed, attn_seed, preferred_element_type=jnp.float32)
    mixed_grad = jnp.einsum(
        "td,ed->te", attn_seed, w_out, preferred_element_type=jnp.float32
    ).astype(jnp.bfloat16)
    query_grad, key_grad, value_grad = attention_back(
        query_all,
        key_all,
        value_all,
        mixed_grad.reshape(length, head_count, DH),
        key_live,
        before,
        through,
        log_totals,
    )
    projected_grad = (
        jnp.stack([query_grad, key_grad, value_grad]).reshape(3, length, -1).astype(jnp.bfloat16)
    )
    qkv_part = jnp.einsum(
        "td,kte->kde", attn_normed, projected_grad, preferred_element_type=jnp.float32
    )
    attn_normed_grad = lax.psum_scatter(
        jnp.einsum("kte,kde->td", projected_grad, w_qkv, preferred_element_type=jnp.float32).astype(
            jnp.bfloat16
        ),
        "narrow",
        scatter_dimension=0,
        tiled=True,
    ).astype(jnp.float32)
    rows_back, attn_gain_part = jax.vjp(normed, rows_in, gain_attn)[1](attn_normed_grad)
    tokens_grad = middle_grad + rows_back
    decay_beta = 1.0 - lax.rsqrt(step_count.astype(jnp.float32))
    wide_rows = w_qkv.shape[1] // lax.axis_size("wide")
    wide_offset = lax.axis_index("wide") * wide_rows
    reduced = lax.psum(
        (qkv_part, out_part, gu_part, down_part, attn_gain_part[None], mlp_gain_part[None]), "wide"
    )
    qkv_grad, out_grad, gu_grad, down_grad, attn_gain_grad, mlp_gain_grad = reduced
    qkv_square = stat_parts(qkv_grad)
    out_square = stat_parts(out_grad[None])
    gu_square = stat_parts(gu_grad)
    down_square = stat_parts(down_grad[None])
    totals = jnp.concatenate([qkv_square[2], out_square[2], gu_square[2], down_square[2]])
    weight_square = jnp.concatenate(
        [square_sums(w_qkv), square_sums(w_out[None]), square_sums(w_gu), square_sums(w_down[None])]
    )
    prior_sums = jnp.stack([jnp.sum(out_rows), jnp.sum(down_rows)])
    (
        qkv_row_sq,
        gu_row_sq,
        out_col_sq,
        down_col_sq,
        totals,
        weight_square,
        prior_sums,
        attn_gain_grad,
        mlp_gain_grad,
    ) = narrow_sums(
        qkv_square[0],
        gu_square[0],
        out_square[1],
        down_square[1],
        totals,
        weight_square,
        prior_sums,
        attn_gain_grad,
        mlp_gain_grad,
    )
    qkv_col_sq, gu_col_sq, out_row_sq, down_row_sq = (
        qkv_square[1],
        gu_square[1],
        out_square[0],
        down_square[0],
    )
    qkv_stats = new_stats(
        decay_beta,
        qkv_rows,
        qkv_cols,
        qkv_row_sq,
        qkv_col_sq,
        totals[0:3],
        jnp.sum(qkv_rows, axis=1),
        D,
        HD,
    )
    out_stats = new_stats(
        decay_beta,
        out_rows[None],
        out_cols[None],
        out_row_sq,
        out_col_sq,
        totals[3:4],
        prior_sums[0:1],
        HD,
        D,
    )
    gu_stats = new_stats(
        decay_beta,
        gu_rows,
        gu_cols,
        gu_row_sq,
        gu_col_sq,
        totals[4:6],
        jnp.sum(gu_rows, axis=1),
        D,
        FF,
    )
    down_stats = new_stats(
        decay_beta,
        down_rows[None],
        down_cols[None],
        down_row_sq,
        down_col_sq,
        totals[6:7],
        prior_sums[1:2],
        FF,
        D,
    )
    qkv_scaled = scaled(qkv_grad, *qkv_stats)
    out_scaled = scaled(out_grad[None], *out_stats)
    gu_scaled = scaled(gu_grad, *gu_stats)
    down_scaled = scaled(down_grad[None], *down_stats)
    qkv_new = applied(w_qkv, qkv_scaled, weight_square[0:3], learn_rate, D * HD)
    out_new = applied(w_out[None], out_scaled, weight_square[3:4], learn_rate, HD * D)[0]
    gu_new = applied(w_gu, gu_scaled, weight_square[4:6], learn_rate, D * FF)
    down_new = applied(w_down[None], down_scaled, weight_square[6:7], learn_rate, FF * D)[0]

    def own_part(values_in, dimension):
        return lax.dynamic_slice_in_dim(values_in, wide_offset, wide_rows, dimension)

    return (
        mixed_out,
        tokens_grad,
        own_part(attn_gain_grad, 1)[0],
        own_part(qkv_grad, 1),
        own_part(out_grad, 1),
        own_part(mlp_gain_grad, 1)[0],
        own_part(gu_grad, 1),
        own_part(down_grad, 1),
        own_part(qkv_new, 1),
        own_part(out_new, 1),
        own_part(gu_new, 1),
        own_part(down_new, 1),
        own_part(qkv_stats[0], 1),
        qkv_stats[1],
        out_stats[0][0],
        own_part(out_stats[1], 1)[0],
        own_part(gu_stats[0], 1),
        gu_stats[1],
        down_stats[0][0],
        own_part(down_stats[1], 1)[0],
    )


def solution(mesh):
    in_specs = (
        P(("wide", "narrow"), None),
        P("wide"),
        P("wide"),
        P(("wide", "narrow"), None),
        P(),
        P(None, None, "narrow"),
        P("narrow", None),
        P(),
        P(None, None, "narrow"),
        P("narrow", None),
        P(),
        P(None, "narrow"),
        P("narrow"),
        P(),
        P(),
        P(None, "narrow"),
        P("narrow"),
        P(),
        P(),
        P(),
    )
    out_specs = (
        P(("wide", "narrow"), None),
        P(("wide", "narrow"), None),
        P("wide"),
        P(None, "wide", "narrow"),
        P("narrow", "wide"),
        P("wide"),
        P(None, "wide", "narrow"),
        P("narrow", "wide"),
        P(None, "wide", "narrow"),
        P("narrow", "wide"),
        P(None, "wide", "narrow"),
        P("narrow", "wide"),
        P(None, "wide"),
        P(None, "narrow"),
        P("narrow"),
        P("wide"),
        P(None, "wide"),
        P(None, "narrow"),
        P("narrow"),
        P("wide"),
    )
    return jax.shard_map(body, mesh=mesh, in_specs=in_specs, out_specs=out_specs, check_vma=False)
```

profile of v0, /device:TPU:0, one launch (start us, length us, event | category | flops | bytes accessed | tf_op | source)
XLA Modules:
  0.0 902.0 jit_solution(10753407116651511193)
XLA Ops:
  11.5 12.3 %all-gather.5.cloned.1.call-done = bf16[1024,768]{1,0:T(8,128)(2,1)} async-done(((bf16[512,768]{1,0:T(8,128)(2,1)}), bf16[1024,768]{1,0:T(8,128)(2,1)}) %all-gather.5.cloned.1.call-update) | async-done | bytes 1572880 | tf_op jit(solution)/shard_map/all_gather | solution.py:277
  28.6 77.1 %while.105 = (s32[]{:T(128)}, bf16[4,256,6,64]{1,3,2,0:T(8,128)(2,1)S(1)}, f32[4,6,256]{2,1,0:T(8,128)S(1)}, s32[4]{0:T(128)S(1)}, s32[4]{0:T(128)S(1)}, /*index...) while((s32[]{:T(128)}, ...), condition=%wide.region_10.11_spmd, body=%wide.region_3.10_spmd.sunk | while | flops 154735120 | bytes 6428555 | solution.py:100
  38.2 9.7 %while.110 = (s32[]{:T(128)}, f32[256,6,64]{0,2,1:T(8,128)S(1)}, s32[]{:T(128)}, bf16[1024,6,64]{0,2,1:T(8,128)(2,1)}, pred[1024]{0:T(1024)(128)(4,1)S(1)}, /*in...) while((s32[]{:T(128)}, f32[256,6,64]{0,2,1:T(8,128)S(1)}, ...), condition=%wide.region_9.9_spmd, body=%wide.region_8.8_spmd.sunk | while | flops 102334472 | bytes 1386671 | solution.py:92
  57.4 9.6 %while.110 = (s32[]{:T(128)}, f32[256,6,64]{0,2,1:T(8,128)S(1)}, s32[]{:T(128)}, bf16[1024,6,64]{0,2,1:T(8,128)(2,1)}, pred[1024]{0:T(1024)(128)(4,1)S(1)}, /*in...) while((s32[]{:T(128)}, f32[256,6,64]{0,2,1:T(8,128)S(1)}, ...), condition=%wide.region_9.9_spmd, body=%wide.region_8.8_spmd.sunk | while | flops 102334472 | bytes 1386671 | solution.py:92
  76.7 9.7 %while.110 = (s32[]{:T(128)}, f32[256,6,64]{0,2,1:T(8,128)S(1)}, s32[]{:T(128)}, bf16[1024,6,64]{0,2,1:T(8,128)(2,1)}, pred[1024]{0:T(1024)(128)(4,1)S(1)}, /*in...) while((s32[]{:T(128)}, f32[256,6,64]{0,2,1:T(8,128)S(1)}, ...), condition=%wide.region_9.9_spmd, body=%wide.region_8.8_spmd.sunk | while | flops 102334472 | bytes 1386671 | solution.py:92
  96.0 9.7 %while.110 = (s32[]{:T(128)}, f32[256,6,64]{0,2,1:T(8,128)S(1)}, s32[]{:T(128)}, bf16[1024,6,64]{0,2,1:T(8,128)(2,1)}, pred[1024]{0:T(1024)(128)(4,1)S(1)}, /*in...) while((s32[]{:T(128)}, f32[256,6,64]{0,2,1:T(8,128)S(1)}, ...), condition=%wide.region_9.9_spmd, body=%wide.region_8.8_spmd.sunk | while | flops 102334472 | bytes 1386671 | solution.py:92
  109.7 55.3 %reduce-scatter.5.cloned.1.call-done = bf16[512,768]{1,0:T(8,128)(2,1)} async-done(((bf16[1024,768]{1,0:T(8,128)(2,1)}), bf16[512,768]{1,0:T(8,128)(2,1)}) %reduce-scatter.5.cloned.1.call-update) | async-done | bytes 786448 | tf_op jit(solution)/shard_map/reduce_scatter | solution.py:289
  169.6 9.4 %all-gather.7.cloned.1.call-done = bf16[1024,768]{1,0:T(8,128)(2,1)} async-done(((bf16[512,768]{1,0:T(8,128)(2,1)}), bf16[1024,768]{1,0:T(8,128)(2,1)}) %all-gather.7.cloned.1.call-update) | async-done | bytes 1572880 | tf_op jit(solution)/shard_map/all_gather | solution.py:295
  179.0 9.0 convolution_bitcast_fusion.1
  188.0 4.0 all-gather.9.cloned.1.call-done
  192.0 9.4 %multiply_bitcast_fusion = (f32[1,1024,1024]{2,1,0:T(8,128)S(1)}, f32[1,1024,1024]{2,1,0:T(8,128)S(1)}, bf16[1024,1024]{1,0:T(8,128)(2,1)}) fusion(f32[2,1024,1024]{2,1,0:T(8,128)} %convolution_bitcast_fusion.1, bf16[1024,768]{1,0:T(8,128)(2,1)} %all-gather.9.cloned.1.call-done, bf16[1024,768]{1,0:T(8,128)(2,1)} %param.41), kind=kOutput, calls=%fused_computation.70 | convolution fusion | flops 1635778560 | bytes 22020096 | tf_op jit(solution)/shard_map/td,fd->tf/dot_general | solution.py:311
  204.6 4.6 bitcast_convert_fusion.1
  209.2 10.3 %reduce-scatter.9.cloned.1.call-done = bf16[512,768]{1,0:T(8,128)(2,1)} async-done(((bf16[1024,768]{1,0:T(8,128)(2,1)}), bf16[512,768]{1,0:T(8,128)(2,1)}) %reduce-scatter.9.cloned.1.call-update) | async-done | bytes 786448 | tf_op jit(solution)/shard_map/reduce_scatter | solution.py:315
  225.0 10.0 %all-gather.11.cloned.1.call-done = bf16[1024,768]{1,0:T(8,128)(2,1)} async-done(((bf16[512,768]{1,0:T(8,128)(2,1)}), bf16[1024,768]{1,0:T(8,128)(2,1)}) %all-gather.11.cloned.1.call-update) | async-done | bytes 1572880 | tf_op jit(solution)/shard_map/all_gather | solution.py:325
  239.7 101.7 %while.108 = (s32[]{:T(128)}, bf16[1024,6,64]{0,2,1:T(8,128)(2,1)}, f32[1024,6,64]{0,2,1:T(8,128)S(1)}, f32[1024,6,64]{0,2,1:T(8,128)}, s32[4]{0:T(128)S(1)}, /*...) while((s32[]{:T(128)}, bf16[1024,6,64]{0,2,1:T(8,128)(2,1)}, ...), condition=%wide.region_22.23_spmd, body=%wide.region_16.22_spmd.sunk | while | flops 357531648 | bytes 16777936 | solution.py:179
  242.5 6.1 while.111
  248.7 15.7 %while.112 = (s32[]{:T(128)}, f32[256,6,64]{0,2,1:T(8,128)S(1)}, f32[1024,6,64]{0,2,1:T(8,128)S(1)}, f32[1024,6,64]{0,2,1:T(8,128)}, s32[]{:T(128)}, /*index=5*/...) while((s32[]{:T(128)}, f32[256,6,64]{0,2,1:T(8,128)S(1)}, ...), condition=%wide.region_21.21_spmd, body=%wide.region_20.20_spmd.sunk | while | flops 254902272 | bytes 10829027 | solution.py:173
  267.9 6.1 while.111
  274.1 15.7 %while.112 = (s32[]{:T(128)}, f32[256,6,64]{0,2,1:T(8,128)S(1)}, f32[1024,6,64]{0,2,1:T(8,128)S(1)}, f32[1024,6,64]{0,2,1:T(8,128)}, s32[]{:T(128)}, /*index=5*/...) while((s32[]{:T(128)}, f32[256,6,64]{0,2,1:T(8,128)S(1)}, ...), condition=%wide.region_21.21_spmd, body=%wide.region_20.20_spmd.sunk | while | flops 254902272 | bytes 10829027 | solution.py:173
  293.4 6.1 while.111
  299.5 15.7 %while.112 = (s32[]{:T(128)}, f32[256,6,64]{0,2,1:T(8,128)S(1)}, f32[1024,6,64]{0,2,1:T(8,128)S(1)}, f32[1024,6,64]{0,2,1:T(8,128)}, s32[]{:T(128)}, /*index=5*/...) while((s32[]{:T(128)}, f32[256,6,64]{0,2,1:T(8,128)S(1)}, ...), condition=%wide.region_21.21_spmd, body=%wide.region_20.20_spmd.sunk | while | flops 254902272 | bytes 10829027 | solution.py:173
  318.8 6.1 while.111
  324.9 15.7 %while.112 = (s32[]{:T(128)}, f32[256,6,64]{0,2,1:T(8,128)S(1)}, f32[1024,6,64]{0,2,1:T(8,128)S(1)}, f32[1024,6,64]{0,2,1:T(8,128)}, s32[]{:T(128)}, /*index=5*/...) while((s32[]{:T(128)}, f32[256,6,64]{0,2,1:T(8,128)S(1)}, ...), condition=%wide.region_21.21_spmd, body=%wide.region_20.20_spmd.sunk | while | flops 254902272 | bytes 10829027 | solution.py:173
  345.5 4.9 bitcast_convert_fusion
  351.8 4.5 convolution_convert_fusion.1
  356.6 5.7 fusion.97
  362.3 5.6 convolution_bitcast_fusion.2
  374.1 4.7 copy.106
  388.6 5.0 convert_element_type.140
  400.6 39.4 %reduce-scatter.11.cloned.1.call-done = bf16[512,768]{1,0:T(8,128)(2,1)} async-done(((bf16[1024,768]{1,0:T(8,128)(2,1)}), bf16[512,768]{1,0:T(8,128)(2,1)}) %reduce-scatter.11.cloned.1.call-update) | async-done | bytes 786448 | tf_op jit(solution)/shard_map/reduce_scatter | solution.py:346
  441.9 86.0 %all-reduce.2 = (f32[1,768]{1,0:T(1,128)S(1)}, f32[1,768]{1,0:T(1,128)S(1)}) all-reduce(f32[1,768]{1,0:T(1,128)S(1)} %reshape.203, f32[1,768]{1,0:T(1,128)S(1)} %reshape.204), channel_id=1, replica_groups=mesh['wide'=16,'narrow'=2] {'wide'}, use_global_device_ids=true, to_apply=%region_26.27 | all-reduce | flops 1536 | bytes 12288 | tf_op jit(solution)/shard_map/psum | solution.py:359
  531.6 321.8 %all-reduce.7.cloned.1.call-done = (f32[3,768,384]{1,2,0:T(8,128)}, f32[384,768]{1,0:T(8,128)}, f32[2,768,1024]{1,2,0:T(8,128)}, f32[1024,768]{1,0:T(8,128)}) async-done(((f32[3,768,384]{1,2,0:T(8,128)}, f32[384,768]{1,0:T(8,128)}, f32[2,768,1024]{1,2,0:T(8,128)}, f32[1024,768]{1,0:T(8,128)}), (f32[3,768,384]{1,2,0:T(8,128)}, f32[384,768]{1,0:T(8,128)}, f32[2,768,1024]{1,2,0:T(8,128)}, ...) | async-done | bytes 14155792 | tf_op jit(solution)/shard_map/psum | solution.py:359
  (442 shorter events, 211.6 us)
Async XLA Ops:
  7.2 16.6 %copy-start.17 = (bf16[3,768,384]{2,1,0:T(8,128)(2,1)S(1)}, bf16[3,768,384]{2,1,0:T(8,128)(2,1)}, u32[]{:S(2)}) copy-start(bf16[3,768,384]{2,1,0:T(8,128)(2,1)} %param.37) | copy-start | bytes 5308420
  7.2 16.5 %all-gather.5.cloned.1.call-start = ((), (), s32[]{:S(2)}) async-start(), calls=%async_computation.4 | async-start | bytes 2359296 | tf_op jit(solution)/shard_map/all_gather | solution.py:277
  8.8 15.0 %copy-start.36 = (f32[512]{0:T(512)}, f32[512]{0:T(512)S(1)}, u32[]{:S(2)}) copy-start(f32[512]{0:T(512)S(1)} %fusion.54) | copy-start | bytes 6148
  8.8 15.0 %copy-start.33 = (f32[512]{0:T(512)}, f32[512]{0:T(512)S(1)}, u32[]{:S(2)}) copy-start(f32[512]{0:T(512)S(1)} %fusion.77) | copy-start | bytes 6148
  11.1 153.9 %reduce-scatter.5.cloned.1.call-start = ((), (), s32[]{:S(2)}) async-start(), calls=%async_computation.5 | async-start | bytes 2359296 | tf_op jit(solution)/shard_map/reduce_scatter | solution.py:289
  107.4 57.6 %copy-start = (bf16[512,768]{1,0:T(8,128)(2,1)S(1)}, bf16[512,768]{1,0:T(8,128)(2,1)}, u32[]{:S(2)}) copy-start(bf16[512,768]{1,0:T(8,128)(2,1)} %param.32) | copy-start | bytes 2359300
  109.6 57.0 %copy-start.25 = (f32[768]{0:T(1024)S(1)}, f32[768]{0:T(1024)}, u32[]{:S(2)}) copy-start(f32[768]{0:T(1024)} %param.39) | copy-start | bytes 9220
  109.6 69.4 %all-gather.7.cloned.1.call-start = ((), (), s32[]{:S(2)}) async-start(), calls=%async_computation.6 | async-start | bytes 2359296 | tf_op jit(solution)/shard_map/all_gather | solution.py:295
  166.6 55.6 %copy-start.27 = (f32[512]{0:T(512)}, f32[512]{0:T(512)S(1)}, u32[]{:S(2)}) copy-start(f32[512]{0:T(512)S(1)} %fusion.78) | copy-start | bytes 6148
  167.8 24.2 %all-gather.9.cloned.1.call-start = ((), (), s32[]{:S(2)}) async-start(), calls=%async_computation.8 | async-start | bytes 2359296 | tf_op jit(solution)/shard_map/all_gather | solution.py:310
  167.9 54.2 %copy-start.31 = (f32[512]{0:T(512)}, f32[512]{0:T(512)S(1)}, u32[]{:S(2)}) copy-start(f32[512]{0:T(512)S(1)} %dynamic-slice_convert_fusion) | copy-start | bytes 6148
  169.0 50.5 %reduce-scatter.9.cloned.1.call-start = ((), (), s32[]{:S(2)}) async-start(), calls=%async_computation.9 | async-start | bytes 2359296 | tf_op jit(solution)/shard_map/reduce_scatter | solution.py:315
  192.0 12.6 %copy-start.12 = (bf16[2,768,1024]{2,1,0:T(8,128)(2,1)S(1)}, bf16[2,768,1024]{2,1,0:T(8,128)(2,1)}, u32[]{:S(2)}) copy-start(bf16[2,768,1024]{2,1,0:T(8,128)(2,1)} %param.40) | copy-start | bytes 9437188
  209.2 25.8 %all-gather.11.cloned.1.call-start = ((), (), s32[]{:S(2)}) async-start(), calls=%async_computation.10 | async-start | bytes 2359296 | tf_op jit(solution)/shard_map/all_gather | solution.py:325
  223.7 11.3 %copy-start.15 = (bf16[384,768]{1,0:T(8,128)(2,1)S(1)}, bf16[384,768]{1,0:T(8,128)(2,1)}, u32[]{:S(2)}) copy-start(bf16[384,768]{1,0:T(8,128)(2,1)} %param.38) | copy-start | bytes 1769476
  223.8 216.2 %reduce-scatter.11.cloned.1.call-start = ((), (), s32[]{:S(2)}) async-start(), calls=%async_computation.11 | async-start | bytes 2359296 | tf_op jit(solution)/shard_map/reduce_scatter | solution.py:346
  350.4 177.6 %reduce-scatter.7.cloned.1.call-start = ((), (), s32[]{:S(2)}) async-start(), calls=%async_computation.7 | async-start | bytes 2359296 | tf_op jit(solution)/shard_map/reduce_scatter | solution.py:302
  356.3 497.0 %all-reduce.7.cloned.1.call-start = ((), (), s32[]{:S(2)}) async-start(), calls=%async_computation.12 | async-start | bytes 28311552 | tf_op jit(solution)/shard_map/psum | solution.py:359
  398.0 42.0 %copy-start.1 = (bf16[512,768]{1,0:T(8,128)(2,1)S(1)}, bf16[512,768]{1,0:T(8,128)(2,1)}, u32[]{:S(2)}) copy-start(bf16[512,768]{1,0:T(8,128)(2,1)} %param.32) | copy-start | bytes 2359300
  398.0 42.0 %copy-start.29 = (f32[768]{0:T(1024)S(1)}, f32[768]{0:T(1024)}, u32[]{:S(2)}) copy-start(f32[768]{0:T(1024)} %param.36) | copy-start | bytes 9220
  398.1 41.9 %copy-start.34 = (f32[512]{0:T(512)S(1)}, f32[512]{0:T(512)}, u32[]{:S(2)}) copy-start(f32[512]{0:T(512)} %copy-done.33) | copy-start | bytes 6148
  398.1 130.0 %copy-start.9 = (bf16[512,768]{1,0:T(8,128)(2,1)S(1)}, bf16[512,768]{1,0:T(8,128)(2,1)}, u32[]{:S(2)}) copy-start(bf16[512,768]{1,0:T(8,128)(2,1)} %reduce-scatter.9.cloned.1.call-done) | copy-start | bytes 2359300
  399.0 129.0 %copy-start.37 = (f32[512]{0:T(512)S(1)}, f32[512]{0:T(512)}, u32[]{:S(2)}) copy-start(f32[512]{0:T(512)} %copy-done.36) | copy-start | bytes 6148
  399.0 129.1 %copy-start.4 = (bf16[512,768]{1,0:T(8,128)(2,1)S(1)}, bf16[512,768]{1,0:T(8,128)(2,1)}, u32[]{:S(2)}) copy-start(bf16[512,768]{1,0:T(8,128)(2,1)} %reduce-scatter.5.cloned.1.call-done) | copy-start | bytes 2359300
  399.0 129.1 %copy-start.7 = (bf16[512,768]{1,0:T(8,128)(2,1)S(1)}, bf16[512,768]{1,0:T(8,128)(2,1)}, u32[]{:S(2)}) copy-start(bf16[512,768]{1,0:T(8,128)(2,1)} %param.35) | copy-start | bytes 2359300
  399.0 129.1 %copy-start.26 = (f32[768]{0:T(1024)S(1)}, f32[768]{0:T(1024)}, u32[]{:S(2)}) copy-start(f32[768]{0:T(1024)} %param.39) | copy-start | bytes 9220
  399.0 129.1 %copy-start.28 = (f32[512]{0:T(512)S(1)}, f32[512]{0:T(512)}, u32[]{:S(2)}) copy-start(f32[512]{0:T(512)} %copy-done.27) | copy-start | bytes 6148
  399.0 129.1 %copy-start.32 = (f32[512]{0:T(512)S(1)}, f32[512]{0:T(512)}, u32[]{:S(2)}) copy-start(f32[512]{0:T(512)} %copy-done.31) | copy-start | bytes 6148
  399.0 129.1 %copy-start.39 = (f32[512]{0:T(512)S(1)}, f32[512]{0:T(512)}, u32[]{:S(2)}) copy-start(f32[512]{0:T(512)} %copy-done.38) | copy-start | bytes 6148
  859.7 10.5 %copy-start.42 = (f32[3,768]{1,0:T(4,128)S(1)}, f32[3,768]{1,0:T(4,128)}, u32[]{:S(2)}) copy-start(f32[3,768]{1,0:T(4,128)} %param.42) | copy-start | bytes 27652
  862.8 24.2 %copy-start.40 = (f32[1024]{0:T(1024)}, f32[1024]{0:T(1024)S(1)}, u32[]{:S(2)}) copy-start(f32[1024]{0:T(1024)S(1)} %get-tuple-element.771) | copy-start | bytes 12292
  863.4 13.1 %copy-start.44 = (f32[384]{0:T(512)}, f32[384]{0:T(512)S(1)}, u32[]{:S(2)}) copy-start(f32[384]{0:T(512)S(1)} %get-tuple-element.773) | copy-start | bytes 4612
  (37 other events, 115.5 us)
Sparse Core Ops, SparseCore 0:
  11.2 12.5 all-gather.4
  109.7 55.2 reduce-scatter.4
  167.9 11.0 all-gather.6
  181.0 10.9 all-gather.8
  209.3 10.2 reduce-scatter.8
  223.9 11.0 all-gather.10
  350.5 89.4 reduce-scatter.10
  442.2 10.3 reduce-scatter.6
  459.0 394.2 all-reduce.6
where the time goes:
time: 911 us; the launch traced here: 902 us
  waiting for transfers between devices  463 us (51%)
  matrix products  127 us (14%)
  blocking collectives  89.4 us (10%)
  loops' own time  82.5 us (9%)
  other arithmetic  61.9 us (7%)
  local copies, waits for them, and re-layouts  56.8 us (6%)
  between operations  20.2 us (2%)
    psum x1, waiting for transfers between devices, body(): lax.psum((qkv_part, out_part, gu_part, down_part, attn_gain_part[None], m...  322 us
    psum x1, blocking collectives, body(): lax.psum((qkv_part, out_part, gu_part, down_part, attn_gain_part[None], m...  86 us
    reduce_scatter x1, waiting for transfers between devices, body(): lax.psum_scatter(jnp.dot(attn_mixed, w_out, preferred_element_type=jnp.fl...  55.3 us
    reduce_scatter x1, waiting for transfers between devices, body(): lax.psum_scatter(jnp.einsum('kte,kde->td', projected_grad, w_qkv, preferr...  39.4 us
    another operation x4, loops' own time, per_block(): lax.fori_loop(before[query_index], through[query_index], spread, (block_s...  25.1 us
    another operation x4, loops' own time, per_block(): lax.fori_loop(before[query_index], through[query_index], weigh, jnp.zeros...  25 us
    dot_general x16, matrix products, recompute(): jnp.einsum('qhd,khd->hqk', grad_rows, value_rows, preferred_element_type=...  23.1 us
    unnamed x131, local copies, waits for them, and re-layouts  21.8 us
  transfers between devices with their start and end apart: 9, of which 8 were waited for; matrix products, arithmetic and copies ran while one was open for 7% of the time, Pallas kernels for 0%

commit v1 on v0

v1 whole, which is shorter than its diff:
```python
import functools
import math

import jax
import jax.numpy as jnp
from jax import lax
from jax.experimental import pallas as pl
from jax.experimental.pallas import tpu as pltpu
from jax.sharding import PartitionSpec as P

DH = 64
LANES = 128
EPSILON = 1e-06
TINIEST = 1e-30
NEGATIVE = -1e30
F32 = jnp.float32
BF16 = jnp.bfloat16
ROOT = math.sqrt(2.0 / math.pi)
CUBE = 0.044715


def mm(a, b):
    return jnp.dot(a, b, preferred_element_type=F32)


def mm_nt(a, b):
    return lax.dot_general(a, b, (((1,), (1,)), ((), ())), preferred_element_type=F32)


def whole(shape):
    return pl.BlockSpec(shape, lambda *_: (0,) * len(shape))


def cost(flops, nbytes):
    return pl.CostEstimate(flops=int(flops), bytes_accessed=int(nbytes), transcendentals=0)


def inverse_rms(rows):
    return lax.rsqrt(jnp.mean(rows * rows, axis=-1, keepdims=True) + EPSILON)


def three_terms(values):
    high = values.astype(BF16)
    rest = values - high.astype(F32)
    middle = rest.astype(BF16)
    return high, middle, (rest - middle.astype(F32)).astype(BF16)


def bit_orders(n_wide):
    bits = n_wide.bit_length() - 1
    straight = list(range(bits))
    turned = straight[1:-1] + straight[:1] + straight[-1:] if bits > 2 else straight
    return straight, turned


def slot_table(wide_index, order, n_wide):
    bits = len(order)
    entries = []
    for slot in range(n_wide):
        mask = 0
        for stage, bit in enumerate(order):
            if slot >> (bits - 1 - stage) & 1:
                mask |= 1 << bit
        entries.append(mask)
    return jnp.bitwise_xor(jnp.asarray(entries, jnp.int32), wide_index.astype(jnp.int32))


def stage_exchange(values, stage, n_wide):
    orders = bit_orders(n_wide)
    pairs = []
    for wide in range(n_wide):
        for core in range(2):
            pairs.append((wide * 2 + core, (wide ^ (1 << orders[core][stage])) * 2 + core))
    return lax.ppermute(values, ("wide", "narrow"), pairs)


def swap(values):
    return lax.ppermute(values, "narrow", [(0, 1), (1, 0)])


def write_slots(table_ref, held_ref, targets, columns, rows_each):
    if targets[0].ndim == 2:
        targets[0][:, columns] = held_ref[...].astype(BF16)
        return
    slot = 0
    for target in targets:
        for at in range(target.shape[0]):
            start = pl.multiple_of(table_ref[slot] * rows_each, 16)
            target[at, :, columns] = held_ref[pl.ds(start, rows_each), :].astype(BF16)
            slot += 1


def project_kernel(own_ref, other_ref, gain_ref, w_ref, normed_t_ref, projected_ref):
    count = own_ref.shape[0]
    for half, rows_ref in enumerate((own_ref, other_ref)):
        rows = rows_ref[...].astype(F32)
        normed = (rows * inverse_rms(rows) * gain_ref[...]).astype(BF16)
        at = slice(half * count, (half + 1) * count)
        normed_t_ref[:, at] = normed.T
        for i in range(3):
            projected_ref[i, at, :] = mm(normed, w_ref[i]).astype(BF16)


def project(own, other, gain, w_qkv):
    count, width = own.shape
    out = w_qkv.shape[2]
    return pl.pallas_call(
        project_kernel,
        out_shape=[
            jax.ShapeDtypeStruct((width, 2 * count), BF16),
            jax.ShapeDtypeStruct((3, 2 * count, out), BF16),
        ],
        cost_estimate=cost(12 * count * width * out, 8 * count * width),
        name="project",
    )(own, other, gain[None], w_qkv)


def key_constants(live, same):
    length = live.shape[0]
    first = jnp.arange(length) < length // 2
    for_own = jnp.where(live & (first | same), 0.0, NEGATIVE)
    for_other = jnp.where(live & (~first | same), 0.0, NEGATIVE)
    lane = jnp.arange(LANES) % DH
    ones = jnp.where((lane >= 2) & (lane < 5), 1.0, 0.0)
    keys = jnp.where(lane == 0, for_own[:, None], jnp.where(lane == 1, for_other[:, None], ones))
    queries = ((lane == 0) & first[:, None]) | ((lane == 1) & ~first[:, None])
    return keys.astype(BF16), queries.astype(BF16)


def attention_kernel(qkv_ref, keys_ref, queries_ref, own_ref, other_ref, kept_ref, held, *, block):
    lane = lax.broadcasted_iota(jnp.int32, (1, LANES), 1)
    lows = (lane < DH, lane >= DH)
    for head in range(2):
        held[head] = jnp.where(lows[head], qkv_ref[1], keys_ref[...])
        held[2 + head] = jnp.where(lows[head], qkv_ref[2], jnp.ones((1, LANES), BF16))
    half = own_ref.shape[0]
    for part, out_ref in enumerate((own_ref, other_ref)):

        def step(i, carry, part=part, out_ref=out_ref):
            inside = pl.ds(pl.multiple_of(i * block, block), block)
            rows = pl.ds(pl.multiple_of(part * half + i * block, block), block)
            queries = qkv_ref[0, rows, :] * jnp.asarray(1.0 / math.sqrt(DH), BF16)
            constants = queries_ref[rows, :]
            results = []
            for head in range(2):
                scores = mm_nt(jnp.where(lows[head], queries, constants), held[head])
                highest = jnp.max(scores, axis=1, keepdims=True)
                weights = jnp.exp(scores - highest).astype(BF16)
                mixed = mm(weights, held[2 + head])
                results.append(mixed / pltpu.roll(mixed, DH, 1))
                high, middle, low = three_terms(highest + jnp.log(mixed))
                base = DH * (1 - head)
                constants_back = jnp.where(
                    lane == base + 2,
                    -high,
                    jnp.where(lane == base + 3, -middle, jnp.where(lane == base + 4, -low, constants)),
                )
                kept_ref[head, rows, :] = jnp.where(lows[head], queries, constants_back)
            out_ref[inside, :] = jnp.where(lows[0], results[0], results[1]).astype(BF16)
            return carry

        lax.fori_loop(0, half // block, step, 0)


def attention(qkv, keys, queries, block=512):
    length, width = qkv.shape[1:]
    pairs, half = width // LANES, length // 2
    return pl.pallas_call(
        functools.partial(attention_kernel, block=block),
        grid=(pairs,),
        in_specs=[
            pl.BlockSpec((3, length, LANES), lambda p: (0, 0, p)),
            whole((length, LANES)),
            whole((length, LANES)),
        ],
        out_specs=[
            pl.BlockSpec((half, LANES), lambda p: (0, p)),
            pl.BlockSpec((half, LANES), lambda p: (0, p)),
            pl.BlockSpec((2, length, LANES), lambda p: (p, 0, 0)),
        ],
        out_shape=[
            jax.ShapeDtypeStruct((half, width), BF16),
            jax.ShapeDtypeStruct((half, width), BF16),
            jax.ShapeDtypeStruct((2 * pairs, length, LANES), BF16),
        ],
        scratch_shapes=[pltpu.VMEM((4, length, LANES), BF16)],
        cost_estimate=cost(16 * pairs * length * length * LANES, 10 * length * width),
        name="attention",
    )(qkv, keys, queries)


def middle_kernel(first, rows_each, *refs):
    refs = list(refs)
    table_ref = refs.pop(0)
    if first:
        (tokens_ref, own_ref, recv_ref, w_own_ref, w_recv_ref) = refs[:5]
        (gain_ref, cot_ref, live_ref, gu_ref, down_ref, middle_ref, total_ref, back_ref, part_ref) = refs[5:14]
        (normed, normed_t, seed, seed_t, held) = refs[14:]
    else:
        (middle_ref, total_in, back_in, gain_ref, cot_ref, live_ref, gu_ref, down_ref) = refs[:8]
        (out_ref, grad_ref, attn_seed_ref, gain_part_ref, part_ref) = refs[8:13]
        (normed, normed_t, seed, seed_t, held, total_ref, back_ref) = refs[13:]
    step = pl.program_id(0)

    @pl.when(step == 0)
    def _():
        if first:
            middle = tokens_ref[...].astype(F32) + (
                mm(own_ref[...], w_own_ref[...]) + mm(recv_ref[...], w_recv_ref[...])
            )
            middle_ref[...] = middle
            total_ref[...] = middle
            back_ref[...] = jnp.zeros_like(back_ref)
        else:
            middle = middle_ref[...]
            total_ref[...] = total_in[...]
            back_ref[...] = back_in[...]
        value = (middle * inverse_rms(middle) * gain_ref[...]).astype(BF16)
        normed[...] = value
        normed_t[...] = value.T
        seed_value = (cot_ref[...].astype(F32) * live_ref[...]).astype(BF16)
        seed[...] = seed_value
        seed_t[...] = seed_value.T

    gate = mm(normed[...], gu_ref[0])
    up = mm(normed[...], gu_ref[1])
    bent = jnp.tanh(ROOT * (gate + CUBE * gate * gate * gate))
    soft = 0.5 * gate * (1.0 + bent)
    slope = 0.5 * (1.0 + bent) + 0.5 * gate * (1.0 - bent * bent) * (ROOT * (1.0 + 3.0 * CUBE * gate * gate))
    hidden = (soft * up).astype(BF16)
    hidden_grad = mm_nt(seed[...], down_ref[...])
    gate_grad = (hidden_grad * up * slope).astype(BF16)
    up_grad = (hidden_grad * soft).astype(BF16)
    total_ref[...] += mm(hidden, down_ref[...])
    back_ref[...] += mm_nt(gate_grad, gu_ref[0]) + mm_nt(up_grad, gu_ref[1])
    chunk = gate.shape[1]
    held[:, 0:chunk] = mm(normed_t[...], gate_grad)
    held[:, chunk : 2 * chunk] = mm(normed_t[...], up_grad)
    held[:, 2 * chunk : 3 * chunk] = mm(seed_t[...], hidden)
    write_slots(table_ref, held, [part_ref], slice(None), rows_each)

    if not first:

        @pl.when(step == pl.num_programs(0) - 1)
        def _():
            out_ref[...] = total_ref[...].astype(BF16)
            middle = middle_ref[...]
            factor = inverse_rms(middle)
            back = back_ref[...]
            scaled = back * gain_ref[...]
            inner = jnp.mean(scaled * middle, axis=-1, keepdims=True)
            grad = (
                cot_ref[...].astype(F32) * live_ref[...]
                + factor * scaled
                - middle * (factor * factor * factor * inner)
            )
            grad_ref[...] = grad
            attn_seed_ref[...] = grad.astype(BF16)
            gain_part_ref[...] = jnp.sum(back * middle * factor, axis=0, keepdims=True)


def middle_call(first, inputs, gain, cot, live, w_gu, w_down, table, n_wide, chunk=256):
    count, width = cot.shape
    units = w_down.shape[0]
    rows_each = width // n_wide
    steps = units // chunk
    tall = rows_each % 16 == 0
    rows = (count, width)
    if tall:
        part_spec = pl.BlockSpec((n_wide, rows_each, 3 * chunk), lambda j, *_: (0, 0, j))
        part_shape = jax.ShapeDtypeStruct((n_wide, rows_each, 3 * units), BF16)
    else:
        part_spec = pl.BlockSpec((width, 3 * chunk), lambda j, *_: (0, j))
        part_shape = jax.ShapeDtypeStruct((width, 3 * units), BF16)
    in_specs = [whole(v.shape) for v in inputs] + [
        whole((1, width)),
        whole(rows),
        whole((count, 1)),
        pl.BlockSpec((2, width, chunk), lambda j, *_: (0, 0, j)),
        pl.BlockSpec((chunk, width), lambda j, *_: (j, 0)),
    ]
    scratch = [
        pltpu.VMEM(rows, BF16),
        pltpu.VMEM((width, count), BF16),
        pltpu.VMEM(rows, BF16),
        pltpu.VMEM((width, count), BF16),
        pltpu.VMEM((width, 3 * chunk), F32),
    ]
    if first:
        out_specs = [whole(rows)] * 3
        out_shape = [jax.ShapeDtypeStruct(rows, F32)] * 3
    else:
        out_specs = [whole(rows), whole(rows), whole(rows), whole((1, width))]
        out_shape = [
            jax.ShapeDtypeStruct(rows, BF16),
            jax.ShapeDtypeStruct(rows, F32),
            jax.ShapeDtypeStruct(rows, BF16),
            jax.ShapeDtypeStruct((1, width), F32),
        ]
        scratch += [pltpu.VMEM(rows, F32)] * 2
    outs = pl.pallas_call(
        functools.partial(middle_kernel, first, rows_each),
        grid_spec=pltpu.PrefetchScalarGridSpec(
            num_scalar_prefetch=1,
            grid=(steps,),
            in_specs=in_specs,
            out_specs=out_specs + [part_spec],
            scratch_shapes=scratch,
        ),
        out_shape=out_shape + [part_shape],
        cost_estimate=cost(18 * count * width * units, 16 * width * units),
        name="middle_first" if first else "middle_last",
    )(table, *inputs, gain[None], cot, live, w_gu, w_down)
    return outs[:-1], in_slots(outs[-1], table, n_wide)


def in_slots(part, table, n_wide):
    if part.ndim == 3:
        return part
    return jnp.take(part.reshape(n_wide, -1, part.shape[-1]), table, axis=0)


def seeds_kernel(own_ref, other_ref, w_ref, grad_ref, seed_t_ref):
    count = own_ref.shape[0]
    for half, seed_ref in enumerate((own_ref, other_ref)):
        at = slice(half * count, (half + 1) * count)
        grad_ref[at, :] = mm_nt(seed_ref[...], w_ref[...]).astype(BF16)
        seed_t_ref[:, at] = seed_ref[...].T


def seeds_call(own, other, w_out):
    count, width = own.shape
    out = w_out.shape[0]
    return pl.pallas_call(
        seeds_kernel,
        out_shape=[
            jax.ShapeDtypeStruct((2 * count, out), BF16),
            jax.ShapeDtypeStruct((width, 2 * count), BF16),
        ],
        cost_estimate=cost(4 * count * width * out, 8 * count * width),
        name="seeds",
    )(own, other, w_out)


def attention_back_kernel(last, block, rows_each, split, *refs):
    refs = list(refs)
    table_ref = refs.pop(0)
    (qkv_ref, grad_ref, mixed_own_ref, mixed_other_ref, kept_ref, keys_ref) = refs[:6]
    (normed_t_ref, seed_t_ref, w_ref) = refs[6:9]
    refs = refs[9:]
    carried_ref = refs.pop(0) if last else None
    part_refs = [refs.pop(0) for _ in range(split)]
    back_refs = [refs.pop(0) for _ in range(2 if last else 1)]
    grads, queries, query_total, pieces, mixed, held, total = refs
    lane = lax.broadcasted_iota(jnp.int32, (1, LANES), 1)
    lows = (lane < DH, lane >= DH)
    nothing = jnp.zeros((1, LANES), BF16)
    length = grad_ref.shape[0]
    half = length // 2
    mixed[0:half, :] = mixed_own_ref[...]
    mixed[half:length, :] = mixed_other_ref[...]
    product = grad_ref[...].astype(F32) * mixed[...].astype(F32)
    for head in range(2):
        base = DH * (1 - head)
        dots = jnp.sum(jnp.where(lows[head], product, 0.0), axis=1, keepdims=True)
        high, middle, low = three_terms(dots)
        constants = jnp.where(
            lane == base + 2,
            -high,
            jnp.where(lane == base + 3, -middle, jnp.where(lane == base + 4, -low, nothing)),
        )
        grads[head] = jnp.where(lows[head], grad_ref[...], constants)
        grads[2 + head] = jnp.where(lows[head], grad_ref[...], nothing)
        queries[head] = jnp.where(lows[head], kept_ref[head], nothing)
    query_total[...] = jnp.zeros_like(query_total)

    def step(i, carry):
        rows = pl.ds(pl.multiple_of(i * block, block), block)
        keys, values, constants = qkv_ref[1, rows, :], qkv_ref[2, rows, :], keys_ref[rows, :]
        key_grad, value_grad = [], []
        for head in range(2):
            base = DH * (1 - head)
            ones = jnp.where((lane >= base + 2) & (lane < base + 5), 1.0, 0.0).astype(BF16)
            keys_only = jnp.where(lows[head], keys, nothing) * jnp.asarray(1.0 / math.sqrt(DH), BF16)
            weights = jnp.exp(mm_nt(jnp.where(lows[head], keys, constants), kept_ref[head]))
            score_grads = weights * mm_nt(jnp.where(lows[head], values, ones), grads[head])
            score_grads = score_grads.astype(BF16)
            value_grad.append(mm(weights.astype(BF16), grads[2 + head]))
            key_grad.append(mm(score_grads, queries[head]))
            query_total[...] += mm(keys_only.T, score_grads)
        pieces[rows, LANES : 2 * LANES] = (key_grad[0] + key_grad[1]).astype(BF16)
        pieces[rows, 2 * LANES : 3 * LANES] = (value_grad[0] + value_grad[1]).astype(BF16)
        return carry

    lax.fori_loop(0, length // block, step, 0)
    pieces[:, 0:LANES] = query_total[...].T.astype(BF16)
    held[:, 0 : 3 * LANES] = mm(normed_t_ref[...], pieces[...])
    held[:, 3 * LANES : 4 * LANES] = mm(seed_t_ref[...], mixed[...])
    write_slots(table_ref, held, part_refs, slice(None), rows_each)
    back = sum(mm_nt(pieces[:, i * LANES : (i + 1) * LANES], w_ref[i]) for i in range(3))
    pair = pl.program_id(0)

    @pl.when(pair == 0)
    def _():
        total[...] = back + carried_ref[...] if last else back

    @pl.when(pair > 0)
    def _():
        total[...] += back

    @pl.when(pair == pl.num_programs(0) - 1)
    def _():
        if last:
            back_refs[0][...] = total[0:half, :]
            back_refs[1][...] = total[half:length, :].astype(BF16)
        else:
            back_refs[0][...] = total[...]


def attention_back(first, count, last, qkv, grad, mixed_own, mixed_other, kept, keys, normed_t, seed_t, w_qkv, carried, table, n_wide, block=512):
    length = qkv.shape[1]
    half = length // 2
    width = normed_t.shape[0]
    rows_each = width // n_wide
    tall = rows_each % 16 == 0
    columns = 4 * LANES
    if tall:
        part_specs = [pl.BlockSpec((n_wide // 2, rows_each, columns), lambda p, *_: (0, 0, p))] * 2
        part_shapes = [jax.ShapeDtypeStruct((n_wide // 2, rows_each, count * columns), BF16)] * 2
    else:
        part_specs = [pl.BlockSpec((width, columns), lambda p, *_: (0, p))]
        part_shapes = [jax.ShapeDtypeStruct((width, count * columns), BF16)]
    in_specs = [
        pl.BlockSpec((3, length, LANES), lambda p, *_: (0, 0, p + first)),
        pl.BlockSpec((length, LANES), lambda p, *_: (0, p + first)),
        pl.BlockSpec((half, LANES), lambda p, *_: (0, p + first)),
        pl.BlockSpec((half, LANES), lambda p, *_: (0, p + first)),
        pl.BlockSpec((2, length, LANES), lambda p, *_: (p + first, 0, 0)),
        whole((length, LANES)),
        whole((width, length)),
        whole((width, length)),
        pl.BlockSpec((3, width, LANES), lambda p, *_: (0, 0, p + first)),
    ]
    inputs = [qkv, grad, mixed_own, mixed_other, kept, keys, normed_t, seed_t, w_qkv]
    if last:
        in_specs.append(whole((length, width)))
        inputs.append(carried)
        back_specs = [whole((half, width))] * 2
        back_shapes = [jax.ShapeDtypeStruct((half, width), F32), jax.ShapeDtypeStruct((half, width), BF16)]
    else:
        back_specs = [whole((length, width))]
        back_shapes = [jax.ShapeDtypeStruct((length, width), F32)]
    outs = pl.pallas_call(
        functools.partial(attention_back_kernel, last, block, rows_each, len(part_specs)),
        grid_spec=pltpu.PrefetchScalarGridSpec(
            num_scalar_prefetch=1,
            grid=(count,),
            in_specs=in_specs,
            out_specs=part_specs + back_specs,
            scratch_shapes=[
                pltpu.VMEM((4, length, LANES), BF16),
                pltpu.VMEM((2, length, LANES), BF16),
                pltpu.VMEM((LANES, length), F32),
                pltpu.VMEM((length, 3 * LANES), BF16),
                pltpu.VMEM((length, LANES), BF16),
                pltpu.VMEM((width, columns), F32),
                pltpu.VMEM((length, width), F32),
            ],
        ),
        out_shape=part_shapes + back_shapes,
        cost_estimate=cost(count * 50 * length * length * LANES, count * 16 * length * LANES),
        name="attention_back",
    )(table, *inputs)
    parts, backs = outs[: len(part_specs)], outs[len(part_specs) :]
    if not tall:
        slots = in_slots(parts[0], table, n_wide)
        parts = [slots[: n_wide // 2], slots[n_wide // 2 :]]
    return parts, backs


def added(arrays, low, high):
    return sum(a[low:high].astype(F32) for a in arrays)


def scatter(pieces, send, n_wide):
    slots = n_wide // 2
    stage = 0
    while True:
        pieces = pieces + [stage_exchange(send, stage, n_wide)]
        stage += 1
        if slots == 1:
            return pieces
        slots //= 2
        send = added(pieces, slots, 2 * slots).astype(BF16)


def input_grad_kernel(own_ref, recv_ref, tokens_ref, gain_ref, middle_grad_ref, out_ref, part_ref):
    back = own_ref[...] + recv_ref[...].astype(F32)
    rows = tokens_ref[...].astype(F32)
    factor = inverse_rms(rows)
    scaled = back * gain_ref[...]
    inner = jnp.mean(scaled * rows, axis=-1, keepdims=True)
    out_ref[...] = middle_grad_ref[...] + factor * scaled - rows * (factor * factor * factor * inner)
    part_ref[...] = jnp.sum(back * rows * factor, axis=0, keepdims=True)


def input_grad(own, recv, tokens, gain, middle_grad):
    count, width = tokens.shape
    return pl.pallas_call(
        input_grad_kernel,
        out_shape=[jax.ShapeDtypeStruct((count, width), F32), jax.ShapeDtypeStruct((1, width), F32)],
        cost_estimate=cost(20 * count * width, 18 * count * width),
        name="input_grad",
    )(own, recv, tokens, gain[None], middle_grad)


def gather_kernel(counts, chunk, *refs):
    refs = list(refs)
    groups = [[refs.pop(0) for _ in range(count)] for count in counts]
    qkv_ref, out_ref, gu_ref, down_ref, columns_ref, rows_ref, turned = refs
    sums = []
    for group in groups:
        total = group[0][0].astype(F32)
        for ref in group[1:]:
            total = total + ref[0].astype(F32)
        sums.append(total)
    wide_part, pair_parts = sums[0], sums[1:]
    pairs = [part[:, i : i + 4 * LANES] for part in pair_parts for i in range(0, part.shape[1], 4 * LANES)]
    mats = [
        jnp.concatenate([pair[:, i * LANES : (i + 1) * LANES] for pair in pairs], axis=1) for i in range(4)
    ]
    kinds = [
        jnp.concatenate(
            [
                wide_part[:, j + i * chunk : j + (i + 1) * chunk]
                for j in range(0, wide_part.shape[1], 3 * chunk)
            ],
            axis=1,
        )
        for i in range(3)
    ]
    rows = wide_part.shape[0]
    for i in range(3):
        qkv_ref[i] = mats[i]
    for i in range(2):
        gu_ref[i] = kinds[i]
    for value, ref in ((mats[3], out_ref), (kinds[2], down_ref)):
        count = value.shape[1]
        turned[0:rows, 0:count] = value
        ref[...] = turned[:, 0:count].T[:, 0:rows]
    columns_ref[...] = jnp.zeros_like(columns_ref)
    rows_ref[...] = jnp.zeros_like(rows_ref)
    lane = lax.broadcasted_iota(jnp.int32, (1, LANES), 1)
    row_sums = jnp.zeros((rows, LANES), F32)
    for i, value in enumerate((mats[0], mats[1], mats[2], mats[3], kinds[0], kinds[1], kinds[2])):
        squares = value * value
        columns_ref[i : i + 1, 0 : value.shape[1]] = jnp.sum(squares, axis=0, keepdims=True)
        row_sums = jnp.where(lane == i, jnp.sum(squares, axis=1, keepdims=True), row_sums)
    rows_ref[0:rows, :] = row_sums


def gather_own(groups, heads_width, units, chunk):
    rows = groups[0][0].shape[1]
    inputs = [a for group in groups for a in group]
    widest = max(heads_width, units)
    shapes = [(3, rows, heads_width), (heads_width, rows), (2, rows, units), (units, rows), (8, widest)]
    shapes.append((max(8, -(-rows // 8) * 8), LANES))
    return pl.pallas_call(
        functools.partial(gather_kernel, [len(g) for g in groups], chunk),
        grid=(1,),
        in_specs=[pl.BlockSpec((1,) + a.shape[1:], lambda *_: (0, 0, 0)) for a in inputs],
        out_specs=[whole(s) for s in shapes],
        out_shape=[jax.ShapeDtypeStruct(s, F32) for s in shapes],
        scratch_shapes=[pltpu.VMEM((LANES, widest), F32)],
        cost_estimate=cost(1 << 20, 4 << 20),
        name="gather_own",
    )(*inputs)


def update_kernel(sizes, *refs):
    (scalar_ref, qkv_ref, out_ref, gu_ref, down_ref, columns_ref, rows_ref, prior_rows_ref) = refs[:8]
    (qkv_cols, out_rows, gu_cols, down_rows, w_qkv, w_out, w_gu, w_down) = refs[8:16]
    (qkv_new, out_new, gu_new, down_new, qkv_cols_new, out_rows_new, gu_cols_new, down_rows_new, rows_new_ref) = refs[16:25]
    (turned,) = refs[25:]
    beta = scalar_ref[0]
    fresh = 1.0 - beta
    rows = qkv_ref.shape[1]
    lane = lax.broadcasted_iota(jnp.int32, (1, LANES), 1)
    all_rows = jnp.zeros((rows, LANES), F32)
    width = sizes[0]
    priors = [qkv_cols[0:1], qkv_cols[1:2], qkv_cols[2:3], out_rows[...], gu_cols[0:1], gu_cols[1:2], down_rows[...]]
    for i in range(7):
        across = sizes[1 + i]
        row_new = beta * prior_rows_ref[0:rows, i : i + 1] + fresh * (rows_ref[0:rows, i : i + 1] / across + TINIEST)
        count = priors[i].shape[1]
        col_new = beta * priors[i] + fresh * (columns_ref[i : i + 1, 0:count] / width + TINIEST)
        all_rows = jnp.where(lane == i, row_new, all_rows)
        mean, rate = scalar_ref[1 + i], scalar_ref[8 + i]
        if i in (3, 6):
            turned[0:rows, :] = jnp.broadcast_to(row_new, (rows, LANES))
            row_line = turned[...].T[0:1, 0:rows]
            gradient_ref, weight_ref, new_ref = ((out_ref, w_out, out_new), (down_ref, w_down, down_new))[i == 6]
            column = jnp.broadcast_to(col_new, (LANES, count)).T[:, 0:1]
            step = gradient_ref[...] * lax.rsqrt(row_line * column / mean)
            new_ref[...] = (weight_ref[...].astype(F32) - rate * step).astype(BF16)
            (out_rows_new, down_rows_new)[i == 6][...] = col_new
        else:
            at = i if i < 3 else i - 4
            gradient_ref, weight_ref, new_ref = (qkv_ref, w_qkv, qkv_new) if i < 3 else (gu_ref, w_gu, gu_new)
            step = gradient_ref[at] * lax.rsqrt(row_new * col_new / mean)
            new_ref[at] = (weight_ref[at].astype(F32) - rate * step).astype(BF16)
            (qkv_cols_new if i < 3 else gu_cols_new)[at : at + 1] = col_new
    turned[0:rows, :] = all_rows
    rows_new_ref[...] = turned[...].T[0:8, 0:rows]


def update(scalars, grads, columns, rows_sq, prior_rows, col_priors, weights, sizes):
    rows = grads[0].shape[1]
    new_shapes = [jax.ShapeDtypeStruct(w.shape, BF16) for w in weights]
    col_shapes = [jax.ShapeDtypeStruct(c.shape, F32) for c in col_priors]
    inputs = [*grads, columns, rows_sq, prior_rows, *col_priors, *weights]
    out_shape = new_shapes + col_shapes + [jax.ShapeDtypeStruct((8, rows), F32)]
    return pl.pallas_call(
        functools.partial(update_kernel, sizes),
        grid_spec=pltpu.PrefetchScalarGridSpec(
            num_scalar_prefetch=1,
            grid=(1,),
            in_specs=[whole(a.shape) for a in inputs],
            out_specs=[whole(s.shape) for s in out_shape],
            scratch_shapes=[pltpu.VMEM((LANES, LANES), F32)],
        ),
        out_shape=out_shape,
        cost_estimate=cost(1 << 20, 4 << 20),
        name="update",
    )(scalars, *inputs)


def square_sum(values):
    wide = values.astype(F32)
    return jnp.sum(wide * wide, axis=(-2, -1))


def body(
    n_wide,
    tokens,
    plot_slot,
    patch_mask,
    cotangent,
    gain_attn,
    w_qkv,
    w_out,
    gain_mlp,
    w_gu,
    w_down,
    qkv_rows,
    qkv_cols,
    out_rows,
    out_cols,
    gu_rows,
    gu_cols,
    down_rows,
    down_cols,
    step_count,
    learn_rate,
):
    count, width = tokens.shape
    heads_width, units = w_out.shape[0], w_down.shape[0]
    rows_each = width // n_wide
    chunk = 256
    core = lax.axis_index("narrow")
    wide = lax.axis_index("wide")
    tables = [slot_table(wide, order, n_wide) for order in bit_orders(n_wide)]
    own_table = jnp.where(core == 0, tables[0], tables[1])
    other_table = jnp.where(core == 0, tables[1], tables[0])

    tokens_other = swap(tokens)
    own_live = lax.dynamic_slice_in_dim(patch_mask, core * count, count, 0)
    other_live = lax.dynamic_slice_in_dim(patch_mask, (1 - core) * count, count, 0)
    same = plot_slot[0] == plot_slot[2 * count - 1]
    key_const, query_const = key_constants(jnp.concatenate([own_live, other_live]) > 0, same)
    live = own_live.astype(F32)[:, None]

    normed_t, qkv = project(tokens, tokens_other, gain_attn, w_qkv)
    w_out_other, w_gu_other, w_down_other = swap(w_out), swap(w_gu), swap(w_down)
    mixed_own, mixed_other, kept = attention(qkv, key_const, query_const)
    mixed_recv = swap(mixed_other)
    (middle, total, back), part_other = middle_call(
        True,
        [tokens, mixed_own, mixed_recv, w_out, w_out_other],
        gain_mlp,
        cotangent,
        live,
        w_gu_other,
        w_down_other,
        other_table,
        n_wide,
        chunk,
    )
    part_recv = swap(part_other)
    (mixed_out, middle_grad, attn_seed, mlp_gain_part), part_own = middle_call(
        False, [middle, total, back], gain_mlp, cotangent, live, w_gu, w_down, own_table, n_wide, chunk
    )
    seed_other = swap(attn_seed)
    half = n_wide // 2
    mlp_pieces = [part_own, part_recv]
    mlp_pieces = scatter(mlp_pieces, added(mlp_pieces, half, n_wide).astype(BF16), n_wide)

    mixed_grad, seed_t = seeds_call(attn_seed, seed_other, w_out)
    pairs = heads_width // LANES
    back_args = (qkv, mixed_grad, mixed_own, mixed_other, kept, key_const, normed_t, seed_t, w_qkv)
    (keep, send), (carried,) = attention_back(0, pairs - 1, False, *back_args, None, own_table, n_wide)
    first_pieces = scatter([keep], send, n_wide)
    (keep, send), (back_own, back_other) = attention_back(
        pairs - 1, 1, True, *back_args, carried, own_table, n_wide
    )
    last_pieces = scatter([keep], send, n_wide)
    tokens_grad, attn_gain_part = input_grad(back_own, swap(back_other), tokens, gain_attn, middle_grad)

    *grads, columns, rows_sq = gather_own([mlp_pieces, first_pieces, last_pieces], heads_width, units, chunk)
    qkv_grad, out_grad, gu_grad, down_grad = grads

    weight_sq = jnp.concatenate(
        [square_sum(w_qkv), square_sum(w_out)[None], square_sum(w_gu), square_sum(w_down)[None]]
    )
    prior_sums = jnp.stack([jnp.sum(out_rows), jnp.sum(down_rows)])
    widest = columns.shape[1]
    small = jnp.concatenate(
        [
            jnp.pad(attn_gain_part, ((0, 0), (0, widest - width))),
            jnp.pad(mlp_gain_part, ((0, 0), (0, widest - width))),
            jnp.pad(jnp.concatenate([weight_sq, prior_sums])[None], ((0, 0), (0, widest - 9))),
            jnp.zeros((5, widest), F32),
        ]
    )
    rows_sq, small = (lambda pair: (rows_sq + pair[0], small + pair[1]))((swap(rows_sq), swap(small)))
    totals = jnp.sum(rows_sq, axis=0)[:8]
    summed = jnp.concatenate(
        [columns[:7], jnp.pad(totals[None], ((0, 0), (0, widest - 8))), small[:2]], axis=0
    )
    for stage in range(n_wide.bit_length() - 1):
        summed = summed + stage_exchange(summed, stage, n_wide)
    columns, totals = summed[:8], summed[7, :7]
    gains = lax.dynamic_slice_in_dim(summed[8:10, :width], wide * rows_each, rows_each, 1)
    weight_sq, prior_sums = small[2, :7], small[2, 7:9]

    beta = 1.0 - lax.rsqrt(step_count.astype(F32))
    fresh = 1.0 - beta
    across = [2 * heads_width] * 4 + [2 * units] * 3
    entries = jnp.asarray([width * a for a in across], F32)
    own_prior = jnp.concatenate(
        [
            jnp.mean(qkv_rows, axis=1),
            prior_sums[:1] / (2 * heads_width),
            jnp.mean(gu_rows, axis=1),
            prior_sums[1:] / (2 * units),
        ]
    )
    means = beta * own_prior + fresh * (totals / entries + TINIEST)
    rates = learn_rate * jnp.sqrt(jnp.concatenate([weight_sq[:7]]) / entries)
    scalars = jnp.concatenate([beta[None], means, rates])

    def own_rows(values, dimension):
        return lax.dynamic_slice_in_dim(values, wide * rows_each, rows_each, dimension)

    prior_rows = jnp.concatenate([qkv_rows, out_cols[None], gu_rows, down_cols[None]], axis=0)
    prior_rows = own_rows(prior_rows, 1).T
    outs = update(
        scalars,
        grads,
        columns,
        rows_sq,
        prior_rows,
        [qkv_cols, out_rows[None], gu_cols, down_rows[None]],
        [own_rows(w_qkv, 1), own_rows(w_out, 1), own_rows(w_gu, 1), own_rows(w_down, 1)],
        [width, *across],
    )
    qkv_new, out_new, gu_new, down_new, qkv_cols_new, out_rows_new, gu_cols_new, down_rows_new, rows_new = outs
    return (
        mixed_out,
        tokens_grad,
        gains[0],
        qkv_grad,
        out_grad,
        gains[1],
        gu_grad,
        down_grad,
        qkv_new,
        out_new,
        gu_new,
        down_new,
        rows_new[0:3],
        qkv_cols_new,
        out_rows_new[0],
        rows_new[3],
        rows_new[4:6],
        gu_cols_new,
        down_rows_new[0],
        rows_new[6],
    )


def solution(mesh):
    in_specs = (
        P(("wide", "narrow"), None),
        P("wide"),
        P("wide"),
        P(("wide", "narrow"), None),
        P(),
        P(None, None, "narrow"),
        P("narrow", None),
        P(),
        P(None, None, "narrow"),
        P("narrow", None),
        P(),
        P(None, "narrow"),
        P("narrow"),
        P(),
        P(),
        P(None, "narrow"),
        P("narrow"),
        P(),
        P(),
        P(),
    )
    out_specs = (
        P(("wide", "narrow"), None),
        P(("wide", "narrow"), None),
        P("wide"),
        P(None, "wide", "narrow"),
        P("narrow", "wide"),
        P("wide"),
        P(None, "wide", "narrow"),
        P("narrow", "wide"),
        P(None, "wide", "narrow"),
        P("narrow", "wide"),
        P(None, "wide", "narrow"),
        P("narrow", "wide"),
        P(None, "wide"),
        P(None, "narrow"),
        P("narrow"),
        P("wide"),
        P(None, "wide"),
        P(None, "narrow"),
        P("narrow"),
        P("wide"),
    )
    return jax.shard_map(
        functools.partial(body, mesh.shape["wide"]),
        mesh=mesh,
        in_specs=in_specs,
        out_specs=out_specs,
        check_vma=False,
    )
```

time: 911 us -> 247 us (0.27)
  waiting for transfers between devices: 463 us -> 43.1 us
  matrix products: 127 us -> 0 us
  Pallas kernels: 0 us -> 107 us
  blocking collectives: 89.4 us -> 0 us
  loops' own time: 82.5 us -> 0 us
  other arithmetic: 61.9 us -> 35.5 us
  local copies, waits for them, and re-layouts: 56.8 us -> 33 us
  starting transfers between devices: 1.28 us -> 19.2 us
  between operations: 20.2 us -> 5.24 us
    psum x1 -> x0, waiting for transfers between devices: 322 us -> none  [body(): lax.psum((qkv_part, out_part, gu_part, down_part, attn_gain_part[None], m...]
    dot_general x84 -> x0, matrix products: 127 us -> none  [the longest x16 23.1 us: recompute(): jnp.einsum('qhd,khd->hqk', grad_rows, value_rows, preferred_element_type=...]
    pallas_call x0 -> x10, Pallas kernels: none -> 107 us  [the longest x2 39 us: attention_back(): pl.pallas_call(functools.partial(attention_back_kernel, last, block, rows...]
    reduce_scatter x4 -> x0, waiting for transfers between devices: 105 us -> none  [the longest x1 55.3 us: body(): lax.psum_scatter(jnp.dot(attn_mixed, w_out, preferred_element_type=jnp.fl...]
    psum x2 -> x0, blocking collectives: 89.4 us -> none  [the longest x1 86 us: body(): lax.psum((qkv_part, out_part, gu_part, down_part, attn_gain_part[None], m...]
    another operation x18 -> x0, loops' own time: 82.5 us -> none  [the longest x4 25.1 us: per_block(): lax.fori_loop(before[query_index], through[query_index], spread, (block_s...]
    ppermute x0 -> x26, waiting for transfers between devices: none -> 43.1 us  [the longest x16 42.5 us: stage_exchange(): return lax.ppermute(values, ('wide', 'narrow'), pairs)]
    all_gather x4 -> x0, waiting for transfers between devices: 35.7 us -> none  [the longest x1 12.3 us: body(): lax.all_gather(normed(rows_in, gain_attn).astype(jnp.bfloat16), 'narrow',...]
  transfers between devices with their start and end apart: 9 -> 26, of which waited for: 8 -> 7; matrix products, arithmetic and copies ran while one was open for 7% -> 21% of each run, Pallas kernels for 0% -> 36%
where the time goes in v1:
time: 247 us; the launch traced here: 243 us
  Pallas kernels  107 us (43%)
  waiting for transfers between devices  43.1 us (17%)
  other arithmetic  35.5 us (14%)
  local copies, waits for them, and re-layouts  33 us (13%)
  starting transfers between devices  19.2 us (8%)
  between operations  5.24 us (2%)
    ppermute x16, waiting for transfers between devices, stage_exchange(): return lax.ppermute(values, ('wide', 'narrow'), pairs)  42.5 us
    pallas_call x2, Pallas kernels, attention_back(): pl.pallas_call(functools.partial(attention_back_kernel, last, block, rows...  39 us
    pallas_call x2, Pallas kernels, middle_call(): pl.pallas_call(functools.partial(middle_kernel, first, rows_each), grid_s...  33.1 us
    ppermute x16, starting transfers between devices, stage_exchange(): return lax.ppermute(values, ('wide', 'narrow'), pairs)  17 us
    pallas_call x1, Pallas kernels, attention(): pl.pallas_call(functools.partial(attention_kernel, block=block), grid=(pa...  13.5 us
    unnamed x77, local copies, waits for them, and re-layouts  12.3 us
    convert_element_type x9, other arithmetic, scatter(): send = added(pieces, slots, 2 * slots).astype(BF16)  11.3 us
    dynamic_slice x4, local copies, waits for them, and re-layouts, own_rows(): lax.dynamic_slice_in_dim(values, wide * rows_each, rows_each, dimension)  6.72 us
  transfers between devices with their start and end apart: 26, of which 7 were waited for; matrix products, arithmetic and copies ran while one was open for 21% of the time, Pallas kernels for 36%

profile of v1, /device:TPU:0, one launch (start us, length us, event | category | flops | bytes accessed | tf_op | source)
XLA Modules:
  0.0 243.1 jit_solution(8381719760561099776)
XLA Ops:
  8.7 6.7 %project.1 = (bf16[768,1024]{1,0:T(8,128)(2,1)}, bf16[3,1024,384]{2,1,0:T(8,128)(2,1)}) custom-call(bf16[512,768]{1,0:T(8,128)(2,1)} %tokens_ref.1, bf16[512,768]{1,0:T(8,128)(2,1)} %collective-permute-done.other_ref, f32[1,768]{1,0:T(1,128)} %broadcast_in_dim.97.gain_ref, bf16[3,768,384]{2,1,0:T(8,128)(2,1)} %refs_9_.3), custom_call_target="tpu_custom_call" | custom-call | flops 1811939328 | bytes 3145728 | tf_op jit(solution)/shard_map/project/pallas_call | solution.py:107
  15.4 13.5 %attention.1 = (bf16[512,384]{1,0:T(8,128)(2,1)}, bf16[512,384]{1,0:T(8,128)(2,1)}, bf16[6,1024,128]{2,1,0:T(8,128)(2,1)}) custom-call(bf16[3,1024,384]{2,1,0:T(8,128)(2,1)} %get-tuple-element.60.qkv_ref.refs_1_, bf16[1024,128]{1,0:T(8,128)(2,1)} %select_convert_fusion.keys_ref.refs_6_, bf16[1024,128]{1,0:T(8,128)(2,1)} %or_convert_fusion.queries_ref), custom_call_target="tpu_custom_call" | custom-call | flops 6442450944 | bytes 3932160 | tf_op jit(solution)/shard_map/attention/pallas_call | solution.py:168
  33.1 15.6 %middle_first.1 = (f32[512,768]{1,0:T(8,128)}, f32[512,768]{1,0:T(8,128)}, f32[512,768]{1,0:T(8,128)}, bf16[16,48,3072]{2,1,0:T(8,128)(2,1)}) custom-call(s32[16]{0:T(128)} %get-tuple-element.175.refs_0_, bf16[512,768]{1,0:T(8,128)(2,1)} %tokens_ref.1, bf16[512,384]{1,0:T(8,128)(2,1)} %get-tuple-element.61.refs_2_.refs_3_, bf16[512,384]{1,0:T(8,128)(2,1)} %copy-done.35, ...), custom_call_target="tpu_custom_call" | custom-call | flops 7247757312 | bytes 12582912 | tf_op jit(solution)/shard_map/middle_first/pallas_call | solution.py:301
  50.9 2.0 multiply_reduce_fusion.3
  52.8 2.0 multiply_reduce_fusion.1
  55.8 17.5 %middle_last.1 = (bf16[512,768]{1,0:T(8,128)(2,1)}, f32[512,768]{1,0:T(8,128)}, bf16[512,768]{1,0:T(8,128)(2,1)}, f32[1,768]{1,0:T(1,128)}, bf16[16,48,3072]{2,1,0:T(8,128)(2,1)}) custom-call(s32[16]{0:T(128)} %get-tuple-element.176.refs_0_, f32[512,768]{1,0:T(8,128)} %get-tuple-element.63.refs_1_, f32[512,768]{1,0:T(8,128)} %get-tuple-element.64.refs_2_, ...), custom_call_target="tpu_custom_call" | custom-call | flops 7247757312 | bytes 12582912 | tf_op jit(solution)/shard_map/middle_last/pallas_call | solution.py:301
  73.7 4.9 %add_convert_fusion = bf16[8,48,3072]{2,1,0:T(8,128)(2,1)} fusion(bf16[16,48,3072]{2,1,0:T(8,128)(2,1)} %collective-permute-done.7.refs_1_, bf16[16,48,3072]{2,1,0:T(8,128)(2,1)} %get-tuple-element.77.refs_0_), kind=kLoop, calls=%fused_computation.1 | loop fusion | flops 4718592 | bytes 7077888 | tf_op jit(solution)/shard_map/convert_element_type | solution.py:706
  78.6 2.6 %collective-permute-start.8 = (bf16[8,48,3072]{2,1,0:T(8,128)(2,1)}, bf16[8,48,3072]{2,1,0:T(8,128)(2,1)S(1)}, u32[]{:S(2)}, u32[]{:S(2)}) collective-permute-start(bf16[8,48,3072]{2,1,0:T(8,128)(2,1)} %add_convert_fusion), channel_id=1, source_target_pairs={{0,2},{1,5},{2,0},{3,7},{4,6},{5,1},{6,4},{7,3},{8,10},{9,13},{10,... | collective-permute-start | bytes 7077896 | tf_op jit(solution)/shard_map/ppermute | solution.py:74
  82.6 3.2 %concatenate.29 = f32[9]{0:T(128)} concatenate(f32[3]{0:T(128)S(1)} %multiply_reduce_fusion.1, f32[1]{0:T(128)} %bitcast.3, f32[2]{0:T(128)S(1)} %multiply_reduce_fusion, f32[1]{0:T(128)} %bitcast.4, f32[1]{0:T(128)} %bitcast.5, f32[1]{0:T(128)} %bitcast.6), dimensions={0} | concatenate | bytes 72 | tf_op jit(solution)/shard_map/concatenate | solution.py:731
  87.2 4.0 %seeds.1 = (bf16[1024,384]{1,0:T(8,128)(2,1)}, bf16[768,1024]{1,0:T(8,128)(2,1)}) custom-call(bf16[512,768]{1,0:T(8,128)(2,1)} %get-tuple-element.67.own_ref, bf16[512,768]{1,0:T(8,128)(2,1)} %copy-done.34, bf16[384,768]{1,0:T(8,128)(2,1)} %w_ref.3), custom_call_target="tpu_custom_call" | custom-call | flops 603979776 | bytes 3145728 | tf_op jit(solution)/shard_map/seeds/pallas_call | solution.py:334
  91.1 24.3 %attention_back.2 = (bf16[8,48,1024]{2,1,0:T(8,128)(2,1)}, bf16[8,48,1024]{2,1,0:T(8,128)(2,1)}, f32[1024,768]{1,0:T(8,128)}) custom-call(s32[16]{0:T(128)} %get-tuple-element.176.refs_0_, bf16[3,1024,384]{2,1,0:T(8,128)(2,1)} %get-tuple-element.60.qkv_ref.refs_1_, bf16[1024,384]{1,0:T(8,128)(2,1)} %get-tuple-element.68.refs_2_, ...), custom_call_target="tpu_custom_call" | custom-call | flops 13421772800 | bytes 4194304 | tf_op jit(solution)/shard_map/attention_back/pallas_call | solution.py:453
  115.4 14.7 %attention_back.3 = (bf16[8,48,512]{2,1,0:T(8,128)(2,1)}, bf16[8,48,512]{2,1,0:T(8,128)(2,1)}, f32[512,768]{1,0:T(8,128)}, bf16[512,768]{1,0:T(8,128)(2,1)}) custom-call(s32[16]{0:T(128)} %get-tuple-element.176.refs_0_, bf16[3,1024,384]{2,1,0:T(8,128)(2,1)} %get-tuple-element.60.qkv_ref.refs_1_, bf16[1024,384]{1,0:T(8,128)(2,1)} %get-tuple-element.68.refs_2_, ...), custom_call_target="tpu_custom_call" | custom-call | flops 6710886400 | bytes 2097152 | tf_op jit(solution)/shard_map/attention_back/pallas_call | solution.py:453
  130.2 3.1 %add_convert_fusion.1 = bf16[4,48,3072]{2,1,0:T(8,128)(2,1)S(1)} fusion(bf16[8,48,3072]{2,1,0:T(8,128)(2,1)S(1)} %collective-permute-done.8.refs_2_, bf16[16,48,3072]{2,1,0:T(8,128)(2,1)} %collective-permute-done.7.refs_1_, bf16[16,48,3072]{2,1,0:T(8,128)(2,1)} %get-tuple-element.77.refs_0_), kind=kLoop, calls=%fused_computation.4 | loop fusion | flops 3538944 | bytes 4718592 | tf_op jit(solution)/shard_map/convert_element_type | solution.py:494
  133.3 2.2 collective-permute-start.9
  135.6 1.9 constant_dynamic-slice_fusion.refs_15_
  138.7 1.6 constant_dynamic-slice_fusion.1.refs_14_
  141.5 19.0 %collective-permute-done.17.refs_13_ = bf16[4,48,512]{2,1,0:T(8,128)(2,1)S(1)} collective-permute-done((bf16[4,48,512]{2,1,0:T(8,128)(2,1)S(1)}, bf16[4,48,512]{2,1,0:T(8,128)(2,1)S(1)}, u32[]{:S(2)}, u32[]{:S(2)}) %collective-permute-start.17) | collective-permute-done | bytes 196640 | tf_op jit(solution)/shard_map/ppermute | solution.py:74
  160.6 1.9 collective-permute-start.18
  165.0 2.9 %add_convert_fusion.2 = bf16[2,48,3072]{2,1,0:T(8,128)(2,1)} fusion(bf16[4,48,3072]{2,1,0:T(8,128)(2,1)S(1)} %collective-permute-done.9.refs_3_, bf16[8,48,3072]{2,1,0:T(8,128)(2,1)S(1)} %collective-permute-done.8.refs_2_, bf16[16,48,3072]{2,1,0:T(8,128)(2,1)} %collective-permute-done.7.refs_1_, bf16[16,48,3072]{2,1,0:T(8,128)(2,1)} %get-tuple-element.77.refs_0_), kind=kLoop, calls=%fused_computation.6 | loop fusion | flops 2359296 | bytes 2949120 | tf_op jit(solution)/shard_map/convert_element_type | solution.py:494
  169.0 2.6 %collective-permute-start.19 = (bf16[1,48,512]{2,1,0:T(8,128)(2,1)}, bf16[1,48,512]{2,1,0:T(8,128)(2,1)}, u32[]{:S(2)}, u32[]{:S(2)}) collective-permute-start(bf16[1,48,512]{2,1,0:T(8,128)(2,1)} %add_convert_fusion.9), channel_id=1, source_target_pairs={{0,16},{1,17},{2,18},{3,19},{4,20},{5,21},{6,22},{7,23},{8,24},{9,... | collective-permute-start | bytes 147464 | tf_op jit(solution)/shard_map/ppermute | solution.py:74
  171.6 4.3 %input_grad.1 = (f32[512,768]{1,0:T(8,128)}, f32[1,768]{1,0:T(1,128)}) custom-call(f32[512,768]{1,0:T(8,128)} %get-tuple-element.73.own_ref, bf16[512,768]{1,0:T(8,128)(2,1)} %collective-permute-done.6.recv_ref, bf16[512,768]{1,0:T(8,128)(2,1)} %tokens_ref.1, f32[1,768]{1,0:T(1,128)} %broadcast_in_dim.97.gain_ref, f32[512,768]{1,0:T(8,128)} %get-tuple-element.75.middle_grad_ref), custom_call_target="tpu_custom_call" | custom-call | flops 7864320 | bytes 7077888 | tf_op jit(solution)/shard_map/input_grad/pallas_call | solution.py:509
  178.4 1.6 collective-permute-start.14
  182.0 2.6 %collective-permute-done.14.refs_9_ = bf16[2,48,1024]{2,1,0:T(8,128)(2,1)S(1)} collective-permute-done((bf16[2,48,1024]{2,1,0:T(8,128)(2,1)S(1)}, bf16[2,48,1024]{2,1,0:T(8,128)(2,1)S(1)}, u32[]{:S(2)}, u32[]{:S(2)}) %collective-permute-start.14) | collective-permute-done | bytes 196640 | tf_op jit(solution)/shard_map/ppermute | solution.py:74
  188.0 13.7 %collective-permute-done.15.refs_10_ = bf16[1,48,1024]{2,1,0:T(8,128)(2,1)S(1)} collective-permute-done((bf16[1,48,1024]{2,1,0:T(8,128)(2,1)S(1)}, bf16[1,48,1024]{2,1,0:T(8,128)(2,1)S(1)}, u32[]{:S(2)}, u32[]{:S(2)}) %collective-permute-start.15) | collective-permute-done | bytes 98336 | tf_op jit(solution)/shard_map/ppermute | solution.py:74
  203.1 2.9 %gather_own.1 = (f32[3,48,384]{2,1,0:T(8,128)}, f32[384,48]{1,0:T(8,128)}, f32[2,48,1024]{2,1,0:T(8,128)}, f32[1024,48]{1,0:T(8,128)}, f32[8,1024]{1,0:T(8,128)}, /*index=5*/f32[48,128]{1,0:T(8,128)}) custom-call(bf16[16,48,3072]{2,1,0:T(8,128)(2,1)} %get-tuple-element.77.refs_0_, bf16[16,48,3072]{2,1,0:T(8,128)(2,1)} %collective-permute-done.7.refs_1_, ...), custom_call_target="tpu_custom_call" | custom-call | flops 1048576 | bytes 4194304 | tf_op jit(solution)/shard_map/gather_own/pallas_call | solution.py:568
  210.5 1.7 constant_dynamic-slice_fusion.2.refs_13_
  212.1 1.8 collective-permute-done.22
  219.2 4.2 %collective-permute-done.24 = f32[10,1024]{1,0:T(8,128)S(1)} collective-permute-done((f32[10,1024]{1,0:T(8,128)S(1)}, f32[10,1024]{1,0:T(8,128)S(1)}, u32[]{:S(2)}, u32[]{:S(2)}) %collective-permute-start.24) | collective-permute-done | bytes 40992 | tf_op jit(solution)/shard_map/ppermute | solution.py:74
  225.4 1.9 copy.63
  227.3 1.7 copy.62
  230.3 3.7 %update.1 = (bf16[3,48,384]{2,1,0:T(8,128)(2,1)}, bf16[384,48]{1,0:T(8,128)(2,1)}, bf16[2,48,1024]{2,1,0:T(8,128)(2,1)}, bf16[1024,48]{1,0:T(8,128)(2,1)}, f32[3...) custom-call(f32[15]{0:T(128)} %pad_maximum_fusion.refs_0_, ...), custom_call_target="tpu_custom_call" | custom-call | flops 1048576 | bytes 4194304 | tf_op jit(solution)/shard_map/update/pallas_call | solution.py:623
  237.7 1.7 copy.65
  (173 shorter events, 50.0 us)
Async XLA Ops:
  0.7 30.7 %collective-permute-start.3 = (bf16[2,768,1024]{2,1,0:T(8,128)(2,1)}, bf16[2,768,1024]{2,1,0:T(8,128)(2,1)S(1)}, u32[]{:S(2)}, u32[]{:S(2)}) collective-permute-start(bf16[2,768,1024]{2,1,0:T(8,128)(2,1)} %refs_7_.3), channel_id=1, source_target_pairs={{0,1},{1,0},{2,3},{3,2},{4,5},{5,4},{6,7},{7,6},{8,9},{9,8},{10,11... | collective-permute-start | bytes 9437192 | tf_op jit(solution)/shard_map/ppermute | solution.py:78
  1.2 7.5 %collective-permute-start = (bf16[512,768]{1,0:T(8,128)(2,1)}, bf16[512,768]{1,0:T(8,128)(2,1)}, u32[]{:S(2)}, u32[]{:S(2)}) collective-permute-start(bf16[512,768]{1,0:T(8,128)(2,1)} %tokens_ref.1), channel_id=1, source_target_pairs={{0,1},{1,0},{2,3},{3,2},{4,5},{5,4},{6,7},{7,6},{8,9},{9,8},{10,11... | collective-permute-start | bytes 2359304 | tf_op jit(solution)/shard_map/ppermute | solution.py:78
  1.3 30.1 %collective-permute-start.4 = (bf16[1024,768]{1,0:T(8,128)(2,1)}, bf16[1024,768]{1,0:T(8,128)(2,1)}, u32[]{:S(2)}, u32[]{:S(2)}) collective-permute-start(bf16[1024,768]{1,0:T(8,128)(2,1)} %refs_8_.2), channel_id=1, source_target_pairs={{0,1},{1,0},{2,3},{3,2},{4,5},{5,4},{6,7},{7,6},{8,9},{9,8},{10,11... | collective-permute-start | bytes 4718600 | tf_op jit(solution)/shard_map/ppermute | solution.py:78
  1.7 29.6 %collective-permute-start.2 = (bf16[384,768]{1,0:T(8,128)(2,1)}, bf16[384,768]{1,0:T(8,128)(2,1)}, u32[]{:S(2)}, u32[]{:S(2)}) collective-permute-start(bf16[384,768]{1,0:T(8,128)(2,1)} %w_ref.3), channel_id=1, source_target_pairs={{0,1},{1,0},{2,3},{3,2},{4,5},{5,4},{6,7},{7,6},{8,9},{9,8},{10,11... | collective-permute-start | bytes 1769480 | tf_op jit(solution)/shard_map/ppermute | solution.py:78
  29.0 2.4 collective-permute-start.1
  48.7 25.0 %collective-permute-start.7 = (bf16[16,48,3072]{2,1,0:T(8,128)(2,1)}, bf16[16,48,3072]{2,1,0:T(8,128)(2,1)}, u32[]{:S(2)}, u32[]{:S(2)}) collective-permute-start(bf16[16,48,3072]{2,1,0:T(8,128)(2,1)} %get-tuple-element.78), channel_id=1, source_target_pairs={{0,1},{1,0},{2,3},{3,2},{4,5},{5,4},{6,7},{7,6},{8,9},{9,8},{10,11... | collective-permute-start | bytes 14155784 | tf_op jit(solution)/shard_map/ppermute | solution.py:78
  73.3 13.0 %collective-permute-start.5 = (bf16[512,768]{1,0:T(8,128)(2,1)}, bf16[512,768]{1,0:T(8,128)(2,1)S(1)}, u32[]{:S(2)}, u32[]{:S(2)}) collective-permute-start(bf16[512,768]{1,0:T(8,128)(2,1)} %get-tuple-element.67.own_ref), channel_id=1, source_target_pairs={{0,1},{1,0},{2,3},{3,2},{4,5},{5,4},{6,7},{7,6},{8,9},{9,8},{10,11... | collective-permute-start | bytes 2359304 | tf_op jit(solution)/shard_map/ppermute | solution.py:78
  78.6 51.6 %collective-permute-start.8 = (bf16[8,48,3072]{2,1,0:T(8,128)(2,1)}, bf16[8,48,3072]{2,1,0:T(8,128)(2,1)S(1)}, u32[]{:S(2)}, u32[]{:S(2)}) collective-permute-start(bf16[8,48,3072]{2,1,0:T(8,128)(2,1)} %add_convert_fusion), channel_id=1, source_target_pairs={{0,2},{1,5},{2,0},{3,7},{4,6},{5,1},{6,4},{7,3},{8,10},{9,13},{10,... | collective-permute-start | bytes 7077896 | tf_op jit(solution)/shard_map/ppermute | solution.py:74
  130.1 32.4 %copy-start.3 = (bf16[8,48,1024]{2,1,0:T(8,128)(2,1)S(1)}, bf16[8,48,1024]{2,1,0:T(8,128)(2,1)}, u32[]{:S(2)}) copy-start(bf16[8,48,1024]{2,1,0:T(8,128)(2,1)} %get-tuple-element.79.refs_6_) | copy-start | bytes 2359300
  130.1 10.2 %collective-permute-start.16 = (bf16[8,48,512]{2,1,0:T(8,128)(2,1)}, bf16[8,48,512]{2,1,0:T(8,128)(2,1)S(1)}, u32[]{:S(2)}, u32[]{:S(2)}) collective-permute-start(bf16[8,48,512]{2,1,0:T(8,128)(2,1)} %get-tuple-element.82), channel_id=1, source_target_pairs={{0,2},{1,5},{2,0},{3,7},{4,6},{5,1},{6,4},{7,3},{8,10},{9,13},{10,... | collective-permute-start | bytes 1179656 | tf_op jit(solution)/shard_map/ppermute | solution.py:74
  130.2 49.9 %copy-start = (bf16[8,48,3072]{2,1,0:T(8,128)(2,1)}, bf16[8,48,3072]{2,1,0:T(8,128)(2,1)S(1)}, u32[]{:S(2)}) copy-start(bf16[8,48,3072]{2,1,0:T(8,128)(2,1)S(1)} %collective-permute-done.8.refs_2_) | copy-start | bytes 7077892
  133.3 31.7 %collective-permute-start.9 = (bf16[4,48,3072]{2,1,0:T(8,128)(2,1)S(1)}, bf16[4,48,3072]{2,1,0:T(8,128)(2,1)S(1)}, u32[]{:S(2)}, u32[]{:S(2)}) collective-permute-start(bf16[4,48,3072]{2,1,0:T(8,128)(2,1)S(1)} %add_convert_fusion.1), channel_id=1, source_target_pairs={{0,4},{1,9},{2,6},{3,11},{4,0},{5,13},{6,2},{7,15},{8,12},{9,1},{1... | collective-permute-start | bytes 3538952 | tf_op jit(solution)/shard_map/ppermute | solution.py:74
  137.4 25.0 %collective-permute-start.12 = (bf16[8,48,1024]{2,1,0:T(8,128)(2,1)S(1)}, bf16[8,48,1024]{2,1,0:T(8,128)(2,1)S(1)}, u32[]{:S(2)}, u32[]{:S(2)}) collective-permute-start(bf16[8,48,1024]{2,1,0:T(8,128)(2,1)S(1)} %copy-done.33), channel_id=1, source_target_pairs={{0,2},{1,5},{2,0},{3,7},{4,6},{5,1},{6,4},{7,3},{8,10},{9,13},{10,... | collective-permute-start | bytes 2359304 | tf_op jit(solution)/shard_map/ppermute | solution.py:74
  140.4 28.0 %copy-start.7 = (bf16[8,48,512]{2,1,0:T(8,128)(2,1)}, bf16[8,48,512]{2,1,0:T(8,128)(2,1)S(1)}, u32[]{:S(2)}) copy-start(bf16[8,48,512]{2,1,0:T(8,128)(2,1)S(1)} %collective-permute-done.16.refs_12_) | copy-start | bytes 1179652
  140.4 20.1 %collective-permute-start.17 = (bf16[4,48,512]{2,1,0:T(8,128)(2,1)S(1)}, bf16[4,48,512]{2,1,0:T(8,128)(2,1)S(1)}, u32[]{:S(2)}, u32[]{:S(2)}) collective-permute-start(bf16[4,48,512]{2,1,0:T(8,128)(2,1)S(1)} %add_convert_fusion.5), channel_id=1, source_target_pairs={{0,4},{1,9},{2,6},{3,11},{4,0},{5,13},{6,2},{7,15},{8,12},{9,1},{1... | collective-permute-start | bytes 589832 | tf_op jit(solution)/shard_map/ppermute | solution.py:74
  141.5 30.1 %collective-permute-start.6 = (bf16[512,768]{1,0:T(8,128)(2,1)S(1)}, bf16[512,768]{1,0:T(8,128)(2,1)}, u32[]{:S(2)}, u32[]{:S(2)}) collective-permute-start(bf16[512,768]{1,0:T(8,128)(2,1)S(1)} %copy-done.32), channel_id=1, source_target_pairs={{0,1},{1,0},{2,3},{3,2},{4,5},{5,4},{6,7},{7,6},{8,9},{9,8},{10,11... | collective-permute-start | bytes 2359304 | tf_op jit(solution)/shard_map/ppermute | solution.py:78
  160.6 7.7 %collective-permute-start.18 = (bf16[2,48,512]{2,1,0:T(8,128)(2,1)S(1)}, bf16[2,48,512]{2,1,0:T(8,128)(2,1)S(1)}, u32[]{:S(2)}, u32[]{:S(2)}) collective-permute-start(bf16[2,48,512]{2,1,0:T(8,128)(2,1)S(1)} %add_convert_fusion.7), channel_id=1, source_target_pairs={{0,8},{1,3},{2,10},{3,1},{4,12},{5,7},{6,14},{7,5},{8,0},{9,11},{1... | collective-permute-start | bytes 294920 | tf_op jit(solution)/shard_map/ppermute | solution.py:74
  163.5 13.8 %collective-permute-start.13 = (bf16[4,48,1024]{2,1,0:T(8,128)(2,1)}, bf16[4,48,1024]{2,1,0:T(8,128)(2,1)}, u32[]{:S(2)}, u32[]{:S(2)}) collective-permute-start(bf16[4,48,1024]{2,1,0:T(8,128)(2,1)} %add_convert_fusion.3), channel_id=1, source_target_pairs={{0,4},{1,9},{2,6},{3,11},{4,0},{5,13},{6,2},{7,15},{8,12},{9,1},{1... | collective-permute-start | bytes 1179656 | tf_op jit(solution)/shard_map/ppermute | solution.py:74
  167.8 12.2 %collective-permute-start.10 = (bf16[2,48,3072]{2,1,0:T(8,128)(2,1)}, bf16[2,48,3072]{2,1,0:T(8,128)(2,1)}, u32[]{:S(2)}, u32[]{:S(2)}) collective-permute-start(bf16[2,48,3072]{2,1,0:T(8,128)(2,1)} %add_convert_fusion.2), channel_id=1, source_target_pairs={{0,8},{1,3},{2,10},{3,1},{4,12},{5,7},{6,14},{7,5},{8,0},{9,11},{1... | collective-permute-start | bytes 1769480 | tf_op jit(solution)/shard_map/ppermute | solution.py:74
  169.0 19.1 %collective-permute-start.19 = (bf16[1,48,512]{2,1,0:T(8,128)(2,1)}, bf16[1,48,512]{2,1,0:T(8,128)(2,1)}, u32[]{:S(2)}, u32[]{:S(2)}) collective-permute-start(bf16[1,48,512]{2,1,0:T(8,128)(2,1)} %add_convert_fusion.9), channel_id=1, source_target_pairs={{0,16},{1,17},{2,18},{3,19},{4,20},{5,21},{6,22},{7,23},{8,24},{9,... | collective-permute-start | bytes 147464 | tf_op jit(solution)/shard_map/ppermute | solution.py:74
  177.2 28.9 %collective-permute-start.21 = (f32[8,1024]{1,0:T(8,128)}, f32[8,1024]{1,0:T(8,128)}, u32[]{:S(2)}, u32[]{:S(2)}) collective-permute-start(f32[8,1024]{1,0:T(8,128)} %fusion.2), channel_id=1, source_target_pairs={{0,1},{1,0},{2,3},{3,2},{4,5},{5,4},{6,7},{7,6},{8,9},{9,8},{10,11... | collective-permute-start | bytes 98312 | tf_op jit(solution)/shard_map/ppermute | solution.py:78
  178.4 6.2 %collective-permute-start.14 = (bf16[2,48,1024]{2,1,0:T(8,128)(2,1)S(1)}, bf16[2,48,1024]{2,1,0:T(8,128)(2,1)S(1)}, u32[]{:S(2)}, u32[]{:S(2)}) collective-permute-start(bf16[2,48,1024]{2,1,0:T(8,128)(2,1)S(1)} %add_convert_fusion.6), channel_id=1, source_target_pairs={{0,8},{1,3},{2,10},{3,1},{4,12},{5,7},{6,14},{7,5},{8,0},{9,11},{1... | collective-permute-start | bytes 589832 | tf_op jit(solution)/shard_map/ppermute | solution.py:74
  181.4 20.4 %collective-permute-start.11 = (bf16[1,48,3072]{2,1,0:T(8,128)(2,1)S(1)}, bf16[1,48,3072]{2,1,0:T(8,128)(2,1)S(1)}, u32[]{:S(2)}, u32[]{:S(2)}) collective-permute-start(bf16[1,48,3072]{2,1,0:T(8,128)(2,1)S(1)} %add_convert_fusion.4), channel_id=1, source_target_pairs={{0,16},{1,17},{2,18},{3,19},{4,20},{5,21},{6,22},{7,23},{8,24},{9,... | collective-permute-start | bytes 884744 | tf_op jit(solution)/shard_map/ppermute | solution.py:74
  186.3 15.4 %collective-permute-start.15 = (bf16[1,48,1024]{2,1,0:T(8,128)(2,1)S(1)}, bf16[1,48,1024]{2,1,0:T(8,128)(2,1)S(1)}, u32[]{:S(2)}, u32[]{:S(2)}) collective-permute-start(bf16[1,48,1024]{2,1,0:T(8,128)(2,1)S(1)} %add_convert_fusion.8), channel_id=1, source_target_pairs={{0,16},{1,17},{2,18},{3,19},{4,20},{5,21},{6,22},{7,23},{8,24},{9,... | collective-permute-start | bytes 294920 | tf_op jit(solution)/shard_map/ppermute | solution.py:74
  188.0 27.3 %copy-start.15 = (f32[2,768]{1,0:T(2,128)S(1)}, f32[2,768]{1,0:T(2,128)}, u32[]{:S(2)}) copy-start(f32[2,768]{1,0:T(2,128)} %param.37) | copy-start | bytes 18436
  188.0 27.4 %copy-start.20 = (f32[384]{0:T(512)S(1)}, f32[384]{0:T(512)}, u32[]{:S(2)}) copy-start(f32[384]{0:T(512)} %param.35) | copy-start | bytes 4612
  188.0 31.2 %copy-start.26 = (f32[1,7]{1,0:T(1,128)S(1)}, f32[1,7]{1,0:T(1,128)}, u32[]{:S(2)}) copy-start(f32[1,7]{1,0:T(1,128)} %constant.88) | copy-start | bytes 88
  206.1 1.5 collective-permute-start.20
  209.7 4.3 %collective-permute-start.22 = (f32[10,1024]{1,0:T(8,128)S(1)}, f32[10,1024]{1,0:T(8,128)S(1)}, u32[]{:S(2)}, u32[]{:S(2)}) collective-permute-start(f32[10,1024]{1,0:T(8,128)S(1)} %fusion), channel_id=1, source_target_pairs={{0,2},{1,5},{2,0},{3,7},{4,6},{5,1},{6,4},{7,3},{8,10},{9,13},{10,... | collective-permute-start | bytes 122888 | tf_op jit(solution)/shard_map/ppermute | solution.py:74
  214.8 4.3 %collective-permute-start.23 = (f32[10,1024]{1,0:T(8,128)S(1)}, f32[10,1024]{1,0:T(8,128)S(1)}, u32[]{:S(2)}, u32[]{:S(2)}) collective-permute-start(f32[10,1024]{1,0:T(8,128)S(1)} %fusion.16), channel_id=1, source_target_pairs={{0,4},{1,9},{2,6},{3,11},{4,0},{5,13},{6,2},{7,15},{8,12},{9,1},{1... | collective-permute-start | bytes 122888 | tf_op jit(solution)/shard_map/ppermute | solution.py:74
  219.1 4.3 %collective-permute-start.24 = (f32[10,1024]{1,0:T(8,128)S(1)}, f32[10,1024]{1,0:T(8,128)S(1)}, u32[]{:S(2)}, u32[]{:S(2)}) collective-permute-start(f32[10,1024]{1,0:T(8,128)S(1)} %add.159), channel_id=1, source_target_pairs={{0,8},{1,3},{2,10},{3,1},{4,12},{5,7},{6,14},{7,5},{8,0},{9,11},{1... | collective-permute-start | bytes 122888 | tf_op jit(solution)/shard_map/ppermute | solution.py:74
  223.5 5.5 %collective-permute-start.25 = (f32[10,1024]{1,0:T(8,128)S(1)}, f32[10,1024]{1,0:T(8,128)S(1)}, u32[]{:S(2)}, u32[]{:S(2)}) collective-permute-start(f32[10,1024]{1,0:T(8,128)S(1)} %add.160), channel_id=1, source_target_pairs={{0,16},{1,17},{2,18},{3,19},{4,20},{5,21},{6,22},{7,23},{8,24},{9,... | collective-permute-start | bytes 122888 | tf_op jit(solution)/shard_map/ppermute | solution.py:74
  (30 other events, 357.3 us)

commit v2 on v1

v2 whole, which is shorter than its diff:
```python
import functools
import math

import jax
import jax.numpy as jnp
from jax import lax
from jax.experimental import pallas as pl
from jax.experimental.pallas import tpu as pltpu
from jax.sharding import PartitionSpec as P

DH = 64
LANES = 128
EPSILON = 1e-06
TINIEST = 1e-30
NEGATIVE = -1e30
F32 = jnp.float32
BF16 = jnp.bfloat16
ROOT = math.sqrt(2.0 / math.pi)
CUBE = 0.044715
MIB = 1024 * 1024


def mm(a, b):
    return jnp.dot(a, b, preferred_element_type=F32)


def mm_nt(a, b):
    return lax.dot_general(a, b, (((1,), (1,)), ((), ())), preferred_element_type=F32)


def whole(shape):
    return pl.BlockSpec(shape, lambda *_: (0,) * len(shape))


def cost(flops, nbytes):
    return pl.CostEstimate(flops=int(flops), bytes_accessed=int(nbytes), transcendentals=0)


def inverse_rms(rows):
    return lax.rsqrt(jnp.mean(rows * rows, axis=-1, keepdims=True) + EPSILON)


def three_terms(values):
    high = values.astype(BF16)
    rest = values - high.astype(F32)
    middle = rest.astype(BF16)
    return high, middle, (rest - middle.astype(F32)).astype(BF16)


def bit_orders(n_wide):
    bits = n_wide.bit_length() - 1
    straight = list(range(bits))
    turned = straight[1:-1] + straight[:1] + straight[-1:] if bits > 2 else straight
    return straight, turned


def slot_table(wide_index, order, n_wide):
    bits = len(order)
    entries = []
    for slot in range(n_wide):
        mask = 0
        for stage, bit in enumerate(order):
            if slot >> (bits - 1 - stage) & 1:
                mask |= 1 << bit
        entries.append(mask)
    return jnp.bitwise_xor(jnp.asarray(entries, jnp.int32), wide_index.astype(jnp.int32))


def stage_exchange(values, stage, n_wide):
    orders = bit_orders(n_wide)
    pairs = []
    for wide in range(n_wide):
        for core in range(2):
            pairs.append((wide * 2 + core, (wide ^ (1 << orders[core][stage])) * 2 + core))
    return lax.ppermute(values, ("wide", "narrow"), pairs)


def swap(values):
    return lax.ppermute(values, "narrow", [(0, 1), (1, 0)])


def write_slots(table_ref, held_ref, targets, rows_each, more_ref=None):
    if targets[0].ndim == 2:
        more = 0.0 if more_ref is None else more_ref[...].astype(F32)
        targets[0][...] = (held_ref[...] + more).astype(BF16)
        return
    slot = 0
    for target in targets:
        for at in range(target.shape[0]):
            start = pl.multiple_of(table_ref[slot] * rows_each, 16)
            value = held_ref[pl.ds(start, rows_each), :]
            if more_ref is not None:
                value = value + more_ref[slot].astype(F32)
            target[at] = value.astype(BF16)
            slot += 1


def project_kernel(own_ref, other_ref, gain_ref, w_ref, normed_t_ref, projected_ref):
    count = own_ref.shape[0]
    for half, rows_ref in enumerate((own_ref, other_ref)):
        rows = rows_ref[...].astype(F32)
        normed = (rows * inverse_rms(rows) * gain_ref[...]).astype(BF16)
        at = slice(half * count, (half + 1) * count)
        normed_t_ref[:, at] = normed.T
        for i in range(3):
            projected_ref[i, at, :] = mm(normed, w_ref[i]).astype(BF16)


def project(own, other, gain, w_qkv):
    count, width = own.shape
    out = w_qkv.shape[2]
    return pl.pallas_call(
        project_kernel,
        out_shape=[
            jax.ShapeDtypeStruct((width, 2 * count), BF16),
            jax.ShapeDtypeStruct((3, 2 * count, out), BF16),
        ],
        cost_estimate=cost(12 * count * width * out, 8 * count * width),
        compiler_params=pltpu.CompilerParams(vmem_limit_bytes=10 * MIB),
        name="project",
    )(own, other, gain[None], w_qkv)


def key_lines(plot_slot, patch_mask, core):
    length = plot_slot.shape[0]
    turned = lambda values: jnp.roll(values, length // 2)
    live = jnp.where(core == 0, patch_mask, turned(patch_mask)) > 0
    same = plot_slot == turned(plot_slot)
    same = jnp.where(core == 0, same, turned(same))
    first = jnp.arange(length) < length // 2
    for_own = jnp.where(live & (first | same), 0.0, NEGATIVE)
    for_other = jnp.where(live & (~first | same), 0.0, NEGATIVE)
    return jnp.stack([for_own, for_other, live.astype(F32)])


def column(line):
    return jnp.broadcast_to(line, (LANES, line.shape[1])).T


def attention_kernel(qkv_ref, lines_ref, own_ref, other_ref, kept_ref, keys_ref, held, *, block):
    lane = lax.broadcasted_iota(jnp.int32, (1, LANES), 1)
    lows = (lane < DH, lane >= DH)
    within = jnp.bitwise_and(lane, DH - 1)

    @pl.when(pl.program_id(0) == 0)
    def _():
        ones = jnp.where((within >= 2) & (within < 5), 1.0, 0.0)
        bias = jnp.where(within == 1, column(lines_ref[1:2, :]), ones)
        keys_ref[...] = jnp.where(within == 0, column(lines_ref[0:1, :]), bias).astype(BF16)

    for head in range(2):
        held[head] = jnp.where(lows[head], qkv_ref[1], keys_ref[...])
        held[2 + head] = jnp.where(lows[head], qkv_ref[2], jnp.ones((1, LANES), BF16))
    half = own_ref.shape[0]
    for part, out_ref in enumerate((own_ref, other_ref)):

        def step(i, carry, part=part, out_ref=out_ref):
            inside = pl.ds(pl.multiple_of(i * block, block), block)
            rows = pl.ds(pl.multiple_of(part * half + i * block, block), block)
            queries = qkv_ref[0, rows, :] * jnp.asarray(1.0 / math.sqrt(DH), BF16)
            constants = jnp.where(within == part, 1.0, 0.0).astype(BF16)
            results = []
            for head in range(2):
                scores = mm_nt(jnp.where(lows[head], queries, constants), held[head])
                highest = jnp.max(scores, axis=1, keepdims=True)
                weights = jnp.exp(scores - highest).astype(BF16)
                mixed = mm(weights, held[2 + head])
                results.append(mixed / pltpu.roll(mixed, DH, 1))
                high, middle, low = three_terms(highest + jnp.log(mixed))
                base = DH * (1 - head)
                constants_back = jnp.where(
                    lane == base + 2,
                    -high,
                    jnp.where(lane == base + 3, -middle, jnp.where(lane == base + 4, -low, constants)),
                )
                kept_ref[head, rows, :] = jnp.where(lows[head], queries, constants_back)
            out_ref[inside, :] = jnp.where(lows[0], results[0], results[1]).astype(BF16)
            return carry

        lax.fori_loop(0, half // block, step, 0)


def attention(qkv, lines, block=512):
    length, width = qkv.shape[1:]
    pairs, half = width // LANES, length // 2
    return pl.pallas_call(
        functools.partial(attention_kernel, block=block),
        grid=(pairs,),
        in_specs=[
            pl.BlockSpec((3, length, LANES), lambda p: (0, 0, p)),
            whole(lines.shape),
        ],
        out_specs=[
            pl.BlockSpec((half, LANES), lambda p: (0, p)),
            pl.BlockSpec((half, LANES), lambda p: (0, p)),
            pl.BlockSpec((2, length, LANES), lambda p: (p, 0, 0)),
            whole((length, LANES)),
        ],
        out_shape=[
            jax.ShapeDtypeStruct((half, width), BF16),
            jax.ShapeDtypeStruct((half, width), BF16),
            jax.ShapeDtypeStruct((2 * pairs, length, LANES), BF16),
            jax.ShapeDtypeStruct((length, LANES), BF16),
        ],
        scratch_shapes=[pltpu.VMEM((4, length, LANES), BF16)],
        cost_estimate=cost(16 * pairs * length * length * LANES, 10 * length * width),
        compiler_params=pltpu.CompilerParams(vmem_limit_bytes=14 * MIB),
        name="attention",
    )(qkv, lines)


def middle_kernel(first, last, rows_each, *refs):
    refs = list(refs)
    take = lambda n: [refs.pop(0) for _ in range(n)]
    (table_ref,) = take(1)
    if first:
        (tokens_ref, own_ref, recv_ref, w_own_ref, w_recv_ref, gain_ref, cot_ref, lines_ref) = take(8)
    else:
        (normed, normed_t, seed, seed_t, total_in, back_in) = take(6)
        if last:
            (middle_ref, gain_ref) = take(2)
    (gu_ref, down_ref) = take(2)
    part_in = None if last is None else take(1)[0]
    if first:
        (middle_ref, normed, normed_t, seed, seed_t) = take(5)
    if last:
        (out_ref, grad_ref, attn_seed_ref, gain_part_ref) = take(4)
    else:
        (total_ref, back_ref) = take(2)
    part_refs = take(len(refs) - (3 if last else 1))
    (held,) = take(1)
    if last:
        (total_ref, back_ref) = take(2)
    step = pl.program_id(0)

    @pl.when(step == 0)
    def _():
        if first:
            middle = tokens_ref[...].astype(F32) + (
                mm(own_ref[...], w_own_ref[...]) + mm(recv_ref[...], w_recv_ref[...])
            )
            middle_ref[...] = middle
            total_ref[...] = middle
            back_ref[...] = jnp.zeros_like(back_ref)
            count = cot_ref.shape[0]
            live = column(lines_ref[2:3, 0:count])[:, 0:1]
            seed_value = (cot_ref[...].astype(F32) * live).astype(BF16)
            seed[...] = seed_value
            seed_t[...] = seed_value.T
            value = (middle * inverse_rms(middle) * gain_ref[...]).astype(BF16)
            normed[...] = value
            normed_t[...] = value.T
        else:
            total_ref[...] = total_in[...]
            back_ref[...] = back_in[...]

    gate = mm(normed[...], gu_ref[0])
    up = mm(normed[...], gu_ref[1])
    bent = jnp.tanh(ROOT * (gate + CUBE * gate * gate * gate))
    soft = 0.5 * gate * (1.0 + bent)
    slope = 0.5 * (1.0 + bent) + 0.5 * gate * (1.0 - bent * bent) * (ROOT * (1.0 + 3.0 * CUBE * gate * gate))
    hidden = (soft * up).astype(BF16)
    hidden_grad = mm_nt(seed[...], down_ref[...])
    gate_grad = (hidden_grad * up * slope).astype(BF16)
    up_grad = (hidden_grad * soft).astype(BF16)
    total_ref[...] += mm(hidden, down_ref[...])
    back_ref[...] += mm_nt(gate_grad, gu_ref[0]) + mm_nt(up_grad, gu_ref[1])
    chunk = gate.shape[1]
    held[:, 0:chunk] = mm(normed_t[...], gate_grad)
    held[:, chunk : 2 * chunk] = mm(normed_t[...], up_grad)
    held[:, 2 * chunk : 3 * chunk] = mm(seed_t[...], hidden)
    write_slots(table_ref, held, part_refs, rows_each, part_in)

    if last:

        @pl.when(step == pl.num_programs(0) - 1)
        def _():
            out_ref[...] = total_ref[...].astype(BF16)
            middle = middle_ref[...]
            factor = inverse_rms(middle)
            back = back_ref[...]
            scaled = back * gain_ref[...]
            inner = jnp.mean(scaled * middle, axis=-1, keepdims=True)
            grad = seed[...].astype(F32) + factor * scaled - middle * (factor * factor * factor * inner)
            grad_ref[...] = grad
            attn_seed_ref[...] = grad.astype(BF16)
            gain_part_ref[...] = jnp.sum(back * middle * factor, axis=0, keepdims=True)


def middle_call(first, last, inputs, w_gu, w_down, at, steps, part_in, table, n_wide, chunk):
    count, width = inputs[0].shape
    rows_each = width // n_wide
    tall = rows_each % 16 == 0
    rows, turned = (count, width), (width, count)
    columns = 3 * chunk * steps
    if tall:
        slots = [n_wide] if last is None else [n_wide // 2] * 2
        part_specs = [pl.BlockSpec((n, rows_each, 3 * chunk), lambda j, *_: (0, 0, j)) for n in slots]
        part_shapes = [jax.ShapeDtypeStruct((n, rows_each, columns), BF16) for n in slots]
    else:
        part_specs = [pl.BlockSpec((width, 3 * chunk), lambda j, *_: (0, j))]
        part_shapes = [jax.ShapeDtypeStruct((width, columns), BF16)]
    in_specs = [whole(v.shape) for v in inputs] + [
        pl.BlockSpec((2, width, chunk), lambda j, *_: (0, 0, at + j)),
        pl.BlockSpec((chunk, width), lambda j, *_: (at + j, 0)),
    ]
    inputs = [*inputs, w_gu, w_down]
    if last is not None:
        inputs.append(part_in)
        in_specs.append(
            pl.BlockSpec((n_wide, rows_each, 3 * chunk), lambda j, *_: (0, 0, j)) if tall else part_specs[0]
        )
    shape = jax.ShapeDtypeStruct
    scratch = [pltpu.VMEM((width, 3 * chunk), F32)]
    out_shape = []
    if first:
        out_shape += [shape(rows, F32), shape(rows, BF16), shape(turned, BF16), shape(rows, BF16), shape(turned, BF16)]
    if last:
        out_shape += [shape(rows, BF16), shape(rows, F32), shape(rows, BF16), shape((1, width), F32)]
        scratch += [pltpu.VMEM(rows, F32)] * 2
    else:
        out_shape += [shape(rows, F32)] * 2
    outs = pl.pallas_call(
        functools.partial(middle_kernel, first, last, rows_each),
        grid_spec=pltpu.PrefetchScalarGridSpec(
            num_scalar_prefetch=1,
            grid=(steps,),
            in_specs=in_specs,
            out_specs=[whole(s.shape) for s in out_shape] + part_specs,
            scratch_shapes=scratch,
        ),
        out_shape=out_shape + part_shapes,
        compiler_params=pltpu.CompilerParams(vmem_limit_bytes=24 * MIB),
        cost_estimate=cost(36 * count * width * chunk * steps, 32 * width * chunk * steps),
        name="middle",
    )(table, *inputs)
    parts = outs[len(out_shape) :]
    if not tall and last is not None:
        slots = in_slots(parts[0], table, n_wide)
        parts = [slots[: n_wide // 2], slots[n_wide // 2 :]]
    return outs[: len(out_shape)], parts


def in_slots(part, table, n_wide):
    return jnp.take(part.reshape(n_wide, -1, part.shape[-1]), table, axis=0)


def seeds_kernel(own_ref, other_ref, w_ref, grad_ref, seed_t_ref):
    count = own_ref.shape[0]
    for half, seed_ref in enumerate((own_ref, other_ref)):
        at = slice(half * count, (half + 1) * count)
        grad_ref[at, :] = mm_nt(seed_ref[...], w_ref[...]).astype(BF16)
        seed_t_ref[:, at] = seed_ref[...].T


def seeds_call(own, other, w_out):
    count, width = own.shape
    out = w_out.shape[0]
    return pl.pallas_call(
        seeds_kernel,
        out_shape=[
            jax.ShapeDtypeStruct((2 * count, out), BF16),
            jax.ShapeDtypeStruct((width, 2 * count), BF16),
        ],
        cost_estimate=cost(4 * count * width * out, 8 * count * width),
        compiler_params=pltpu.CompilerParams(vmem_limit_bytes=8 * MIB),
        name="seeds",
    )(own, other, w_out)


def attention_back_kernel(block, rows_each, split, carried, *refs):
    refs = list(refs)
    table_ref = refs.pop(0)
    (qkv_ref, grad_ref, mixed_own_ref, mixed_other_ref, kept_ref, keys_ref) = refs[:6]
    (normed_t_ref, seed_t_ref) = refs[6:8]
    refs = refs[8 + carried :]
    pieces = refs.pop(0)
    part_refs = [refs.pop(0) for _ in range(split)]
    grads, queries, query_total, mixed, held = refs
    lane = lax.broadcasted_iota(jnp.int32, (1, LANES), 1)
    lows = (lane < DH, lane >= DH)
    nothing = jnp.zeros((1, LANES), BF16)
    length = grad_ref.shape[0]
    half = length // 2
    mixed[0:half, :] = mixed_own_ref[...]
    mixed[half:length, :] = mixed_other_ref[...]
    product = grad_ref[...].astype(F32) * mixed[...].astype(F32)
    for head in range(2):
        base = DH * (1 - head)
        dots = jnp.sum(jnp.where(lows[head], product, 0.0), axis=1, keepdims=True)
        high, middle, low = three_terms(dots)
        constants = jnp.where(
            lane == base + 2,
            -high,
            jnp.where(lane == base + 3, -middle, jnp.where(lane == base + 4, -low, nothing)),
        )
        grads[head] = jnp.where(lows[head], grad_ref[...], constants)
        grads[2 + head] = jnp.where(lows[head], grad_ref[...], nothing)
        queries[head] = jnp.where(lows[head], kept_ref[head], nothing)
    query_total[...] = jnp.zeros_like(query_total)

    def step(i, carry):
        rows = pl.ds(pl.multiple_of(i * block, block), block)
        keys, values, constants = qkv_ref[1, rows, :], qkv_ref[2, rows, :], keys_ref[rows, :]
        key_grad, value_grad = [], []
        for head in range(2):
            base = DH * (1 - head)
            ones = jnp.where((lane >= base + 2) & (lane < base + 5), 1.0, 0.0).astype(BF16)
            keys_only = jnp.where(lows[head], keys, nothing) * jnp.asarray(1.0 / math.sqrt(DH), BF16)
            weights = jnp.exp(mm_nt(jnp.where(lows[head], keys, constants), kept_ref[head]))
            score_grads = weights * mm_nt(jnp.where(lows[head], values, ones), grads[head])
            score_grads = score_grads.astype(BF16)
            value_grad.append(mm(weights.astype(BF16), grads[2 + head]))
            key_grad.append(mm(score_grads, queries[head]))
            query_total[...] += mm(keys_only.T, score_grads)
        pieces[rows, LANES : 2 * LANES] = (key_grad[0] + key_grad[1]).astype(BF16)
        pieces[rows, 2 * LANES : 3 * LANES] = (value_grad[0] + value_grad[1]).astype(BF16)
        return carry

    lax.fori_loop(0, length // block, step, 0)
    pieces[:, 0:LANES] = query_total[...].T.astype(BF16)
    held[:, 0 : 3 * LANES] = mm(normed_t_ref[...], pieces[...])
    held[:, 3 * LANES : 4 * LANES] = mm(seed_t_ref[...], mixed[...])
    write_slots(table_ref, held, part_refs, rows_each)


def attention_back(pair, at, total, carried, qkv, grad, mixed_own, mixed_other, kept, keys, normed_t, seed_t, table, n_wide, block=512):
    length = qkv.shape[1]
    half = length // 2
    width = normed_t.shape[0]
    rows_each = width // n_wide
    tall = rows_each % 16 == 0
    columns = 4 * LANES
    if tall:
        part_specs = [pl.BlockSpec((n_wide // 2, rows_each, columns), lambda p, *_: (0, 0, at))] * 2
        part_shapes = [jax.ShapeDtypeStruct((n_wide // 2, rows_each, total * columns), BF16)] * 2
    else:
        part_specs = [pl.BlockSpec((width, columns), lambda p, *_: (0, at))]
        part_shapes = [jax.ShapeDtypeStruct((width, total * columns), BF16)]
    in_specs = [
        pl.BlockSpec((3, length, LANES), lambda p, *_: (0, 0, pair)),
        pl.BlockSpec((length, LANES), lambda p, *_: (0, pair)),
        pl.BlockSpec((half, LANES), lambda p, *_: (0, pair)),
        pl.BlockSpec((half, LANES), lambda p, *_: (0, pair)),
        pl.BlockSpec((2, length, LANES), lambda p, *_: (pair, 0, 0)),
        whole((length, LANES)),
        whole((width, length)),
        whole((width, length)),
    ]
    inputs = [qkv, grad, mixed_own, mixed_other, kept, keys, normed_t, seed_t]
    aliases = {1 + len(inputs) + i: 1 + i for i in range(len(carried))}
    outs = pl.pallas_call(
        functools.partial(attention_back_kernel, block, rows_each, len(part_specs), len(carried)),
        grid_spec=pltpu.PrefetchScalarGridSpec(
            num_scalar_prefetch=1,
            grid=(1,),
            in_specs=in_specs + [pl.BlockSpec(memory_space=pl.ANY)] * len(carried),
            out_specs=[whole((length, 3 * LANES))] + part_specs,
            scratch_shapes=[
                pltpu.VMEM((4, length, LANES), BF16),
                pltpu.VMEM((2, length, LANES), BF16),
                pltpu.VMEM((LANES, length), F32),
                pltpu.VMEM((length, LANES), BF16),
                pltpu.VMEM((width, columns), F32),
            ],
        ),
        out_shape=[jax.ShapeDtypeStruct((length, 3 * LANES), BF16)] + part_shapes,
        input_output_aliases=aliases,
        compiler_params=pltpu.CompilerParams(vmem_limit_bytes=24 * MIB),
        cost_estimate=cost(50 * length * length * LANES, 16 * length * LANES),
        name="attention_back",
    )(table, *inputs, *carried)
    return outs[0], list(outs[1:])


def kept_and_sent(parts, table, n_wide):
    if len(parts) == 2:
        return parts
    slots = in_slots(parts[0], table, n_wide)
    return slots[: n_wide // 2], slots[n_wide // 2 :]


def added(arrays, low, high):
    return sum(a[low:high].astype(F32) for a in arrays)


class Scatter:
    def __init__(self, keep, send, n_wide):
        self.pieces, self.send, self.n_wide, self.slots, self.stage = [keep], send, n_wide, n_wide // 2, 0

    def go(self):
        self.pieces.append(stage_exchange(self.send, self.stage, self.n_wide))
        self.stage += 1

    def turn(self):
        self.slots //= 2
        self.send = added(self.pieces, self.slots, 2 * self.slots).astype(BF16)
        return self.send

    @property
    def done(self):
        return self.slots == 1 and self.stage > 0 and self.stage == self.n_wide.bit_length() - 1

    def finish(self):
        while not self.done:
            self.turn()
            self.go()
        return [added(self.pieces[:-1], 0, 1), self.pieces[-1]]


def input_other_kernel(pairs, *refs):
    *piece_refs, w_ref, out_ref = refs
    back = 0.0
    for i in range(3):
        columns = slice(i * LANES, (i + 1) * LANES)
        back = back + mm_nt(jnp.concatenate([ref[:, columns] for ref in piece_refs], axis=1), w_ref[i])
    out_ref[...] = back.astype(BF16)


def input_other(pieces, w_qkv):
    length, columns = pieces[0].shape
    half, width = length // 2, w_qkv.shape[1]
    return pl.pallas_call(
        functools.partial(input_other_kernel, len(pieces)),
        grid=(1,),
        in_specs=[pl.BlockSpec((half, columns), lambda *_: (1, 0))] * len(pieces) + [whole(w_qkv.shape)],
        out_specs=whole((half, width)),
        out_shape=jax.ShapeDtypeStruct((half, width), BF16),
        compiler_params=pltpu.CompilerParams(vmem_limit_bytes=12 * MIB),
        cost_estimate=cost(2 * half * width * columns * len(pieces), 4 << 20),
        name="input_other",
    )(*pieces, w_qkv)


def input_grad_kernel(pairs, *refs):
    piece_refs, refs = refs[:pairs], refs[pairs:]
    w_ref, recv_ref, tokens_ref, gain_ref, middle_grad_ref, out_ref, part_ref = refs
    back = recv_ref[...].astype(F32)
    for i in range(3):
        columns = slice(i * LANES, (i + 1) * LANES)
        back = back + mm_nt(jnp.concatenate([ref[:, columns] for ref in piece_refs], axis=1), w_ref[i])
    rows = tokens_ref[...].astype(F32)
    factor = inverse_rms(rows)
    scaled = back * gain_ref[...]
    inner = jnp.mean(scaled * rows, axis=-1, keepdims=True)
    out_ref[...] = middle_grad_ref[...] + factor * scaled - rows * (factor * factor * factor * inner)
    part_ref[...] = jnp.sum(back * rows * factor, axis=0, keepdims=True)


def input_grad(pieces, w_qkv, recv, tokens, gain_line, middle_grad):
    count, width = tokens.shape
    columns = pieces[0].shape[1]
    rest = [w_qkv, recv, tokens, gain_line, middle_grad]
    return pl.pallas_call(
        functools.partial(input_grad_kernel, len(pieces)),
        grid=(1,),
        in_specs=[pl.BlockSpec((count, columns), lambda *_: (0, 0))] * len(pieces) + [whole(v.shape) for v in rest],
        out_specs=[whole((count, width)), whole((1, width))],
        out_shape=[jax.ShapeDtypeStruct((count, width), F32), jax.ShapeDtypeStruct((1, width), F32)],
        compiler_params=pltpu.CompilerParams(vmem_limit_bytes=16 * MIB),
        cost_estimate=cost(2 * count * width * columns * len(pieces), 8 << 20),
        name="input_grad",
    )(*pieces, *rest)


def padded(rows):
    return -(-rows // 8) * 8


def gather_kernel(counts, wides, chunk, *refs):
    refs = list(refs)
    groups = [[refs.pop(0) for _ in range(count)] for count in counts]
    attn_gain_ref, mlp_gain_ref, sums_ref = refs[:3]
    qkv_ref, out_ref, gu_ref, down_ref, columns_ref, pair_ref = refs[3:]
    sums = []
    for group in groups:
        total = group[0][0].astype(F32)
        for ref in group[1:]:
            total = total + ref[0].astype(F32)
        sums.append(total)
    wide_part, pair_parts = jnp.concatenate(sums[:wides], axis=1), sums[wides:]
    pairs = [part[:, i : i + 4 * LANES] for part in pair_parts for i in range(0, part.shape[1], 4 * LANES)]
    mats = [
        jnp.concatenate([pair[:, i * LANES : (i + 1) * LANES] for pair in pairs], axis=1) for i in range(4)
    ]
    kinds = [
        jnp.concatenate(
            [
                wide_part[:, j + i * chunk : j + (i + 1) * chunk]
                for j in range(0, wide_part.shape[1], 3 * chunk)
            ],
            axis=1,
        )
        for i in range(3)
    ]
    rows = wide_part.shape[0]
    for i in range(3):
        qkv_ref[i] = mats[i]
    for i in range(2):
        gu_ref[i] = kinds[i]
    out_ref[...] = mats[3]
    down_ref[...] = kinds[2]
    columns_ref[...] = jnp.zeros_like(columns_ref)
    lane = lax.broadcasted_iota(jnp.int32, (1, LANES), 1)
    row_sums = jnp.zeros((rows, LANES), F32)
    for i, value in enumerate((mats[0], mats[1], mats[2], mats[3], kinds[0], kinds[1], kinds[2])):
        squares = value * value
        columns_ref[i : i + 1, 0 : value.shape[1]] = jnp.sum(squares, axis=0, keepdims=True)
        row_sums = jnp.where(lane == i, jnp.sum(squares, axis=1, keepdims=True), row_sums)
    pair_ref[...] = jnp.zeros_like(pair_ref)
    pair_ref[0:rows, :] = row_sums
    at = padded(rows)
    for ref in (attn_gain_ref, mlp_gain_ref):
        for i in range(0, ref.shape[1], LANES):
            pair_ref[at : at + 1, :] = ref[:, i : i + LANES]
            at += 1
    pair_ref[at : at + 1, :] = sums_ref[...]


def gather_own(groups, wides, attn_gain_part, mlp_gain_part, local_sums, heads_width, units, chunk):
    rows = groups[0][0].shape[1]
    width = attn_gain_part.shape[1]
    pieces = [a for group in groups for a in group]
    lines = [attn_gain_part, mlp_gain_part, local_sums]
    shapes = [(3, rows, heads_width), (rows, heads_width), (2, rows, units), (rows, units)]
    shapes += [(8, max(heads_width, units, width)), (padded(rows) + padded(2 * width // LANES + 1), LANES)]
    return pl.pallas_call(
        functools.partial(gather_kernel, [len(g) for g in groups], wides, chunk),
        grid=(1,),
        in_specs=[pl.BlockSpec((1,) + a.shape[1:], lambda *_: (0, 0, 0)) for a in pieces]
        + [whole(a.shape) for a in lines],
        out_specs=[whole(s) for s in shapes],
        out_shape=[jax.ShapeDtypeStruct(s, F32) for s in shapes],
        compiler_params=pltpu.CompilerParams(vmem_limit_bytes=8 * MIB),
        cost_estimate=cost(1 << 20, 4 << 20),
        name="gather_own",
    )(*pieces, *lines)


def combine_kernel(rows, width, columns_ref, own_ref, recv_ref, summed_ref, pair_ref):
    pair = own_ref[...] + recv_ref[...]
    pair_ref[...] = pair
    summed_ref[...] = jnp.zeros_like(summed_ref)
    summed_ref[0:8, :] = columns_ref[...]
    summed_ref[7:8, 0:LANES] = jnp.sum(pair[0:rows, :], axis=0, keepdims=True)
    at = padded(rows)
    for line in (8, 9):
        for i in range(0, width, LANES):
            summed_ref[line : line + 1, i : i + LANES] = pair[at : at + 1, :]
            at += 1


def combine(columns, own, recv, rows, width):
    shapes = [(16, columns.shape[1]), own.shape]
    return pl.pallas_call(
        functools.partial(combine_kernel, rows, width),
        out_shape=[jax.ShapeDtypeStruct(s, F32) for s in shapes],
        compiler_params=pltpu.CompilerParams(vmem_limit_bytes=4 * MIB),
        name="combine",
    )(columns, own, recv)


def update_kernel(sizes, *refs):
    (whole_ref, scalar_ref, qkv_ref, out_ref, gu_ref, down_ref, summed_ref, pair_ref, prior_rows_ref) = refs[:9]
    (qkv_cols, out_rows, gu_cols, down_rows, w_qkv, w_out, w_gu, w_down) = refs[9:17]
    (qkv_new, out_new, gu_new, down_new, qkv_cols_new, out_rows_new, gu_cols_new, down_rows_new) = refs[17:25]
    (qkv_rows_new, out_cols_new, gu_rows_new, down_cols_new, attn_gain_ref, mlp_gain_ref, turned) = refs[25:]
    rows = qkv_ref.shape[1]
    width = sizes[0]
    lane = lax.broadcasted_iota(jnp.int32, (1, LANES), 1)
    beta = 1.0 - lax.rsqrt(jnp.full((1, 1), scalar_ref[0], F32))
    fresh = 1.0 - beta
    start = lax.rem(width - whole_ref[0] * rows, width)
    own = pltpu.roll(prior_rows_ref[...], start, 1)[:, 0:LANES]
    turned[...] = jnp.zeros_like(turned)
    turned[0:8, :] = own
    prior_columns = turned[...].T
    gains = pltpu.roll(summed_ref[8:16, 0:width], start, 1)
    attn_gain_ref[...] = jnp.reshape(gains[0:1, 0:rows], (rows,))
    mlp_gain_ref[...] = jnp.reshape(gains[1:2, 0:rows], (rows,))
    sums = pair_ref[pl.ds(padded(rows) + 2 * width // LANES, 1), :]
    totals = summed_ref[7:8, 0:LANES]
    all_rows = jnp.zeros((rows, LANES), F32)
    priors = [qkv_cols[0:1], qkv_cols[1:2], qkv_cols[2:3], out_rows[...], gu_cols[0:1], gu_cols[1:2], down_rows[...]]
    for i in range(7):
        across = sizes[1 + i]
        entries = float(across * width)
        row_new = beta * prior_columns[0:rows, i : i + 1] + fresh * (pair_ref[0:rows, i : i + 1] / across + TINIEST)
        count = priors[i].shape[1]
        col_new = beta * priors[i] + fresh * (summed_ref[i : i + 1, 0:count] / width + TINIEST)
        all_rows = jnp.where(lane == i, row_new, all_rows)
        if i in (3, 6):
            at = 7 + (i == 6)
            prior_mean = sums[:, at : at + 1] / across
        else:
            prior_mean = jnp.mean(prior_rows_ref[i : i + 1, :], axis=1, keepdims=True)
        mean = beta * prior_mean + fresh * (totals[:, i : i + 1] / entries + TINIEST)
        rate = scalar_ref[1] * jnp.sqrt(sums[:, i : i + 1] / entries)
        step = lax.rsqrt(row_new * col_new / mean)
        if i in (3, 6):
            gradient_ref, weight_ref, new_ref = ((out_ref, w_out, out_new), (down_ref, w_down, down_new))[i == 6]
            new_ref[...] = (weight_ref[...].astype(F32) - rate * (gradient_ref[...] * step)).astype(BF16)
            (out_rows_new, down_rows_new)[i == 6][...] = jnp.reshape(col_new, (count,))
        else:
            at = i if i < 3 else i - 4
            gradient_ref, weight_ref, new_ref = (qkv_ref, w_qkv, qkv_new) if i < 3 else (gu_ref, w_gu, gu_new)
            new_ref[at] = (weight_ref[at].astype(F32) - rate * (gradient_ref[at] * step)).astype(BF16)
            (qkv_cols_new if i < 3 else gu_cols_new)[at : at + 1] = col_new
    turned[0:rows, :] = all_rows
    rows_new = turned[...].T
    qkv_rows_new[...] = rows_new[0:3, 0:rows]
    out_cols_new[...] = jnp.reshape(rows_new[3:4, 0:rows], (rows,))
    gu_rows_new[...] = rows_new[4:6, 0:rows]
    down_cols_new[...] = jnp.reshape(rows_new[6:7, 0:rows], (rows,))


def update(place, scalars, grads, summed, pair, prior_rows, col_priors, weights, sizes):
    rows = grads[0].shape[1]
    inputs = [*grads, summed, pair, prior_rows, *col_priors, *weights]
    shapes = [(3, sizes[1] // 2), (sizes[4] // 2,), (2, sizes[5] // 2), (sizes[7] // 2,)]
    shapes += [(3, rows), (rows,), (2, rows), (rows,), (rows,), (rows,)]
    out_shape = [jax.ShapeDtypeStruct(w.shape, BF16) for w in weights]
    out_shape += [jax.ShapeDtypeStruct(s, F32) for s in shapes]
    return pl.pallas_call(
        functools.partial(update_kernel, sizes),
        grid_spec=pltpu.PrefetchScalarGridSpec(
            num_scalar_prefetch=2,
            grid=(1,),
            in_specs=[whole(a.shape) for a in inputs],
            out_specs=[whole(s.shape) for s in out_shape],
            scratch_shapes=[pltpu.VMEM((LANES, LANES), F32)],
        ),
        out_shape=out_shape,
        compiler_params=pltpu.CompilerParams(vmem_limit_bytes=8 * MIB),
        cost_estimate=cost(1 << 20, 4 << 20),
        name="update",
    )(place, scalars, *inputs)


def square_sum(values):
    wide = values.astype(F32)
    return jnp.sum(wide * wide, axis=(-2, -1))


def after(values, *others):
    return lax.optimization_barrier((values, *others))[0]


def body(
    n_wide,
    tokens,
    plot_slot,
    patch_mask,
    cotangent,
    gain_attn,
    w_qkv,
    w_out,
    gain_mlp,
    w_gu,
    w_down,
    qkv_rows,
    qkv_cols,
    out_rows,
    out_cols,
    gu_rows,
    gu_cols,
    down_rows,
    down_cols,
    step_count,
    learn_rate,
):
    width = tokens.shape[1]
    heads_width, units = w_out.shape[0], w_down.shape[0]
    rows_each = width // n_wide
    chunk = 256
    core = lax.axis_index("narrow")
    wide = lax.axis_index("wide")
    tables = [slot_table(wide, order, n_wide) for order in bit_orders(n_wide)]
    own_table = jnp.where(core == 0, tables[0], tables[1])
    other_table = jnp.where(core == 0, tables[1], tables[0])

    tokens_other = swap(tokens)
    lines = key_lines(plot_slot, patch_mask, core)
    normed_t, qkv = project(tokens, tokens_other, gain_attn, w_qkv)
    sent = after((w_out, w_gu, w_down), tokens_other)
    w_out_other, w_gu_other, w_down_other = swap(sent[0]), swap(sent[1]), swap(sent[2])
    mixed_own, mixed_other, kept, keys = attention(qkv, lines)
    mixed_recv = swap(mixed_other)
    gain_line = gain_mlp[None]
    steps = units // chunk // 2
    half = n_wide // 2

    (middle, *handed), (part_other,) = middle_call(
        True,
        None,
        [tokens, mixed_own, mixed_recv, w_out, w_out_other, gain_line, cotangent, lines],
        w_gu_other,
        w_down_other,
        0,
        steps,
        None,
        other_table,
        n_wide,
        chunk,
    )
    part_first = swap(part_other)
    totals, (part_other,) = middle_call(
        False, None, handed, w_gu_other, w_down_other, steps, steps, None, other_table, n_wide, chunk
    )
    part_second = swap(part_other)
    handed = [*handed[:4], *totals]
    totals, parts = middle_call(
        False, False, handed, w_gu, w_down, 0, steps, part_first, own_table, n_wide, chunk
    )
    wide_a = Scatter(*parts, n_wide)
    wide_a.go()
    handed = [*handed[:4], *totals]
    (mixed_out, middle_grad, attn_seed, mlp_gain_part), parts = middle_call(
        False, True, [*handed, middle, gain_line], w_gu, w_down, steps, steps, part_second, own_table, n_wide, chunk
    )
    wide_b = Scatter(*parts, n_wide)
    wide_b.go()
    mixed_grad, seed_t = seeds_call(attn_seed, swap(attn_seed), w_out)

    pairs = heads_width // LANES
    back = functools.partial(
        attention_back,
        qkv=qkv,
        mixed_own=mixed_own,
        mixed_other=mixed_other,
        kept=kept,
        keys=keys,
        normed_t=normed_t,
        seed_t=seed_t,
        table=own_table,
        n_wide=n_wide,
    )
    pieces = []
    piece, carried = back(0, 0, pairs - 1, [], grad=mixed_grad)
    pieces.append(piece)
    mixed_grad = after(mixed_grad, wide_a.turn())
    wide_a.go()
    for pair in range(1, pairs - 1):
        piece, carried = back(pair, pair, pairs - 1, carried, grad=mixed_grad)
        pieces.append(piece)
    first = Scatter(*kept_and_sent(carried, own_table, n_wide), n_wide)
    first.go()
    mixed_grad = after(mixed_grad, wide_a.turn(), wide_b.turn(), first.send)
    wide_a.go()
    wide_b.go()
    piece, carried = back(pairs - 1, 0, 1, [], grad=mixed_grad)
    pieces.append(piece)
    last = Scatter(*kept_and_sent(carried, own_table, n_wide), n_wide)
    last.go()
    groups = [wide_a.finish(), wide_b.finish(), first.finish(), last.finish()]
    back_other = swap(input_other(pieces, w_qkv))
    tokens_grad, attn_gain_part = input_grad(pieces, w_qkv, back_other, tokens, gain_attn[None], middle_grad)

    weights = after((w_qkv, w_out, w_gu, w_down, out_rows, down_rows, qkv_rows, out_cols, gu_rows, down_cols), piece)
    local_sums = jnp.concatenate(
        [square_sum(w.reshape(-1, *w.shape[-2:])) for w in weights[:4]]
        + [jnp.sum(weights[4])[None], jnp.sum(weights[5])[None], jnp.zeros((LANES - 9,), F32)]
    )[None]
    prior_rows = jnp.concatenate(
        [weights[6], weights[7][None], weights[8], weights[9][None], jnp.zeros((1, width), F32)], axis=0
    )

    def own_rows(values, dimension):
        return lax.dynamic_slice_in_dim(values, wide * rows_each, rows_each, dimension)

    own_weights = [own_rows(weights[0], 1), own_rows(weights[1], 1).T, own_rows(weights[2], 1), own_rows(weights[3], 1).T]

    *grads, columns, pair = gather_own(
        groups, 2, attn_gain_part, mlp_gain_part, local_sums, heads_width, units, chunk
    )
    summed, pair = combine(columns, pair, swap(pair), rows_each, width)
    for stage in range(n_wide.bit_length() - 1):
        summed = summed + stage_exchange(summed, stage, n_wide)
    outs = update(
        (wide.astype(jnp.int32))[None],
        jnp.stack([step_count.astype(F32), learn_rate]),
        grads,
        summed,
        pair,
        prior_rows,
        [qkv_cols, out_rows[None], gu_cols, down_rows[None]],
        own_weights,
        [width] + [2 * heads_width] * 4 + [2 * units] * 3,
    )
    qkv_new, out_new, gu_new, down_new, qkv_cols_new, out_rows_new, gu_cols_new, down_rows_new = outs[:8]
    qkv_rows_new, out_cols_new, gu_rows_new, down_cols_new, attn_gain_grad, mlp_gain_grad = outs[8:]
    qkv_grad, out_grad, gu_grad, down_grad = grads
    return (
        mixed_out,
        tokens_grad,
        attn_gain_grad,
        qkv_grad,
        out_grad.T,
        mlp_gain_grad,
        gu_grad,
        down_grad.T,
        qkv_new,
        out_new.T,
        gu_new,
        down_new.T,
        qkv_rows_new,
        qkv_cols_new,
        out_rows_new,
        out_cols_new,
        gu_rows_new,
        gu_cols_new,
        down_rows_new,
        down_cols_new,
    )


def solution(mesh):
    in_specs = (
        P(("wide", "narrow"), None),
        P("wide"),
        P("wide"),
        P(("wide", "narrow"), None),
        P(),
        P(None, None, "narrow"),
        P("narrow", None),
        P(),
        P(None, None, "narrow"),
        P("narrow", None),
        P(),
        P(None, "narrow"),
        P("narrow"),
        P(),
        P(),
        P(None, "narrow"),
        P("narrow"),
        P(),
        P(),
        P(),
    )
    out_specs = (
        P(("wide", "narrow"), None),
        P(("wide", "narrow"), None),
        P("wide"),
        P(None, "wide", "narrow"),
        P("narrow", "wide"),
        P("wide"),
        P(None, "wide", "narrow"),
        P("narrow", "wide"),
        P(None, "wide", "narrow"),
        P("narrow", "wide"),
        P(None, "wide", "narrow"),
        P("narrow", "wide"),
        P(None, "wide"),
        P(None, "narrow"),
        P("narrow"),
        P("wide"),
        P(None, "wide"),
        P(None, "narrow"),
        P("narrow"),
        P("wide"),
    )
    return jax.shard_map(
        functools.partial(body, mesh.shape["wide"]),
        mesh=mesh,
        in_specs=in_specs,
        out_specs=out_specs,
        check_vma=False,
    )
```

time: 247 us -> 200 us (0.81)
  waiting for transfers between devices: 43.1 us -> 22.1 us
  Pallas kernels: 107 us -> 88.8 us
  starting transfers between devices: 19.2 us -> 36.1 us
  other arithmetic: 35.5 us -> 21.4 us
  local copies, waits for them, and re-layouts: 33 us -> 25.4 us
    ppermute x16 -> x20, waiting for transfers between devices: 42.5 us -> 18.3 us  [stage_exchange(): return lax.ppermute(values, ('wide', 'narrow'), pairs)]
    ppermute x16 -> x20, starting transfers between devices: 17 us -> 31.1 us  [stage_exchange(): return lax.ppermute(values, ('wide', 'narrow'), pairs)]
    pallas_call x5 -> x10, Pallas kernels: 76.4 us -> 67.9 us  [the longest x4 30.9 us: middle_call(): pl.pallas_call(functools.partial(middle_kernel, first, last, rows_each),...]
    dynamic_slice x4 -> x2, local copies, waits for them, and re-layouts: 6.72 us -> 0.95 us  [own_rows(): lax.dynamic_slice_in_dim(values, wide * rows_each, rows_each, dimension)]
    convert_element_type x13 -> x12, other arithmetic: 19.1 us -> 14.9 us  [turn(): self.send = added(self.pieces, self.slots, 2 * self.slots).astype(BF16)]
    pallas_call x1, Pallas kernels: 6.69 us -> 2.91 us  [project(): pl.pallas_call(project_kernel, out_shape=[jax.ShapeDtypeStruct((width, 2...]
    optimization_barrier x0 -> x2, local copies, waits for them, and re-layouts: none -> 3.76 us  [after(): return lax.optimization_barrier((values, *others))[0]]
    slice x7 -> x3, local copies, waits for them, and re-layouts: 5.04 us -> 1.54 us  [key_lines(): turned = lambda values: jnp.roll(values, length // 2)]
  transfers between devices with their start and end apart: 26 -> 30, of which waited for: 7 -> 10; matrix products, arithmetic and copies ran while one was open for 21% -> 17% of each run, Pallas kernels for 36% -> 35%
where the time goes in v2:
time: 200 us; the launch traced here: 197 us
  Pallas kernels  88.8 us (44%)
  starting transfers between devices  36.1 us (18%)
  local copies, waits for them, and re-layouts  25.4 us (13%)
  waiting for transfers between devices  22.1 us (11%)
  other arithmetic  21.4 us (11%)
  between operations  2.85 us (1%)
    ppermute x20, starting transfers between devices, stage_exchange(): return lax.ppermute(values, ('wide', 'narrow'), pairs)  31.1 us
    pallas_call x4, Pallas kernels, middle_call(): pl.pallas_call(functools.partial(middle_kernel, first, last, rows_each),...  30.9 us
    pallas_call x3, Pallas kernels, attention_back(): pl.pallas_call(functools.partial(attention_back_kernel, block, rows_each,...  30.6 us
    ppermute x20, waiting for transfers between devices, stage_exchange(): return lax.ppermute(values, ('wide', 'narrow'), pairs)  18.3 us
    convert_element_type x12, other arithmetic, turn(): self.send = added(self.pieces, self.slots, 2 * self.slots).astype(BF16)  14.9 us
    unnamed x118, local copies, waits for them, and re-layouts  14.1 us
    pallas_call x1, Pallas kernels, attention(): pl.pallas_call(functools.partial(attention_kernel, block=block), grid=(pa...  12.6 us
    ppermute x10, starting transfers between devices, swap(): return lax.ppermute(values, 'narrow', [(0, 1), (1, 0)])  4.91 us
  transfers between devices with their start and end apart: 30, of which 10 were waited for; matrix products, arithmetic and copies ran while one was open for 17% of the time, Pallas kernels for 35%

profile of v2, /device:TPU:0, one launch (start us, length us, event | category | flops | bytes accessed | tf_op | source)
XLA Modules:
  0.0 196.6 jit_solution(16788972387356386030)
XLA Ops:
  1.2 2.1 %collective-permute-done.other_ref = bf16[512,768]{1,0:T(8,128)(2,1)S(1)} collective-permute-done((bf16[512,768]{1,0:T(8,128)(2,1)}, bf16[512,768]{1,0:T(8,128)(2,1)S(1)}, u32[]{:S(2)}, u32[]{:S(2)}) %collective-permute-start) | collective-permute-done | bytes 786464 | tf_op jit(solution)/shard_map/ppermute | solution.py:79
  10.2 2.9 %project.1 = (bf16[768,1024]{1,0:T(8,128)(2,1)S(1)}, bf16[3,1024,384]{2,1,0:T(8,128)(2,1)S(1)}) custom-call(bf16[512,768]{1,0:T(8,128)(2,1)S(1)} %copy-done.20, bf16[512,768]{1,0:T(8,128)(2,1)S(1)} %collective-permute-done.other_ref, f32[1,768]{1,0:T(1,128)S(1)} %broadcast_in_dim.47.gain_ref.refs_6_, bf16[3,768,384]{2,1,0:T(8,128)(2,1)S(1)} %copy-done), custom_call_target="tpu_custom_call" | custom-call | flops 1811939328 | bytes 3145728 | tf_op jit(solution)/shard_map/project/pallas_call | solution.py:112
  14.4 12.6 %attention.1 = (bf16[512,384]{1,0:T(8,128)(2,1)S(1)}, bf16[512,384]{1,0:T(8,128)(2,1)}, bf16[6,1024,128]{2,1,0:T(8,128)(2,1)S(1)}, bf16[1024,128]{1,0:T(8,128)(2,1)S(1)}) custom-call(bf16[3,1024,384]{2,1,0:T(8,128)(2,1)S(1)} %get-tuple-element.97.qkv_ref.refs_1_, f32[3,1024]{1,0:T(4,128)S(1)} %pad_maximum_fusion.lines_ref.refs_8_), custom_call_target="tpu_custom_call" | custom-call | flops 6442450944 | bytes 3932160 | tf_op jit(solution)/shard_map/attention/pallas_call | solution.py:186
  32.8 8.3 %middle.4 = (f32[512,768]{1,0:T(8,128)S(1)}, bf16[512,768]{1,0:T(8,128)(2,1)S(1)}, bf16[768,512]{1,0:T(8,128)(2,1)S(1)}, bf16[512,768]{1,0:T(8,128)(2,1)S(1)}, b...) custom-call(s32[16]{0:T(128)S(1)} %get-tuple-element.190.refs_0_, ...), custom_call_target="tpu_custom_call" | custom-call | flops 7247757312 | bytes 12582912 | tf_op jit(solution)/shard_map/middle/pallas_call | solution.py:323
  41.6 7.2 %middle.5 = (f32[512,768]{1,0:T(8,128)S(1)}, f32[512,768]{1,0:T(8,128)S(1)}, bf16[16,48,1536]{2,1,0:T(8,128)(2,1)S(1)}) custom-call(s32[16]{0:T(128)S(1)} %get-tuple-element.190.refs_0_, bf16[512,768]{1,0:T(8,128)(2,1)S(1)} %get-tuple-element.103.refs_1_, bf16[768,512]{1,0:T(8,128)(2,1)S(1)} %get-tuple-element.104.refs_2_, ...), custom_call_target="tpu_custom_call" | custom-call | flops 7247757312 | bytes 12582912 | tf_op jit(solution)/shard_map/middle/pallas_call | solution.py:323
  49.0 7.2 %middle.6 = (f32[512,768]{1,0:T(8,128)S(1)}, f32[512,768]{1,0:T(8,128)S(1)}, bf16[8,48,1536]{2,1,0:T(8,128)(2,1)S(1)}, bf16[8,48,1536]{2,1,0:T(8,128)(2,1)}) custom-call(s32[16]{0:T(128)S(1)} %get-tuple-element.191.refs_0_, bf16[512,768]{1,0:T(8,128)(2,1)S(1)} %get-tuple-element.103.refs_1_, bf16[768,512]{1,0:T(8,128)(2,1)S(1)} %get-tuple-element.104.refs_2_, ...), custom_call_target="tpu_custom_call" | custom-call | flops 7247757312 | bytes 12582912 | tf_op jit(solution)/shard_map/middle/pallas_call | solution.py:323
  57.4 8.2 %middle.7 = (bf16[512,768]{1,0:T(8,128)(2,1)}, f32[512,768]{1,0:T(8,128)S(1)}, bf16[512,768]{1,0:T(8,128)(2,1)}, f32[1,768]{1,0:T(1,128)S(1)}, bf16[8,48,1536]{2...) custom-call(s32[16]{0:T(128)S(1)} %get-tuple-element.191.refs_0_, bf16[512,768]{1,0:T(8,128)(2,1)S(1)} %get-tuple-element.103.refs_1_, ...), custom_call_target="tpu_custom_call" | custom-call | flops 7247757312 | bytes 12582912 | tf_op jit(solution)/shard_map/middle/pallas_call | solution.py:323
  68.1 2.8 %collective-permute-start.8 = (bf16[8,48,1536]{2,1,0:T(8,128)(2,1)}, bf16[8,48,1536]{2,1,0:T(8,128)(2,1)}, u32[]{:S(2)}, u32[]{:S(2)}) collective-permute-start(bf16[8,48,1536]{2,1,0:T(8,128)(2,1)} %get-tuple-element.125), channel_id=1, source_target_pairs={{0,2},{1,5},{2,0},{3,7},{4,6},{5,1},{6,4},{7,3},{8,10},{9,13},{10,... | collective-permute-start | bytes 3538952 | tf_op jit(solution)/shard_map/ppermute | solution.py:75
  72.4 2.5 %seeds.1 = (bf16[1024,384]{1,0:T(8,128)(2,1)S(1)}, bf16[768,1024]{1,0:T(8,128)(2,1)S(1)}) custom-call(bf16[512,768]{1,0:T(8,128)(2,1)} %get-tuple-element.117.own_ref, bf16[512,768]{1,0:T(8,128)(2,1)} %collective-permute-done.7.other_ref, bf16[384,768]{1,0:T(8,128)(2,1)S(1)} %copy-done.11), custom_call_target="tpu_custom_call" | custom-call | flops 603979776 | bytes 3145728 | tf_op jit(solution)/shard_map/seeds/pallas_call | solution.py:359
  78.1 10.3 %attention_back.3 = (bf16[1024,384]{1,0:T(8,128)(2,1)S(1)}, bf16[8,48,1024]{2,1,0:T(8,128)(2,1)S(1)}, bf16[8,48,1024]{2,1,0:T(8,128)(2,1)}) custom-call(s32[16]{0:T(128)S(1)} %get-tuple-element.191.refs_0_, bf16[3,1024,384]{2,1,0:T(8,128)(2,1)S(1)} %copy-done.35, bf16[1024,384]{1,0:T(8,128)(2,1)S(1)} %get-tuple-element.133.refs_2_, ...), custom_call_target="tpu_custom_call" | custom-call | flops 6710886400 | bytes 2097152 | tf_op jit(solution)/shard_map/attention_back/pallas_call | solution.py:452
  89.9 2.0 %collective-permute-start.9 = (bf16[4,48,1536]{2,1,0:T(8,128)(2,1)S(1)}, bf16[4,48,1536]{2,1,0:T(8,128)(2,1)S(1)}, u32[]{:S(2)}, u32[]{:S(2)}) collective-permute-start(bf16[4,48,1536]{2,1,0:T(8,128)(2,1)S(1)} %add_convert_fusion.1), channel_id=1, source_target_pairs={{0,4},{1,9},{2,6},{3,11},{4,0},{5,13},{6,2},{7,15},{8,12},{9,1},{1... | collective-permute-start | bytes 1769480 | tf_op jit(solution)/shard_map/ppermute | solution.py:75
  91.9 6.1 %collective-permute-done.10 = bf16[8,48,1536]{2,1,0:T(8,128)(2,1)S(1)} collective-permute-done((bf16[8,48,1536]{2,1,0:T(8,128)(2,1)}, bf16[8,48,1536]{2,1,0:T(8,128)(2,1)S(1)}, u32[]{:S(2)}, u32[]{:S(2)}) %collective-permute-start.10) | collective-permute-done | bytes 1179680 | tf_op jit(solution)/shard_map/ppermute | solution.py:75
  98.2 2.1 %collective-permute-start.14 = (bf16[4,48,1536]{2,1,0:T(8,128)(2,1)S(1)}, bf16[4,48,1536]{2,1,0:T(8,128)(2,1)S(1)}, u32[]{:S(2)}, u32[]{:S(2)}) collective-permute-start(bf16[4,48,1536]{2,1,0:T(8,128)(2,1)S(1)} %add_convert_fusion), channel_id=1, source_target_pairs={{0,4},{1,9},{2,6},{3,11},{4,0},{5,13},{6,2},{7,15},{8,12},{9,1},{1... | collective-permute-start | bytes 1769480 | tf_op jit(solution)/shard_map/ppermute | solution.py:75
  100.3 10.0 %attention_back.4 = (bf16[1024,384]{1,0:T(8,128)(2,1)S(1)}, bf16[8,48,1024]{2,1,0:T(8,128)(2,1)S(1)}, bf16[8,48,1024]{2,1,0:T(8,128)(2,1)}) custom-call(s32[16]{0:T(128)S(1)} %get-tuple-element.191.refs_0_, bf16[3,1024,384]{2,1,0:T(8,128)(2,1)S(1)} %copy-done.36, ...), custom_call_target="tpu_custom_call", output_to_operand_aliasing={{1}: (9, {}), {2}: (10, {})} | custom-call | flops 6710886400 | bytes 2097152 | tf_op jit(solution)/shard_map/attention_back/pallas_call | solution.py:452
  111.8 2.0 %add_convert_fusion.4 = bf16[2,48,1536]{2,1,0:T(8,128)(2,1)} fusion(bf16[4,48,1536]{2,1,0:T(8,128)(2,1)S(1)} %collective-permute-done.9, bf16[8,48,1536]{2,1,0:T(8,128)(2,1)} %collective-permute-done.8, bf16[8,48,1536]{2,1,0:T(8,128)(2,1)S(1)} %copy-done.17), kind=kLoop, calls=%fused_computation.8 | loop fusion | flops 884736 | bytes 1179648 | tf_op jit(solution)/shard_map/convert_element_type | solution.py:497
  115.3 10.3 %attention_back.5 = (bf16[1024,384]{1,0:T(8,128)(2,1)S(1)}, bf16[8,48,512]{2,1,0:T(8,128)(2,1)S(1)}, bf16[8,48,512]{2,1,0:T(8,128)(2,1)}) custom-call(s32[16]{0:T(128)S(1)} %get-tuple-element.191.refs_0_, bf16[3,1024,384]{2,1,0:T(8,128)(2,1)S(1)} %copy-done.36, bf16[1024,384]{1,0:T(8,128)(2,1)S(1)} %get-tuple-element.133.refs_2_, ...), custom_call_target="tpu_custom_call" | custom-call | flops 6710886400 | bytes 2097152 | tf_op jit(solution)/shard_map/attention_back/pallas_call | solution.py:452
  125.7 2.3 %input_other.1 = bf16[512,768]{1,0:T(8,128)(2,1)} custom-call(bf16[1024,384]{1,0:T(8,128)(2,1)S(1)} %get-tuple-element.123.refs_0_, bf16[1024,384]{1,0:T(8,128)(2,1)S(1)} %get-tuple-element.129.refs_1_, bf16[1024,384]{1,0:T(8,128)(2,1)S(1)} %get-tuple-element.134.refs_2_, bf16[3,768,384]{2,1,0:T(8,128)(2,1)S(1)} %copy-done.1), custom_call_target="tpu_custom_call" | custom-call | flops 905969664 | bytes 4194304 | tf_op jit(solution)/shard_map/input_other/pallas_call | solution.py:523
  128.0 2.2 %collective-permute-start.11 = (bf16[512,768]{1,0:T(8,128)(2,1)}, bf16[512,768]{1,0:T(8,128)(2,1)}, u32[]{:S(2)}, u32[]{:S(2)}) collective-permute-start(bf16[512,768]{1,0:T(8,128)(2,1)} %input_other.1), channel_id=1, source_target_pairs={{0,1},{1,0},{2,3},{3,2},{4,5},{5,4},{6,7},{7,6},{8,9},{9,8},{10,11... | collective-permute-start | bytes 2359304 | tf_op jit(solution)/shard_map/ppermute | solution.py:79
  130.2 2.0 %add_convert_fusion.3 = bf16[2,48,1536]{2,1,0:T(8,128)(2,1)} fusion(bf16[4,48,1536]{2,1,0:T(8,128)(2,1)S(1)} %collective-permute-done.14, bf16[8,48,1536]{2,1,0:T(8,128)(2,1)S(1)} %collective-permute-done.10, bf16[8,48,1536]{2,1,0:T(8,128)(2,1)} %copy-done.15), kind=kLoop, calls=%fused_computation.7 | loop fusion | flops 884736 | bytes 1179648 | tf_op jit(solution)/shard_map/convert_element_type | solution.py:497
  138.3 2.7 %concatenate.20 = f32[128]{0:T(128)S(1)} concatenate(f32[3]{0:T(128)S(1)} %multiply_reduce_fusion.1, f32[1]{0:T(128)} %bitcast.6, f32[2]{0:T(128)S(1)} %multiply_reduce_fusion, f32[1]{0:T(128)} %bitcast.7, f32[1]{0:T(128)} %bitcast.8, f32[1]{0:T(128)} %bitcast.9, f32[119]{0:T(128)S(1)} %broadcast_in_dim.54), dimensions={0} | concatenate | bytes 1024 | tf_op jit(solution)/shard_map/concatenate | solution.py:860
  144.4 2.7 %collective-permute-start.13 = (bf16[1,48,1536]{2,1,0:T(8,128)(2,1)S(1)}, bf16[1,48,1536]{2,1,0:T(8,128)(2,1)S(1)}, u32[]{:S(2)}, u32[]{:S(2)}) collective-permute-start(bf16[1,48,1536]{2,1,0:T(8,128)(2,1)S(1)} %get-tuple-element.178), channel_id=1, source_target_pairs={{0,16},{1,17},{2,18},{3,19},{4,20},{5,21},{6,22},{7,23},{8,24},{9,... | collective-permute-start | bytes 442376 | tf_op jit(solution)/shard_map/ppermute | solution.py:75
  158.4 2.8 %collective-permute-done.19 = bf16[2,48,1024]{2,1,0:T(8,128)(2,1)S(1)} collective-permute-done((bf16[2,48,1024]{2,1,0:T(8,128)(2,1)S(1)}, bf16[2,48,1024]{2,1,0:T(8,128)(2,1)S(1)}, u32[]{:S(2)}, u32[]{:S(2)}) %collective-permute-start.19) | collective-permute-done | bytes 196640 | tf_op jit(solution)/shard_map/ppermute | solution.py:75
  162.3 2.4 %collective-permute-start.20 = (bf16[1,48,1024]{2,1,0:T(8,128)(2,1)S(1)}, bf16[1,48,1024]{2,1,0:T(8,128)(2,1)S(1)}, u32[]{:S(2)}, u32[]{:S(2)}) collective-permute-start(bf16[1,48,1024]{2,1,0:T(8,128)(2,1)S(1)} %get-tuple-element.180), channel_id=1, source_target_pairs={{0,16},{1,17},{2,18},{3,19},{4,20},{5,21},{6,22},{7,23},{8,24},{9,... | collective-permute-start | bytes 294920 | tf_op jit(solution)/shard_map/ppermute | solution.py:75
  166.3 4.1 %input_grad.1 = (f32[512,768]{1,0:T(8,128)}, f32[1,768]{1,0:T(1,128)S(1)}) custom-call(bf16[1024,384]{1,0:T(8,128)(2,1)S(1)} %copy-done.6, bf16[1024,384]{1,0:T(8,128)(2,1)S(1)} %copy-done.8, bf16[1024,384]{1,0:T(8,128)(2,1)S(1)} %copy-done.10, bf16[3,768,384]{2,1,0:T(8,128)(2,1)S(1)} %copy-done.1, bf16[512,768]{1,0:T(8,128)(2,1)} %collective-permute-done.11.refs_4_, ...), custom_call_target="tpu_custom_call" | custom-call | flops 905969664 | bytes 8388608 | tf_op jit(solution)/shard_map/input_grad/pallas_call | solution.py:554
  171.7 2.1 %copy.44 = bf16[384,768]{0,1:T(8,128)(2,1)} copy(bf16[384,768]{1,0:T(8,128)(2,1)} %w_ref.3) | data formatting | bytes 1179648 | tf_op jit(solution)/shard_map/optimization_barrier | solution.py:746
  175.7 1.8 collective-permute-start.26
  180.0 2.0 %collective-permute-start.27 = (f32[16,1024]{1,0:T(8,128)S(1)}, f32[16,1024]{1,0:T(8,128)S(1)}, u32[]{:S(2)}, u32[]{:S(2)}) collective-permute-start(f32[16,1024]{1,0:T(8,128)S(1)} %add.162), channel_id=1, source_target_pairs={{0,4},{1,9},{2,6},{3,11},{4,0},{5,13},{6,2},{7,15},{8,12},{9,1},{1... | collective-permute-start | bytes 196616 | tf_op jit(solution)/shard_map/ppermute | solution.py:75
  182.0 2.3 %collective-permute-done.27 = f32[16,1024]{1,0:T(8,128)S(1)} collective-permute-done((f32[16,1024]{1,0:T(8,128)S(1)}, f32[16,1024]{1,0:T(8,128)S(1)}, u32[]{:S(2)}, u32[]{:S(2)}) %collective-permute-start.27) | collective-permute-done | bytes 65568 | tf_op jit(solution)/shard_map/ppermute | solution.py:75
  184.4 2.5 %collective-permute-start.28 = (f32[16,1024]{1,0:T(8,128)S(1)}, f32[16,1024]{1,0:T(8,128)S(1)}, u32[]{:S(2)}, u32[]{:S(2)}) collective-permute-start(f32[16,1024]{1,0:T(8,128)S(1)} %add.163), channel_id=1, source_target_pairs={{0,8},{1,3},{2,10},{3,1},{4,12},{5,7},{6,14},{7,5},{8,0},{9,11},{1... | collective-permute-start | bytes 196616 | tf_op jit(solution)/shard_map/ppermute | solution.py:75
  189.2 2.2 %collective-permute-start.29 = (f32[16,1024]{1,0:T(8,128)S(1)}, f32[16,1024]{1,0:T(8,128)S(1)}, u32[]{:S(2)}, u32[]{:S(2)}) collective-permute-start(f32[16,1024]{1,0:T(8,128)S(1)} %add.164), channel_id=1, source_target_pairs={{0,16},{1,17},{2,18},{3,19},{4,20},{5,21},{6,22},{7,23},{8,24},{9,... | collective-permute-start | bytes 196616 | tf_op jit(solution)/shard_map/ppermute | solution.py:75
  192.1 2.3 %collective-permute-done.29 = f32[16,1024]{1,0:T(8,128)S(1)} collective-permute-done((f32[16,1024]{1,0:T(8,128)S(1)}, f32[16,1024]{1,0:T(8,128)S(1)}, u32[]{:S(2)}, u32[]{:S(2)}) %collective-permute-start.29) | collective-permute-done | bytes 65568 | tf_op jit(solution)/shard_map/ppermute | solution.py:75
  194.5 1.9 update.1
  (208 shorter events, 58.8 us)
Async XLA Ops:
  0.7 2.7 %collective-permute-start = (bf16[512,768]{1,0:T(8,128)(2,1)}, bf16[512,768]{1,0:T(8,128)(2,1)S(1)}, u32[]{:S(2)}, u32[]{:S(2)}) collective-permute-start(bf16[512,768]{1,0:T(8,128)(2,1)} %refs_5_.1), channel_id=1, source_target_pairs={{0,1},{1,0},{2,3},{3,2},{4,5},{5,4},{6,7},{7,6},{8,9},{9,8},{10,11... | collective-permute-start | bytes 2359304 | tf_op jit(solution)/shard_map/ppermute | solution.py:79
  3.3 28.5 %collective-permute-start.3 = (bf16[2,768,1024]{2,1,0:T(8,128)(2,1)}, bf16[2,768,1024]{2,1,0:T(8,128)(2,1)}, u32[]{:S(2)}, u32[]{:S(2)}) collective-permute-start(bf16[2,768,1024]{2,1,0:T(8,128)(2,1)} %refs_9_.2), channel_id=1, source_target_pairs={{0,1},{1,0},{2,3},{3,2},{4,5},{5,4},{6,7},{7,6},{8,9},{9,8},{10,11... | collective-permute-start | bytes 9437192 | tf_op jit(solution)/shard_map/ppermute | solution.py:79
  5.9 25.8 %collective-permute-start.4 = (bf16[1024,768]{1,0:T(8,128)(2,1)}, bf16[1024,768]{1,0:T(8,128)(2,1)}, u32[]{:S(2)}, u32[]{:S(2)}) collective-permute-start(bf16[1024,768]{1,0:T(8,128)(2,1)} %refs_10_.1), channel_id=1, source_target_pairs={{0,1},{1,0},{2,3},{3,2},{4,5},{5,4},{6,7},{7,6},{8,9},{9,8},{10,11... | collective-permute-start | bytes 4718600 | tf_op jit(solution)/shard_map/ppermute | solution.py:79
  7.5 24.3 %collective-permute-start.2 = (bf16[384,768]{1,0:T(8,128)(2,1)}, bf16[384,768]{1,0:T(8,128)(2,1)S(1)}, u32[]{:S(2)}, u32[]{:S(2)}) collective-permute-start(bf16[384,768]{1,0:T(8,128)(2,1)} %w_ref.3), channel_id=1, source_target_pairs={{0,1},{1,0},{2,3},{3,2},{4,5},{5,4},{6,7},{7,6},{8,9},{9,8},{10,11... | collective-permute-start | bytes 1769480 | tf_op jit(solution)/shard_map/ppermute | solution.py:79
  29.6 2.2 %collective-permute-start.1 = (bf16[512,384]{1,0:T(8,128)(2,1)}, bf16[512,384]{1,0:T(8,128)(2,1)}, u32[]{:S(2)}, u32[]{:S(2)}) collective-permute-start(bf16[512,384]{1,0:T(8,128)(2,1)} %get-tuple-element.99.refs_4_), channel_id=1, source_target_pairs={{0,1},{1,0},{2,3},{3,2},{4,5},{5,4},{6,7},{7,6},{8,9},{9,8},{10,11... | collective-permute-start | bytes 1179656 | tf_op jit(solution)/shard_map/ppermute | solution.py:79
  41.1 7.9 %collective-permute-start.5 = (bf16[16,48,1536]{2,1,0:T(8,128)(2,1)S(1)}, bf16[16,48,1536]{2,1,0:T(8,128)(2,1)S(1)}, u32[]{:S(2)}, u32[]{:S(2)}) collective-permute-start(bf16[16,48,1536]{2,1,0:T(8,128)(2,1)S(1)} %get-tuple-element.111), channel_id=1, source_target_pairs={{0,1},{1,0},{2,3},{3,2},{4,5},{5,4},{6,7},{7,6},{8,9},{9,8},{10,11... | collective-permute-start | bytes 7077896 | tf_op jit(solution)/shard_map/ppermute | solution.py:79
  48.8 8.5 %collective-permute-start.6 = (bf16[16,48,1536]{2,1,0:T(8,128)(2,1)S(1)}, bf16[16,48,1536]{2,1,0:T(8,128)(2,1)S(1)}, u32[]{:S(2)}, u32[]{:S(2)}) collective-permute-start(bf16[16,48,1536]{2,1,0:T(8,128)(2,1)S(1)} %get-tuple-element.115), channel_id=1, source_target_pairs={{0,1},{1,0},{2,3},{3,2},{4,5},{5,4},{6,7},{7,6},{8,9},{9,8},{10,11... | collective-permute-start | bytes 7077896 | tf_op jit(solution)/shard_map/ppermute | solution.py:79
  67.8 4.6 %collective-permute-start.7 = (bf16[512,768]{1,0:T(8,128)(2,1)}, bf16[512,768]{1,0:T(8,128)(2,1)}, u32[]{:S(2)}, u32[]{:S(2)}) collective-permute-start(bf16[512,768]{1,0:T(8,128)(2,1)} %get-tuple-element.117.own_ref), channel_id=1, source_target_pairs={{0,1},{1,0},{2,3},{3,2},{4,5},{5,4},{6,7},{7,6},{8,9},{9,8},{10,11... | collective-permute-start | bytes 2359304 | tf_op jit(solution)/shard_map/ppermute | solution.py:79
  68.1 20.2 %collective-permute-start.8 = (bf16[8,48,1536]{2,1,0:T(8,128)(2,1)}, bf16[8,48,1536]{2,1,0:T(8,128)(2,1)}, u32[]{:S(2)}, u32[]{:S(2)}) collective-permute-start(bf16[8,48,1536]{2,1,0:T(8,128)(2,1)} %get-tuple-element.125), channel_id=1, source_target_pairs={{0,2},{1,5},{2,0},{3,7},{4,6},{5,1},{6,4},{7,3},{8,10},{9,13},{10,... | collective-permute-start | bytes 3538952 | tf_op jit(solution)/shard_map/ppermute | solution.py:75
  72.3 25.7 %collective-permute-start.10 = (bf16[8,48,1536]{2,1,0:T(8,128)(2,1)}, bf16[8,48,1536]{2,1,0:T(8,128)(2,1)S(1)}, u32[]{:S(2)}, u32[]{:S(2)}) collective-permute-start(bf16[8,48,1536]{2,1,0:T(8,128)(2,1)} %copy-done.32), channel_id=1, source_target_pairs={{0,2},{1,5},{2,0},{3,7},{4,6},{5,1},{6,4},{7,3},{8,10},{9,13},{10,... | collective-permute-start | bytes 3538952 | tf_op jit(solution)/shard_map/ppermute | solution.py:75
  88.3 37.3 %copy-start.5 = (bf16[1024,384]{1,0:T(8,128)(2,1)}, bf16[1024,384]{1,0:T(8,128)(2,1)S(1)}, u32[]{:S(2)}) copy-start(bf16[1024,384]{1,0:T(8,128)(2,1)S(1)} %get-tuple-element.123.refs_0_) | copy-start | bytes 2359300
  89.9 21.9 %collective-permute-start.9 = (bf16[4,48,1536]{2,1,0:T(8,128)(2,1)S(1)}, bf16[4,48,1536]{2,1,0:T(8,128)(2,1)S(1)}, u32[]{:S(2)}, u32[]{:S(2)}) collective-permute-start(bf16[4,48,1536]{2,1,0:T(8,128)(2,1)S(1)} %add_convert_fusion.1), channel_id=1, source_target_pairs={{0,4},{1,9},{2,6},{3,11},{4,0},{5,13},{6,2},{7,15},{8,12},{9,1},{1... | collective-permute-start | bytes 1769480 | tf_op jit(solution)/shard_map/ppermute | solution.py:75
  98.0 32.2 %copy-start.47 = (bf16[8,48,1536]{2,1,0:T(8,128)(2,1)}, bf16[8,48,1536]{2,1,0:T(8,128)(2,1)S(1)}, u32[]{:S(2)}) copy-start(bf16[8,48,1536]{2,1,0:T(8,128)(2,1)S(1)} %collective-permute-done.10) | copy-start | bytes 3538948
  98.2 32.0 %collective-permute-start.14 = (bf16[4,48,1536]{2,1,0:T(8,128)(2,1)S(1)}, bf16[4,48,1536]{2,1,0:T(8,128)(2,1)S(1)}, u32[]{:S(2)}, u32[]{:S(2)}) collective-permute-start(bf16[4,48,1536]{2,1,0:T(8,128)(2,1)S(1)} %add_convert_fusion), channel_id=1, source_target_pairs={{0,4},{1,9},{2,6},{3,11},{4,0},{5,13},{6,2},{7,15},{8,12},{9,1},{1... | collective-permute-start | bytes 1769480 | tf_op jit(solution)/shard_map/ppermute | solution.py:75
  110.3 30.7 %collective-permute-start.17 = (bf16[8,48,1024]{2,1,0:T(8,128)(2,1)}, bf16[8,48,1024]{2,1,0:T(8,128)(2,1)}, u32[]{:S(2)}, u32[]{:S(2)}) collective-permute-start(bf16[8,48,1024]{2,1,0:T(8,128)(2,1)} %get-tuple-element.132), channel_id=1, source_target_pairs={{0,2},{1,5},{2,0},{3,7},{4,6},{5,1},{6,4},{7,3},{8,10},{9,13},{10,... | collective-permute-start | bytes 2359304 | tf_op jit(solution)/shard_map/ppermute | solution.py:75
  113.8 29.1 %collective-permute-start.12 = (bf16[2,48,1536]{2,1,0:T(8,128)(2,1)}, bf16[2,48,1536]{2,1,0:T(8,128)(2,1)}, u32[]{:S(2)}, u32[]{:S(2)}) collective-permute-start(bf16[2,48,1536]{2,1,0:T(8,128)(2,1)} %add_convert_fusion.4), channel_id=1, source_target_pairs={{0,8},{1,3},{2,10},{3,1},{4,12},{5,7},{6,14},{7,5},{8,0},{9,11},{1... | collective-permute-start | bytes 884744 | tf_op jit(solution)/shard_map/ppermute | solution.py:75
  128.0 38.3 %collective-permute-start.11 = (bf16[512,768]{1,0:T(8,128)(2,1)}, bf16[512,768]{1,0:T(8,128)(2,1)}, u32[]{:S(2)}, u32[]{:S(2)}) collective-permute-start(bf16[512,768]{1,0:T(8,128)(2,1)} %input_other.1), channel_id=1, source_target_pairs={{0,1},{1,0},{2,3},{3,2},{4,5},{5,4},{6,7},{7,6},{8,9},{9,8},{10,11... | collective-permute-start | bytes 2359304 | tf_op jit(solution)/shard_map/ppermute | solution.py:79
  132.2 14.9 %collective-permute-start.15 = (bf16[2,48,1536]{2,1,0:T(8,128)(2,1)}, bf16[2,48,1536]{2,1,0:T(8,128)(2,1)}, u32[]{:S(2)}, u32[]{:S(2)}) collective-permute-start(bf16[2,48,1536]{2,1,0:T(8,128)(2,1)} %add_convert_fusion.3), channel_id=1, source_target_pairs={{0,8},{1,3},{2,10},{3,1},{4,12},{5,7},{6,14},{7,5},{8,0},{9,11},{1... | collective-permute-start | bytes 884744 | tf_op jit(solution)/shard_map/ppermute | solution.py:75
  132.7 16.3 %collective-permute-start.21 = (bf16[8,48,512]{2,1,0:T(8,128)(2,1)}, bf16[8,48,512]{2,1,0:T(8,128)(2,1)}, u32[]{:S(2)}, u32[]{:S(2)}) collective-permute-start(bf16[8,48,512]{2,1,0:T(8,128)(2,1)} %get-tuple-element.139), channel_id=1, source_target_pairs={{0,2},{1,5},{2,0},{3,7},{4,6},{5,1},{6,4},{7,3},{8,10},{9,13},{10,... | collective-permute-start | bytes 1179656 | tf_op jit(solution)/shard_map/ppermute | solution.py:75
  142.3 9.4 %collective-permute-start.18 = (bf16[4,48,1024]{2,1,0:T(8,128)(2,1)S(1)}, bf16[4,48,1024]{2,1,0:T(8,128)(2,1)S(1)}, u32[]{:S(2)}, u32[]{:S(2)}) collective-permute-start(bf16[4,48,1024]{2,1,0:T(8,128)(2,1)S(1)} %add_convert_fusion.2), channel_id=1, source_target_pairs={{0,4},{1,9},{2,6},{3,11},{4,0},{5,13},{6,2},{7,15},{8,12},{9,1},{1... | collective-permute-start | bytes 1179656 | tf_op jit(solution)/shard_map/ppermute | solution.py:75
  144.4 26.0 %collective-permute-start.13 = (bf16[1,48,1536]{2,1,0:T(8,128)(2,1)S(1)}, bf16[1,48,1536]{2,1,0:T(8,128)(2,1)S(1)}, u32[]{:S(2)}, u32[]{:S(2)}) collective-permute-start(bf16[1,48,1536]{2,1,0:T(8,128)(2,1)S(1)} %get-tuple-element.178), channel_id=1, source_target_pairs={{0,16},{1,17},{2,18},{3,19},{4,20},{5,21},{6,22},{7,23},{8,24},{9,... | collective-permute-start | bytes 442376 | tf_op jit(solution)/shard_map/ppermute | solution.py:75
  148.6 21.8 %collective-permute-start.16 = (bf16[1,48,1536]{2,1,0:T(8,128)(2,1)S(1)}, bf16[1,48,1536]{2,1,0:T(8,128)(2,1)S(1)}, u32[]{:S(2)}, u32[]{:S(2)}) collective-permute-start(bf16[1,48,1536]{2,1,0:T(8,128)(2,1)S(1)} %get-tuple-element.176), channel_id=1, source_target_pairs={{0,16},{1,17},{2,18},{3,19},{4,20},{5,21},{6,22},{7,23},{8,24},{9,... | collective-permute-start | bytes 442376 | tf_op jit(solution)/shard_map/ppermute | solution.py:75
  150.1 5.7 %collective-permute-start.22 = (bf16[4,48,512]{2,1,0:T(8,128)(2,1)S(1)}, bf16[4,48,512]{2,1,0:T(8,128)(2,1)S(1)}, u32[]{:S(2)}, u32[]{:S(2)}) collective-permute-start(bf16[4,48,512]{2,1,0:T(8,128)(2,1)S(1)} %add_convert_fusion.5), channel_id=1, source_target_pairs={{0,4},{1,9},{2,6},{3,11},{4,0},{5,13},{6,2},{7,15},{8,12},{9,1},{1... | collective-permute-start | bytes 589832 | tf_op jit(solution)/shard_map/ppermute | solution.py:75
  152.7 8.5 %collective-permute-start.19 = (bf16[2,48,1024]{2,1,0:T(8,128)(2,1)S(1)}, bf16[2,48,1024]{2,1,0:T(8,128)(2,1)S(1)}, u32[]{:S(2)}, u32[]{:S(2)}) collective-permute-start(bf16[2,48,1024]{2,1,0:T(8,128)(2,1)S(1)} %add_convert_fusion.6), channel_id=1, source_target_pairs={{0,8},{1,3},{2,10},{3,1},{4,12},{5,7},{6,14},{7,5},{8,0},{9,11},{1... | collective-permute-start | bytes 589832 | tf_op jit(solution)/shard_map/ppermute | solution.py:75
  156.8 8.0 %collective-permute-start.23 = (bf16[2,48,512]{2,1,0:T(8,128)(2,1)S(1)}, bf16[2,48,512]{2,1,0:T(8,128)(2,1)S(1)}, u32[]{:S(2)}, u32[]{:S(2)}) collective-permute-start(bf16[2,48,512]{2,1,0:T(8,128)(2,1)S(1)} %add_convert_fusion.9), channel_id=1, source_target_pairs={{0,8},{1,3},{2,10},{3,1},{4,12},{5,7},{6,14},{7,5},{8,0},{9,11},{1... | collective-permute-start | bytes 294920 | tf_op jit(solution)/shard_map/ppermute | solution.py:75
  162.3 8.4 %collective-permute-start.20 = (bf16[1,48,1024]{2,1,0:T(8,128)(2,1)S(1)}, bf16[1,48,1024]{2,1,0:T(8,128)(2,1)S(1)}, u32[]{:S(2)}, u32[]{:S(2)}) collective-permute-start(bf16[1,48,1024]{2,1,0:T(8,128)(2,1)S(1)} %get-tuple-element.180), channel_id=1, source_target_pairs={{0,16},{1,17},{2,18},{3,19},{4,20},{5,21},{6,22},{7,23},{8,24},{9,... | collective-permute-start | bytes 294920 | tf_op jit(solution)/shard_map/ppermute | solution.py:75
  165.6 5.1 %collective-permute-start.24 = (bf16[1,48,512]{2,1,0:T(8,128)(2,1)S(1)}, bf16[1,48,512]{2,1,0:T(8,128)(2,1)S(1)}, u32[]{:S(2)}, u32[]{:S(2)}) collective-permute-start(bf16[1,48,512]{2,1,0:T(8,128)(2,1)S(1)} %get-tuple-element.182), channel_id=1, source_target_pairs={{0,16},{1,17},{2,18},{3,19},{4,20},{5,21},{6,22},{7,23},{8,24},{9,... | collective-permute-start | bytes 147464 | tf_op jit(solution)/shard_map/ppermute | solution.py:75
  171.6 4.0 %collective-permute-start.25 = (f32[64,128]{1,0:T(8,128)S(1)}, f32[64,128]{1,0:T(8,128)S(1)}, u32[]{:S(2)}, u32[]{:S(2)}) collective-permute-start(f32[64,128]{1,0:T(8,128)S(1)} %get-tuple-element.153.own_ref), channel_id=1, source_target_pairs={{0,1},{1,0},{2,3},{3,2},{4,5},{5,4},{6,7},{7,6},{8,9},{9,8},{10,11... | collective-permute-start | bytes 98312 | tf_op jit(solution)/shard_map/ppermute | solution.py:79
  175.7 4.3 %collective-permute-start.26 = (f32[16,1024]{1,0:T(8,128)S(1)}, f32[16,1024]{1,0:T(8,128)S(1)}, u32[]{:S(2)}, u32[]{:S(2)}) collective-permute-start(f32[16,1024]{1,0:T(8,128)S(1)} %get-tuple-element.154), channel_id=1, source_target_pairs={{0,2},{1,5},{2,0},{3,7},{4,6},{5,1},{6,4},{7,3},{8,10},{9,13},{10,... | collective-permute-start | bytes 196616 | tf_op jit(solution)/shard_map/ppermute | solution.py:75
  180.0 4.3 %collective-permute-start.27 = (f32[16,1024]{1,0:T(8,128)S(1)}, f32[16,1024]{1,0:T(8,128)S(1)}, u32[]{:S(2)}, u32[]{:S(2)}) collective-permute-start(f32[16,1024]{1,0:T(8,128)S(1)} %add.162), channel_id=1, source_target_pairs={{0,4},{1,9},{2,6},{3,11},{4,0},{5,13},{6,2},{7,15},{8,12},{9,1},{1... | collective-permute-start | bytes 196616 | tf_op jit(solution)/shard_map/ppermute | solution.py:75
  184.4 4.8 %collective-permute-start.28 = (f32[16,1024]{1,0:T(8,128)S(1)}, f32[16,1024]{1,0:T(8,128)S(1)}, u32[]{:S(2)}, u32[]{:S(2)}) collective-permute-start(f32[16,1024]{1,0:T(8,128)S(1)} %add.163), channel_id=1, source_target_pairs={{0,8},{1,3},{2,10},{3,1},{4,12},{5,7},{6,14},{7,5},{8,0},{9,11},{1... | collective-permute-start | bytes 196616 | tf_op jit(solution)/shard_map/ppermute | solution.py:75
  189.2 5.2 %collective-permute-start.29 = (f32[16,1024]{1,0:T(8,128)S(1)}, f32[16,1024]{1,0:T(8,128)S(1)}, u32[]{:S(2)}, u32[]{:S(2)}) collective-permute-start(f32[16,1024]{1,0:T(8,128)S(1)} %add.164), channel_id=1, source_target_pairs={{0,16},{1,17},{2,18},{3,19},{4,20},{5,21},{6,22},{7,23},{8,24},{9,... | collective-permute-start | bytes 196616 | tf_op jit(solution)/shard_map/ppermute | solution.py:75
  (57 other events, 528.9 us)

commit v3 on v2

--- a/solution.py
+++ b/solution.py
@@ -18,6 +18,7 @@
 ROOT = math.sqrt(2.0 / math.pi)
 CUBE = 0.044715
 MIB = 1024 * 1024
+LIVE = 5
 
 
 def mm(a, b):
@@ -54,16 +55,19 @@
     return straight, turned
 
 
-def slot_table(wide_index, order, n_wide):
-    bits = len(order)
-    entries = []
-    for slot in range(n_wide):
-        mask = 0
-        for stage, bit in enumerate(order):
-            if slot >> (bits - 1 - stage) & 1:
-                mask |= 1 << bit
-        entries.append(mask)
-    return jnp.bitwise_xor(jnp.asarray(entries, jnp.int32), wide_index.astype(jnp.int32))
+def slot_masks(n_wide):
+    bits = n_wide.bit_length() - 1
+    return [
+        [sum(1 << bit for stage, bit in enumerate(order) if slot >> (bits - 1 - stage) & 1) for slot in range(n_wide)]
+        for order in bit_orders(n_wide)
+    ]
+
+
+def slot_row(slot, n_wide, turned):
+    masks = slot_masks(n_wide)
+    wide, core = lax.axis_index("wide"), lax.axis_index("narrow")
+    first, second = masks[turned][slot], masks[1 - turned][slot]
+    return jnp.bitwise_xor(wide, first + (second - first) * core)
 
 
 def stage_exchange(values, stage, n_wide):
@@ -79,7 +83,7 @@
     return lax.ppermute(values, "narrow", [(0, 1), (1, 0)])
 
 
-def write_slots(table_ref, held_ref, targets, rows_each, more_ref=None):
+def write_slots(turned, n_wide, held_ref, targets, rows_each, more_ref=None):
     if targets[0].ndim == 2:
         more = 0.0 if more_ref is None else more_ref[...].astype(F32)
         targets[0][...] = (held_ref[...] + more).astype(BF16)
@@ -87,7 +91,7 @@
     slot = 0
     for target in targets:
         for at in range(target.shape[0]):
-            start = pl.multiple_of(table_ref[slot] * rows_each, 16)
+            start = pl.multiple_of(slot_row(slot, n_wide, turned) * rows_each, 16)
             value = held_ref[pl.ds(start, rows_each), :]
             if more_ref is not None:
                 value = value + more_ref[slot].astype(F32)
@@ -95,49 +99,64 @@
             slot += 1
 
 
-def project_kernel(own_ref, other_ref, gain_ref, w_ref, normed_t_ref, projected_ref):
-    count = own_ref.shape[0]
-    for half, rows_ref in enumerate((own_ref, other_ref)):
-        rows = rows_ref[...].astype(F32)
-        normed = (rows * inverse_rms(rows) * gain_ref[...]).astype(BF16)
-        at = slice(half * count, (half + 1) * count)
-        normed_t_ref[:, at] = normed.T
-        for i in range(3):
-            projected_ref[i, at, :] = mm(normed, w_ref[i]).astype(BF16)
-
-
-def project(own, other, gain, w_qkv):
-    count, width = own.shape
+def in_slots(part, n_wide):
+    rows = jnp.stack([slot_row(slot, n_wide, 0) for slot in range(n_wide)])
+    return jnp.take(part.reshape(n_wide, -1, part.shape[-1]), rows, axis=0)
+
+
+def as_line(ref):
+    return jnp.reshape(ref[...], (1, ref.shape[0]))
+
+
+def project_kernel(carried, rows_ref, gain_ref, w_ref, *refs):
+    normed_t_ref, projected_ref = refs[carried:]
+    rows = rows_ref[...].astype(F32)
+    normed = (rows * inverse_rms(rows) * as_line(gain_ref)).astype(BF16)
+    normed_t_ref[...] = normed.T
+    for i in range(3):
+        projected_ref[i] = mm(normed, w_ref[i]).astype(BF16)
+
+
+def project(half, tokens, gain, w_qkv, carried):
+    count, width = tokens.shape
     out = w_qkv.shape[2]
+    inputs = [tokens, gain, w_qkv]
     return pl.pallas_call(
-        project_kernel,
+        functools.partial(project_kernel, len(carried)),
+        grid=(1,),
+        in_specs=[whole(v.shape) for v in inputs] + [pl.BlockSpec(memory_space=pl.ANY)] * len(carried),
+        out_specs=[
+            pl.BlockSpec((width, count), lambda *_: (0, half)),
+            pl.BlockSpec((3, count, out), lambda *_: (0, half, 0)),
+        ],
         out_shape=[
             jax.ShapeDtypeStruct((width, 2 * count), BF16),
             jax.ShapeDtypeStruct((3, 2 * count, out), BF16),
         ],
-        cost_estimate=cost(12 * count * width * out, 8 * count * width),
-        compiler_params=pltpu.CompilerParams(vmem_limit_bytes=10 * MIB),
+        input_output_aliases={len(inputs) + i: i for i in range(len(carried))},
+        cost_estimate=cost(6 * count * width * out, 4 * count * width),
+        compiler_params=pltpu.CompilerParams(vmem_limit_bytes=8 * MIB),
         name="project",
-    )(own, other, gain[None], w_qkv)
-
-
-def key_lines(plot_slot, patch_mask, core):
-    length = plot_slot.shape[0]
-    turned = lambda values: jnp.roll(values, length // 2)
-    live = jnp.where(core == 0, patch_mask, turned(patch_mask)) > 0
-    same = plot_slot == turned(plot_slot)
-    same = jnp.where(core == 0, same, turned(same))
-    first = jnp.arange(length) < length // 2
-    for_own = jnp.where(live & (first | same), 0.0, NEGATIVE)
-    for_other = jnp.where(live & (~first | same), 0.0, NEGATIVE)
-    return jnp.stack([for_own, for_other, live.astype(F32)])
+    )(*inputs, *carried)
+
+
+def key_lines(slot_ref, mask_ref, core):
+    slot, mask = as_line(slot_ref), as_line(mask_ref)
+    length = mask.shape[1]
+    turned = lambda values: pltpu.roll(values, length // 2, 1)
+    live = mask + (turned(mask) - mask) * core
+    same = jnp.where(slot == turned(slot), live, 0)
+    first = lax.broadcasted_iota(jnp.int32, (1, length), 1) < length // 2
+    for_own = jnp.where(jnp.where(first, live, same) > 0, 0.0, NEGATIVE)
+    for_other = jnp.where(jnp.where(first, same, live) > 0, 0.0, NEGATIVE)
+    return for_own, for_other, live.astype(F32)
 
 
 def column(line):
     return jnp.broadcast_to(line, (LANES, line.shape[1])).T
 
 
-def attention_kernel(qkv_ref, lines_ref, own_ref, other_ref, kept_ref, keys_ref, held, *, block):
+def attention_kernel(qkv_ref, slot_ref, mask_ref, own_ref, other_ref, kept_ref, keys_ref, held, *, block):
     lane = lax.broadcasted_iota(jnp.int32, (1, LANES), 1)
     lows = (lane < DH, lane >= DH)
     within = jnp.bitwise_and(lane, DH - 1)
@@ -145,8 +164,9 @@
     @pl.when(pl.program_id(0) == 0)
     def _():
         ones = jnp.where((within >= 2) & (within < 5), 1.0, 0.0)
-        bias = jnp.where(within == 1, column(lines_ref[1:2, :]), ones)
-        keys_ref[...] = jnp.where(within == 0, column(lines_ref[0:1, :]), bias).astype(BF16)
+        for_own, for_other, live = key_lines(slot_ref, mask_ref, lax.axis_index("narrow"))
+        bias = jnp.where(within == 1, column(for_other), jnp.where(within == LIVE, column(live), ones))
+        keys_ref[...] = jnp.where(within == 0, column(for_own), bias).astype(BF16)
 
     for head in range(2):
         held[head] = jnp.where(lows[head], qkv_ref[1], keys_ref[...])
@@ -180,7 +200,7 @@
         lax.fori_loop(0, half // block, step, 0)
 
 
-def attention(qkv, lines, block=512):
+def attention(qkv, plot_slot, patch_mask, block=512):
     length, width = qkv.shape[1:]
     pairs, half = width // LANES, length // 2
     return pl.pallas_call(
@@ -188,7 +208,8 @@
         grid=(pairs,),
         in_specs=[
             pl.BlockSpec((3, length, LANES), lambda p: (0, 0, p)),
-            whole(lines.shape),
+            whole(plot_slot.shape),
+            whole(patch_mask.shape),
         ],
         out_specs=[
             pl.BlockSpec((half, LANES), lambda p: (0, p)),
@@ -196,25 +217,24 @@
             pl.BlockSpec((2, length, LANES), lambda p: (p, 0, 0)),
             whole((length, LANES)),
         ],
+        scratch_shapes=[pltpu.VMEM((4, length, LANES), BF16)],
         out_shape=[
             jax.ShapeDtypeStruct((half, width), BF16),
             jax.ShapeDtypeStruct((half, width), BF16),
             jax.ShapeDtypeStruct((2 * pairs, length, LANES), BF16),
             jax.ShapeDtypeStruct((length, LANES), BF16),
         ],
-        scratch_shapes=[pltpu.VMEM((4, length, LANES), BF16)],
         cost_estimate=cost(16 * pairs * length * length * LANES, 10 * length * width),
-        compiler_params=pltpu.CompilerParams(vmem_limit_bytes=14 * MIB),
+        compiler_params=pltpu.CompilerParams(vmem_limit_bytes=11 * MIB),
         name="attention",
-    )(qkv, lines)
-
-
-def middle_kernel(first, last, rows_each, *refs):
+    )(qkv, plot_slot, patch_mask)
+
+
+def middle_kernel(first, last, rows_each, n_wide, *refs):
     refs = list(refs)
     take = lambda n: [refs.pop(0) for _ in range(n)]
-    (table_ref,) = take(1)
     if first:
-        (tokens_ref, own_ref, recv_ref, w_own_ref, w_recv_ref, gain_ref, cot_ref, lines_ref) = take(8)
+        (tokens_ref, own_ref, recv_ref, w_own_ref, w_recv_ref, gain_ref, cot_ref, keys_ref) = take(8)
     else:
         (normed, normed_t, seed, seed_t, total_in, back_in) = take(6)
         if last:
@@ -242,12 +262,11 @@
             middle_ref[...] = middle
             total_ref[...] = middle
             back_ref[...] = jnp.zeros_like(back_ref)
-            count = cot_ref.shape[0]
-            live = column(lines_ref[2:3, 0:count])[:, 0:1]
+            live = keys_ref[...].astype(F32)[:, LIVE : LIVE + 1]
             seed_value = (cot_ref[...].astype(F32) * live).astype(BF16)
             seed[...] = seed_value
             seed_t[...] = seed_value.T
-            value = (middle * inverse_rms(middle) * gain_ref[...]).astype(BF16)
+            value = (middle * inverse_rms(middle) * as_line(gain_ref)).astype(BF16)
             normed[...] = value
             normed_t[...] = value.T
         else:
@@ -269,7 +288,7 @@
     held[:, 0:chunk] = mm(normed_t[...], gate_grad)
     held[:, chunk : 2 * chunk] = mm(normed_t[...], up_grad)
     held[:, 2 * chunk : 3 * chunk] = mm(seed_t[...], hidden)
-    write_slots(table_ref, held, part_refs, rows_each, part_in)
+    write_slots(int(last is None), n_wide, held, part_refs, rows_each, part_in)
 
     if last:
 
@@ -279,7 +298,7 @@
             middle = middle_ref[...]
             factor = inverse_rms(middle)
             back = back_ref[...]
-            scaled = back * gain_ref[...]
+            scaled = back * as_line(gain_ref)
             inner = jnp.mean(scaled * middle, axis=-1, keepdims=True)
             grad = seed[...].astype(F32) + factor * scaled - middle * (factor * factor * factor * inner)
             grad_ref[...] = grad
@@ -287,7 +306,7 @@
             gain_part_ref[...] = jnp.sum(back * middle * factor, axis=0, keepdims=True)
 
 
-def middle_call(first, last, inputs, w_gu, w_down, at, steps, part_in, table, n_wide, chunk):
+def middle_call(first, last, inputs, w_gu, w_down, at, steps, part_in, n_wide, chunk):
     count, width = inputs[0].shape
     rows_each = width // n_wide
     tall = rows_each % 16 == 0
@@ -300,7 +319,7 @@
     else:
         part_specs = [pl.BlockSpec((width, 3 * chunk), lambda j, *_: (0, j))]
         part_shapes = [jax.ShapeDtypeStruct((width, columns), BF16)]
-    in_specs = [whole(v.shape) for v in inputs] + [
+    in_specs = [whole((count, LANES) if v.shape[1:] == (LANES,) else v.shape) for v in inputs] + [
         pl.BlockSpec((2, width, chunk), lambda j, *_: (0, 0, at + j)),
         pl.BlockSpec((chunk, width), lambda j, *_: (at + j, 0)),
     ]
@@ -321,28 +340,21 @@
     else:
         out_shape += [shape(rows, F32)] * 2
     outs = pl.pallas_call(
-        functools.partial(middle_kernel, first, last, rows_each),
-        grid_spec=pltpu.PrefetchScalarGridSpec(
-            num_scalar_prefetch=1,
-            grid=(steps,),
-            in_specs=in_specs,
-            out_specs=[whole(s.shape) for s in out_shape] + part_specs,
-            scratch_shapes=scratch,
-        ),
+        functools.partial(middle_kernel, first, last, rows_each, n_wide),
+        grid=(steps,),
+        in_specs=in_specs,
+        out_specs=[whole(s.shape) for s in out_shape] + part_specs,
+        scratch_shapes=scratch,
         out_shape=out_shape + part_shapes,
-        compiler_params=pltpu.CompilerParams(vmem_limit_bytes=24 * MIB),
+        compiler_params=pltpu.CompilerParams(vmem_limit_bytes=(20 if last else 14) * MIB),
         cost_estimate=cost(36 * count * width * chunk * steps, 32 * width * chunk * steps),
         name="middle",
-    )(table, *inputs)
+    )(*inputs)
     parts = outs[len(out_shape) :]
     if not tall and last is not None:
-        slots = in_slots(parts[0], table, n_wide)
+        slots = in_slots(parts[0], n_wide)
         parts = [slots[: n_wide // 2], slots[n_wide // 2 :]]
     return outs[: len(out_shape)], parts
-
-
-def in_slots(part, table, n_wide):
-    return jnp.take(part.reshape(n_wide, -1, part.shape[-1]), table, axis=0)
 
 
 def seeds_kernel(own_ref, other_ref, w_ref, grad_ref, seed_t_ref):
@@ -362,15 +374,14 @@
             jax.ShapeDtypeStruct((2 * count, out), BF16),
             jax.ShapeDtypeStruct((width, 2 * count), BF16),
         ],
-        cost_estimate=cost(4 * count * width * out, 8 * count * width),
-        compiler_params=pltpu.CompilerParams(vmem_limit_bytes=8 * MIB),
+        cost_estimate=cost(count * width, 8 * count),
+        compiler_params=pltpu.CompilerParams(vmem_limit_bytes=4 * MIB),
         name="seeds",
     )(own, other, w_out)
 
 
-def attention_back_kernel(block, rows_each, split, carried, *refs):
+def attention_back_kernel(block, rows_each, n_wide, split, carried, *refs):
     refs = list(refs)
-    table_ref = refs.pop(0)
     (qkv_ref, grad_ref, mixed_own_ref, mixed_other_ref, kept_ref, keys_ref) = refs[:6]
     (normed_t_ref, seed_t_ref) = refs[6:8]
     refs = refs[8 + carried :]
@@ -421,10 +432,10 @@
     pieces[:, 0:LANES] = query_total[...].T.astype(BF16)
     held[:, 0 : 3 * LANES] = mm(normed_t_ref[...], pieces[...])
     held[:, 3 * LANES : 4 * LANES] = mm(seed_t_ref[...], mixed[...])
-    write_slots(table_ref, held, part_refs, rows_each)
-
-
-def attention_back(pair, at, total, carried, qkv, grad, mixed_own, mixed_other, kept, keys, normed_t, seed_t, table, n_wide, block=512):
+    write_slots(0, n_wide, held, part_refs, rows_each)
+
+
+def attention_back(pair, at, total, carried, qkv, grad, mixed_own, mixed_other, kept, keys, normed_t, seed_t, n_wide, block=512):
     length = qkv.shape[1]
     half = length // 2
     width = normed_t.shape[0]
@@ -448,64 +459,91 @@
         whole((width, length)),
     ]
     inputs = [qkv, grad, mixed_own, mixed_other, kept, keys, normed_t, seed_t]
-    aliases = {1 + len(inputs) + i: 1 + i for i in range(len(carried))}
+    aliases = {len(inputs) + i: 1 + i for i in range(len(carried))}
     outs = pl.pallas_call(
-        functools.partial(attention_back_kernel, block, rows_each, len(part_specs), len(carried)),
-        grid_spec=pltpu.PrefetchScalarGridSpec(
-            num_scalar_prefetch=1,
-            grid=(1,),
-            in_specs=in_specs + [pl.BlockSpec(memory_space=pl.ANY)] * len(carried),
-            out_specs=[whole((length, 3 * LANES))] + part_specs,
-            scratch_shapes=[
-                pltpu.VMEM((4, length, LANES), BF16),
-                pltpu.VMEM((2, length, LANES), BF16),
-                pltpu.VMEM((LANES, length), F32),
-                pltpu.VMEM((length, LANES), BF16),
-                pltpu.VMEM((width, columns), F32),
-            ],
-        ),
+        functools.partial(attention_back_kernel, block, rows_each, n_wide, len(part_specs), len(carried)),
+        grid=(1,),
+        in_specs=in_specs + [pl.BlockSpec(memory_space=pl.ANY)] * len(carried),
+        out_specs=[whole((length, 3 * LANES))] + part_specs,
+        scratch_shapes=[
+            pltpu.VMEM((4, length, LANES), BF16),
+            pltpu.VMEM((2, length, LANES), BF16),
+            pltpu.VMEM((LANES, length), F32),
+            pltpu.VMEM((length, LANES), BF16),
+            pltpu.VMEM((width, columns), F32),
+        ],
         out_shape=[jax.ShapeDtypeStruct((length, 3 * LANES), BF16)] + part_shapes,
         input_output_aliases=aliases,
-        compiler_params=pltpu.CompilerParams(vmem_limit_bytes=24 * MIB),
+        compiler_params=pltpu.CompilerParams(vmem_limit_bytes=15 * MIB),
         cost_estimate=cost(50 * length * length * LANES, 16 * length * LANES),
         name="attention_back",
-    )(table, *inputs, *carried)
+    )(*inputs, *carried)
     return outs[0], list(outs[1:])
 
 
-def kept_and_sent(parts, table, n_wide):
+def kept_and_sent(parts, n_wide):
     if len(parts) == 2:
         return parts
-    slots = in_slots(parts[0], table, n_wide)
+    slots = in_slots(parts[0], n_wide)
     return slots[: n_wide // 2], slots[n_wide // 2 :]
 
 
-def added(arrays, low, high):
-    return sum(a[low:high].astype(F32) for a in arrays)
+def turn_kernel(counts, *refs):
+    *refs, out_ref = refs
+    groups = [[refs.pop(0) for _ in range(count)] for count in counts]
+
+    def step(slot, carry):
+        at = 0
+        for group in groups:
+            columns = slice(at, at + group[0].shape[2])
+            total = 0.0
+            for ref in group:
+                total = total + ref[slot].astype(F32)
+            for ref in refs:
+                total = total + ref[slot, :, columns].astype(F32)
+            out_ref[slot, :, columns] = total.astype(BF16)
+            at = columns.stop
+        return carry
+
+    lax.fori_loop(0, out_ref.shape[0], step, 0)
 
 
 class Scatter:
-    def __init__(self, keep, send, n_wide):
-        self.pieces, self.send, self.n_wide, self.slots, self.stage = [keep], send, n_wide, n_wide // 2, 0
+    def __init__(self, groups, n_wide):
+        self.groups, self.joint, self.n_wide, self.stage, self.slots = groups, [], n_wide, 1, n_wide // 2
+
+    def turn(self, *earlier):
+        self.slots //= 2
+        pieces = [a for group in self.groups for a in group] + self.joint
+        if earlier:
+            pieces[-1] = after(pieces[-1], *earlier)
+        rows = pieces[0].shape[1]
+        shape = (self.slots, rows, sum(group[0].shape[2] for group in self.groups))
+        self.send = pl.pallas_call(
+            functools.partial(turn_kernel, [len(group) for group in self.groups]),
+            grid=(1,),
+            in_specs=[pl.BlockSpec((self.slots,) + a.shape[1:], lambda *_: (1, 0, 0)) for a in pieces],
+            out_specs=whole(shape),
+            out_shape=jax.ShapeDtypeStruct(shape, BF16),
+            compiler_params=pltpu.CompilerParams(vmem_limit_bytes=8 * MIB),
+            cost_estimate=cost(math.prod(shape), 4 * math.prod(shape)),
+            name="turn",
+        )(*pieces)
+        return self.send
 
     def go(self):
-        self.pieces.append(stage_exchange(self.send, self.stage, self.n_wide))
+        self.joint.append(stage_exchange(self.send, self.stage, self.n_wide))
         self.stage += 1
 
-    def turn(self):
-        self.slots //= 2
-        self.send = added(self.pieces, self.slots, 2 * self.slots).astype(BF16)
-        return self.send
-
-    @property
-    def done(self):
-        return self.slots == 1 and self.stage > 0 and self.stage == self.n_wide.bit_length() - 1
-
-    def finish(self):
-        while not self.done:
-            self.turn()
-            self.go()
-        return [added(self.pieces[:-1], 0, 1), self.pieces[-1]]
+    def finish(self, other):
+        while other.slots > 1:
+            earlier = []
+            if self.slots > 1:
+                earlier = [self.turn()]
+                self.go()
+            other.turn(*earlier)
+            other.go()
+        return [(batch.groups, batch.joint) for batch in (self, other)]
 
 
 def input_other_kernel(pairs, *refs):
@@ -526,7 +564,7 @@
         in_specs=[pl.BlockSpec((half, columns), lambda *_: (1, 0))] * len(pieces) + [whole(w_qkv.shape)],
         out_specs=whole((half, width)),
         out_shape=jax.ShapeDtypeStruct((half, width), BF16),
-        compiler_params=pltpu.CompilerParams(vmem_limit_bytes=12 * MIB),
+        compiler_params=pltpu.CompilerParams(vmem_limit_bytes=5 * MIB),
         cost_estimate=cost(2 * half * width * columns * len(pieces), 4 << 20),
         name="input_other",
     )(*pieces, w_qkv)
@@ -541,7 +579,7 @@
         back = back + mm_nt(jnp.concatenate([ref[:, columns] for ref in piece_refs], axis=1), w_ref[i])
     rows = tokens_ref[...].astype(F32)
     factor = inverse_rms(rows)
-    scaled = back * gain_ref[...]
+    scaled = back * as_line(gain_ref)
     inner = jnp.mean(scaled * rows, axis=-1, keepdims=True)
     out_ref[...] = middle_grad_ref[...] + factor * scaled - rows * (factor * factor * factor * inner)
     part_ref[...] = jnp.sum(back * rows * factor, axis=0, keepdims=True)
@@ -557,7 +595,7 @@
         in_specs=[pl.BlockSpec((count, columns), lambda *_: (0, 0))] * len(pieces) + [whole(v.shape) for v in rest],
         out_specs=[whole((count, width)), whole((1, width))],
         out_shape=[jax.ShapeDtypeStruct((count, width), F32), jax.ShapeDtypeStruct((1, width), F32)],
-        compiler_params=pltpu.CompilerParams(vmem_limit_bytes=16 * MIB),
+        compiler_params=pltpu.CompilerParams(vmem_limit_bytes=10 * MIB),
         cost_estimate=cost(2 * count * width * columns * len(pieces), 8 << 20),
         name="input_grad",
     )(*pieces, *rest)
@@ -567,19 +605,27 @@
     return -(-rows // 8) * 8
 
 
-def gather_kernel(counts, wides, chunk, *refs):
+def gather_kernel(counts, chunk, *refs):
     refs = list(refs)
-    groups = [[refs.pop(0) for _ in range(count)] for count in counts]
+    sums = []
+    for group_counts, joint_count in counts:
+        groups = [[refs.pop(0) for _ in range(count)] for count in group_counts]
+        joint = [refs.pop(0) for _ in range(joint_count)]
+        parts, at = [], 0
+        for group in groups:
+            columns = slice(at, at + group[0].shape[2])
+            total = 0.0
+            for ref in group:
+                total = total + ref[0].astype(F32)
+            for ref in joint:
+                total = total + ref[0, :, columns].astype(F32)
+            parts.append(total)
+            at = columns.stop
+        sums.append(jnp.concatenate(parts, axis=1))
     attn_gain_ref, mlp_gain_ref, sums_ref = refs[:3]
     qkv_ref, out_ref, gu_ref, down_ref, columns_ref, pair_ref = refs[3:]
-    sums = []
-    for group in groups:
-        total = group[0][0].astype(F32)
-        for ref in group[1:]:
-            total = total + ref[0].astype(F32)
-        sums.append(total)
-    wide_part, pair_parts = jnp.concatenate(sums[:wides], axis=1), sums[wides:]
-    pairs = [part[:, i : i + 4 * LANES] for part in pair_parts for i in range(0, part.shape[1], 4 * LANES)]
+    wide_part, pair_part = sums
+    pairs = [pair_part[:, i : i + 4 * LANES] for i in range(0, pair_part.shape[1], 4 * LANES)]
     mats = [
         jnp.concatenate([pair[:, i * LANES : (i + 1) * LANES] for pair in pairs], axis=1) for i in range(4)
     ]
@@ -617,21 +663,22 @@
     pair_ref[at : at + 1, :] = sums_ref[...]
 
 
-def gather_own(groups, wides, attn_gain_part, mlp_gain_part, local_sums, heads_width, units, chunk):
-    rows = groups[0][0].shape[1]
+def gather_own(batches, attn_gain_part, mlp_gain_part, local_sums, heads_width, units, chunk):
+    rows = batches[0][0][0][0].shape[1]
     width = attn_gain_part.shape[1]
-    pieces = [a for group in groups for a in group]
+    pieces = [a for groups, joint in batches for group in [*groups, joint] for a in group]
+    counts = [([len(group) for group in groups], len(joint)) for groups, joint in batches]
     lines = [attn_gain_part, mlp_gain_part, local_sums]
     shapes = [(3, rows, heads_width), (rows, heads_width), (2, rows, units), (rows, units)]
     shapes += [(8, max(heads_width, units, width)), (padded(rows) + padded(2 * width // LANES + 1), LANES)]
     return pl.pallas_call(
-        functools.partial(gather_kernel, [len(g) for g in groups], wides, chunk),
+        functools.partial(gather_kernel, counts, chunk),
         grid=(1,),
         in_specs=[pl.BlockSpec((1,) + a.shape[1:], lambda *_: (0, 0, 0)) for a in pieces]
         + [whole(a.shape) for a in lines],
         out_specs=[whole(s) for s in shapes],
         out_shape=[jax.ShapeDtypeStruct(s, F32) for s in shapes],
-        compiler_params=pltpu.CompilerParams(vmem_limit_bytes=8 * MIB),
+        compiler_params=pltpu.CompilerParams(vmem_limit_bytes=5 * MIB),
         cost_estimate=cost(1 << 20, 4 << 20),
         name="gather_own",
     )(*pieces, *lines)
@@ -661,16 +708,24 @@
 
 
 def update_kernel(sizes, *refs):
-    (whole_ref, scalar_ref, qkv_ref, out_ref, gu_ref, down_ref, summed_ref, pair_ref, prior_rows_ref) = refs[:9]
+    (scalar_ref, qkv_ref, out_ref, gu_ref, down_ref, summed_ref, pair_ref) = refs[:7]
+    prior_refs, refs = refs[7:11], refs[2:]
     (qkv_cols, out_rows, gu_cols, down_rows, w_qkv, w_out, w_gu, w_down) = refs[9:17]
     (qkv_new, out_new, gu_new, down_new, qkv_cols_new, out_rows_new, gu_cols_new, down_rows_new) = refs[17:25]
-    (qkv_rows_new, out_cols_new, gu_rows_new, down_cols_new, attn_gain_ref, mlp_gain_ref, turned) = refs[25:]
+    (qkv_rows_new, out_cols_new, gu_rows_new, down_cols_new, attn_gain_ref, mlp_gain_ref, turned, prior_rows_ref) = refs[25:]
     rows = qkv_ref.shape[1]
     width = sizes[0]
     lane = lax.broadcasted_iota(jnp.int32, (1, LANES), 1)
-    beta = 1.0 - lax.rsqrt(jnp.full((1, 1), scalar_ref[0], F32))
+    scalars = as_line(scalar_ref)
+    beta = 1.0 - lax.rsqrt(scalars[:, 0:1])
     fresh = 1.0 - beta
-    start = lax.rem(width - whole_ref[0] * rows, width)
+    start = lax.rem(width - lax.axis_index("wide") * rows, width)
+    prior_rows_ref[...] = jnp.zeros_like(prior_rows_ref)
+    at = 0
+    for ref in prior_refs:
+        value = as_line(ref) if len(ref.shape) == 1 else ref[...]
+        prior_rows_ref[at : at + value.shape[0], :] = value
+        at += value.shape[0]
     own = pltpu.roll(prior_rows_ref[...], start, 1)[:, 0:LANES]
     turned[...] = jnp.zeros_like(turned)
     turned[0:8, :] = own
@@ -681,7 +736,7 @@
     sums = pair_ref[pl.ds(padded(rows) + 2 * width // LANES, 1), :]
     totals = summed_ref[7:8, 0:LANES]
     all_rows = jnp.zeros((rows, LANES), F32)
-    priors = [qkv_cols[0:1], qkv_cols[1:2], qkv_cols[2:3], out_rows[...], gu_cols[0:1], gu_cols[1:2], down_rows[...]]
+    priors = [qkv_cols[0:1], qkv_cols[1:2], qkv_cols[2:3], as_line(out_rows), gu_cols[0:1], gu_cols[1:2], as_line(down_rows)]
     for i in range(7):
         across = sizes[1 + i]
         entries = float(across * width)
@@ -695,7 +750,7 @@
         else:
             prior_mean = jnp.mean(prior_rows_ref[i : i + 1, :], axis=1, keepdims=True)
         mean = beta * prior_mean + fresh * (totals[:, i : i + 1] / entries + TINIEST)
-        rate = scalar_ref[1] * jnp.sqrt(sums[:, i : i + 1] / entries)
+        rate = scalars[:, 1:2] * jnp.sqrt(sums[:, i : i + 1] / entries)
         step = lax.rsqrt(row_new * col_new / mean)
         if i in (3, 6):
             gradient_ref, weight_ref, new_ref = ((out_ref, w_out, out_new), (down_ref, w_down, down_new))[i == 6]
@@ -714,36 +769,114 @@
     down_cols_new[...] = jnp.reshape(rows_new[6:7, 0:rows], (rows,))
 
 
-def update(place, scalars, grads, summed, pair, prior_rows, col_priors, weights, sizes):
+def update(step_count, learn_rate, grads, summed, pair, prior_rows, col_priors, weights, sizes):
     rows = grads[0].shape[1]
-    inputs = [*grads, summed, pair, prior_rows, *col_priors, *weights]
+    scalars = jnp.where(jnp.arange(LANES) == 0, step_count.astype(F32), learn_rate)
+    inputs = [scalars, *grads, summed, pair, *prior_rows, *col_priors, *weights]
     shapes = [(3, sizes[1] // 2), (sizes[4] // 2,), (2, sizes[5] // 2), (sizes[7] // 2,)]
     shapes += [(3, rows), (rows,), (2, rows), (rows,), (rows,), (rows,)]
     out_shape = [jax.ShapeDtypeStruct(w.shape, BF16) for w in weights]
     out_shape += [jax.ShapeDtypeStruct(s, F32) for s in shapes]
     return pl.pallas_call(
         functools.partial(update_kernel, sizes),
-        grid_spec=pltpu.PrefetchScalarGridSpec(
-            num_scalar_prefetch=2,
-            grid=(1,),
-            in_specs=[whole(a.shape) for a in inputs],
-            out_specs=[whole(s.shape) for s in out_shape],
-            scratch_shapes=[pltpu.VMEM((LANES, LANES), F32)],
-        ),
+        grid=(1,),
+        in_specs=[whole(a.shape) for a in inputs],
+        out_specs=[whole(s.shape) for s in out_shape],
+        scratch_shapes=[pltpu.VMEM((LANES, LANES), F32), pltpu.VMEM((8, sizes[0]), F32)],
         out_shape=out_shape,
         compiler_params=pltpu.CompilerParams(vmem_limit_bytes=8 * MIB),
         cost_estimate=cost(1 << 20, 4 << 20),
         name="update",
-    )(place, scalars, *inputs)
-
-
-def square_sum(values):
-    wide = values.astype(F32)
-    return jnp.sum(wide * wide, axis=(-2, -1))
+    )(*inputs)
+
+
+def weights_kernel(rows, qkv_ref, out_ref, gu_ref, down_ref, out_rows_ref, down_rows_ref, line_ref, *refs):
+    qkv_own, out_own, gu_own, down_own, sums, qkv_total, gu_total = refs
+    step = pl.program_id(0)
+    values = [qkv_ref.at[0], qkv_ref.at[1], qkv_ref.at[2], out_ref, gu_ref.at[0], gu_ref.at[1], down_ref]
+    width = out_ref.shape[1]
+    block = qkv_ref.shape[1]
+    start = lax.axis_index("wide") * rows
+
+    @pl.when(step == 0)
+    def _():
+        for ref in (sums, qkv_total, gu_total):
+            ref[...] = jnp.zeros_like(ref)
+
+    def chosen(first, count):
+        shape = (qkv_total.shape[1], count)
+        own = lax.broadcasted_iota(jnp.int32, shape, 0) + start
+        return jnp.where(lax.broadcasted_iota(jnp.int32, shape, 1) + first == own, 1.0, 0.0).astype(BF16)
+
+    for i, ref in enumerate(values):
+        count = ref.shape[1]
+        value = ref[...].astype(F32)
+        sums[i : i + 1, 0:count] += jnp.sum(value * value, axis=0, keepdims=True)
+    across = chosen(0, width)
+    for ref, own_ref in ((out_ref, out_own), (down_ref, down_own)):
+        own_ref[...] = mm_nt(across, ref[...])[0:rows].astype(BF16)
+    below = chosen(step * block, block)
+    for ref, total in ((qkv_ref, qkv_total), (gu_ref, gu_total)):
+        for i in range(ref.shape[0]):
+            total[i] += mm(below, ref[i])
+
+    @pl.when(step == pl.num_programs(0) - 1)
+    def _():
+        lane = lax.broadcasted_iota(jnp.int32, (1, LANES), 1)
+        line = jnp.zeros((1, LANES), F32)
+        for i in range(7):
+            line = jnp.where(lane == i, jnp.sum(sums[i : i + 1, :], axis=1, keepdims=True), line)
+        for i, ref in enumerate((out_rows_ref, down_rows_ref)):
+            line = jnp.where(lane == 7 + i, jnp.sum(as_line(ref), axis=1, keepdims=True), line)
+        line_ref[...] = line
+        qkv_own[...] = qkv_total[:, 0:rows, :].astype(BF16)
+        gu_own[...] = gu_total[:, 0:rows, :].astype(BF16)
+
+
+def weights_call(w_qkv, w_out, w_gu, w_down, out_rows, down_rows, n_wide):
+    width = w_out.shape[1]
+    rows, held = width // n_wide, -(-(width // n_wide) // 16) * 16
+    heads_width, units = w_qkv.shape[2], w_gu.shape[2]
+    steps = 3 if heads_width % (3 * LANES) == 0 and units % (3 * LANES) == 0 else 1
+    each = lambda n: n // steps
+    shapes = [(3, rows, heads_width), (rows, heads_width), (2, rows, units), (rows, units)]
+    line, *own = pl.pallas_call(
+        functools.partial(weights_kernel, rows),
+        grid=(steps,),
+        in_specs=[
+            pl.BlockSpec((3, each(width), heads_width), lambda j: (0, j, 0)),
+            pl.BlockSpec((each(heads_width), width), lambda j: (j, 0)),
+            pl.BlockSpec((2, each(width), units), lambda j: (0, j, 0)),
+            pl.BlockSpec((each(units), width), lambda j: (j, 0)),
+            whole(out_rows.shape),
+            whole(down_rows.shape),
+        ],
+        out_specs=[
+            whole((1, LANES)),
+            whole(shapes[0]),
+            pl.BlockSpec((rows, each(heads_width)), lambda j: (0, j)),
+            whole(shapes[2]),
+            pl.BlockSpec((rows, each(units)), lambda j: (0, j)),
+        ],
+        out_shape=[jax.ShapeDtypeStruct((1, LANES), F32)] + [jax.ShapeDtypeStruct(shape, BF16) for shape in shapes],
+        scratch_shapes=[
+            pltpu.VMEM((8, max(width, units)), F32),
+            pltpu.VMEM((3, held, heads_width), F32),
+            pltpu.VMEM((2, held, units), F32),
+        ],
+        compiler_params=pltpu.CompilerParams(vmem_limit_bytes=20 * MIB),
+        cost_estimate=cost(1 << 20, 7 << 20),
+        name="weights",
+    )(w_qkv, w_out, w_gu, w_down, out_rows, down_rows)
+    return line, own
 
 
 def after(values, *others):
     return lax.optimization_barrier((values, *others))[0]
+
+
+def far(values):
+    return pltpu.with_memory_space_constraint(values, pltpu.HBM)
 
 
 def body(
@@ -773,54 +906,44 @@
     heads_width, units = w_out.shape[0], w_down.shape[0]
     rows_each = width // n_wide
     chunk = 256
-    core = lax.axis_index("narrow")
-    wide = lax.axis_index("wide")
-    tables = [slot_table(wide, order, n_wide) for order in bit_orders(n_wide)]
-    own_table = jnp.where(core == 0, tables[0], tables[1])
-    other_table = jnp.where(core == 0, tables[1], tables[0])
-
     tokens_other = swap(tokens)
-    lines = key_lines(plot_slot, patch_mask, core)
-    normed_t, qkv = project(tokens, tokens_other, gain_attn, w_qkv)
-    sent = after((w_out, w_gu, w_down), tokens_other)
+    carried = project(0, far(tokens), far(gain_attn), far(w_qkv), [])
+    normed_t, qkv = project(1, tokens_other, gain_attn, w_qkv, carried)
+    sent = after((w_out, w_gu, w_down), tokens_other, *carried)
     w_out_other, w_gu_other, w_down_other = swap(sent[0]), swap(sent[1]), swap(sent[2])
-    mixed_own, mixed_other, kept, keys = attention(qkv, lines)
+    mixed_own, mixed_other, kept, keys = attention(qkv, plot_slot, patch_mask)
     mixed_recv = swap(mixed_other)
-    gain_line = gain_mlp[None]
     steps = units // chunk // 2
-    half = n_wide // 2
 
     (middle, *handed), (part_other,) = middle_call(
         True,
         None,
-        [tokens, mixed_own, mixed_recv, w_out, w_out_other, gain_line, cotangent, lines],
+        [tokens, mixed_own, mixed_recv, w_out, w_out_other, gain_mlp, cotangent, keys],
         w_gu_other,
         w_down_other,
         0,
         steps,
         None,
-        other_table,
         n_wide,
         chunk,
     )
     part_first = swap(part_other)
     totals, (part_other,) = middle_call(
-        False, None, handed, w_gu_other, w_down_other, steps, steps, None, other_table, n_wide, chunk
+        False, None, handed, w_gu_other, w_down_other, steps, steps, None, n_wide, chunk
     )
     part_second = swap(part_other)
     handed = [*handed[:4], *totals]
     totals, parts = middle_call(
-        False, False, handed, w_gu, w_down, 0, steps, part_first, own_table, n_wide, chunk
+        False, False, handed, w_gu, w_down, 0, steps, part_first, n_wide, chunk
     )
-    wide_a = Scatter(*parts, n_wide)
-    wide_a.go()
+    wide_a = [parts[0], stage_exchange(parts[1], 0, n_wide)]
     handed = [*handed[:4], *totals]
     (mixed_out, middle_grad, attn_seed, mlp_gain_part), parts = middle_call(
-        False, True, [*handed, middle, gain_line], w_gu, w_down, steps, steps, part_second, own_table, n_wide, chunk
+        False, True, [*handed, middle, gain_mlp], w_gu, w_down, steps, steps, part_second, n_wide, chunk
     )
-    wide_b = Scatter(*parts, n_wide)
-    wide_b.go()
+    wide_b = [parts[0], stage_exchange(parts[1], 0, n_wide)]
     mixed_grad, seed_t = seeds_call(attn_seed, swap(attn_seed), w_out)
+    mixed_grad = after(mixed_grad, wide_a[1])
 
     pairs = heads_width // LANES
     back = functools.partial(
@@ -832,58 +955,45 @@
         keys=keys,
         normed_t=normed_t,
         seed_t=seed_t,
-        table=own_table,
         n_wide=n_wide,
     )
     pieces = []
     piece, carried = back(0, 0, pairs - 1, [], grad=mixed_grad)
     pieces.append(piece)
-    mixed_grad = after(mixed_grad, wide_a.turn())
-    wide_a.go()
+    weights = after((w_qkv, w_out, w_gu, w_down, out_rows, down_rows), piece)
+    local_sums, own_weights = weights_call(*weights, n_wide)
+    wide_batch = Scatter([wide_a, wide_b], n_wide)
+    mixed_grad = after(mixed_grad, wide_batch.turn(piece, local_sums))
+    wide_batch.go()
     for pair in range(1, pairs - 1):
         piece, carried = back(pair, pair, pairs - 1, carried, grad=mixed_grad)
         pieces.append(piece)
-    first = Scatter(*kept_and_sent(carried, own_table, n_wide), n_wide)
-    first.go()
-    mixed_grad = after(mixed_grad, wide_a.turn(), wide_b.turn(), first.send)
-    wide_a.go()
-    wide_b.go()
+    keep, send = kept_and_sent(carried, n_wide)
+    first = [keep, stage_exchange(send, 0, n_wide)]
+    mixed_grad = after(mixed_grad, send)
     piece, carried = back(pairs - 1, 0, 1, [], grad=mixed_grad)
     pieces.append(piece)
-    last = Scatter(*kept_and_sent(carried, own_table, n_wide), n_wide)
-    last.go()
-    groups = [wide_a.finish(), wide_b.finish(), first.finish(), last.finish()]
+    keep, send = kept_and_sent(carried, n_wide)
+    last = [keep, stage_exchange(send, 0, n_wide)]
+    pair_batch = Scatter([first, last], n_wide)
+    batches = wide_batch.finish(pair_batch)
     back_other = swap(input_other(pieces, w_qkv))
-    tokens_grad, attn_gain_part = input_grad(pieces, w_qkv, back_other, tokens, gain_attn[None], middle_grad)
-
-    weights = after((w_qkv, w_out, w_gu, w_down, out_rows, down_rows, qkv_rows, out_cols, gu_rows, down_cols), piece)
-    local_sums = jnp.concatenate(
-        [square_sum(w.reshape(-1, *w.shape[-2:])) for w in weights[:4]]
-        + [jnp.sum(weights[4])[None], jnp.sum(weights[5])[None], jnp.zeros((LANES - 9,), F32)]
-    )[None]
-    prior_rows = jnp.concatenate(
-        [weights[6], weights[7][None], weights[8], weights[9][None], jnp.zeros((1, width), F32)], axis=0
-    )
-
-    def own_rows(values, dimension):
-        return lax.dynamic_slice_in_dim(values, wide * rows_each, rows_each, dimension)
-
-    own_weights = [own_rows(weights[0], 1), own_rows(weights[1], 1).T, own_rows(weights[2], 1), own_rows(weights[3], 1).T]
+    tokens_grad, attn_gain_part = input_grad(pieces, w_qkv, back_other, tokens, gain_attn, middle_grad)
 
     *grads, columns, pair = gather_own(
-        groups, 2, attn_gain_part, mlp_gain_part, local_sums, heads_width, units, chunk
+        batches, attn_gain_part, mlp_gain_part, local_sums, heads_width, units, chunk
     )
     summed, pair = combine(columns, pair, swap(pair), rows_each, width)
     for stage in range(n_wide.bit_length() - 1):
         summed = summed + stage_exchange(summed, stage, n_wide)
     outs = update(
-        (wide.astype(jnp.int32))[None],
-        jnp.stack([step_count.astype(F32), learn_rate]),
-        grads,
+        step_count,
+        learn_rate,
+        [far(grad) for grad in grads],
         summed,
         pair,
-        prior_rows,
-        [qkv_cols, out_rows[None], gu_cols, down_rows[None]],
+        [qkv_rows, out_cols, gu_rows, down_cols],
+        [qkv_cols, out_rows, gu_cols, down_rows],
         own_weights,
         [width] + [2 * heads_width] * 4 + [2 * units] * 3,
     )

time: 200 us -> 161 us (0.81)
  local copies, waits for them, and re-layouts: 25.4 us -> 0.09 us
  waiting for transfers between devices: 22.1 us -> 46.8 us
  other arithmetic: 21.4 us -> 0.04 us
  Pallas kernels: 88.8 us -> 78.9 us
  starting transfers between devices: 36.1 us -> 29.3 us
    ppermute x20 -> x14, waiting for transfers between devices: 18.3 us -> 43.4 us  [stage_exchange(): return lax.ppermute(values, ('wide', 'narrow'), pairs)]
    convert_element_type x12 -> x0, other arithmetic: 14.9 us -> none  [turn(): self.send = added(self.pieces, self.slots, 2 * self.slots).astype(BF16)]
    unnamed x118 -> x36, local copies, waits for them, and re-layouts: 14.1 us -> 0.09 us
    pallas_call x3, Pallas kernels: 30.6 us -> 23.3 us  [attention_back(): pl.pallas_call(functools.partial(attention_back_kernel, block, rows_each,...]
    reduce_sum x6 -> x0, other arithmetic: 4.98 us -> none  [the longest x4 3.78 us: square_sum(): return jnp.sum(wide * wide, axis=(-2, -1))]
    ppermute x20 -> x14, starting transfers between devices: 31.1 us -> 26.9 us  [stage_exchange(): return lax.ppermute(values, ('wide', 'narrow'), pairs)]
    optimization_barrier x2 -> x0, local copies, waits for them, and re-layouts: 3.76 us -> none  [after(): return lax.optimization_barrier((values, *others))[0]]
    concatenate x2 -> x0, local copies, waits for them, and re-layouts: 2.7 us -> none  [the longest x1 2.66 us: body(): jnp.concatenate([square_sum(w.reshape(-1, *w.shape[-2:])) for w in weight...]
  transfers between devices with their start and end apart: 30 -> 24, of which waited for: 10 -> 15; matrix products, arithmetic and copies ran while one was open for 17% -> 0% of each run, Pallas kernels for 35% -> 43%
where the time goes in v3:
time: 161 us; the launch traced here: 158 us
  Pallas kernels  78.9 us (49%)
  waiting for transfers between devices  46.8 us (29%)
  starting transfers between devices  29.3 us (18%)
  between operations  2.62 us (2%)
    ppermute x14, waiting for transfers between devices, stage_exchange(): return lax.ppermute(values, ('wide', 'narrow'), pairs)  43.4 us
    ppermute x14, starting transfers between devices, stage_exchange(): return lax.ppermute(values, ('wide', 'narrow'), pairs)  26.9 us
    pallas_call x4, Pallas kernels, middle_call(): pl.pallas_call(functools.partial(middle_kernel, first, last, rows_each, n...  25.7 us
    pallas_call x3, Pallas kernels, attention_back(): pl.pallas_call(functools.partial(attention_back_kernel, block, rows_each,...  23.3 us
    pallas_call x1, Pallas kernels, attention(): pl.pallas_call(functools.partial(attention_kernel, block=block), grid=(pa...  12.2 us
    pallas_call x2, Pallas kernels, project(): pl.pallas_call(functools.partial(project_kernel, len(carried)), grid=(1,)...  5.17 us
    ppermute x10, waiting for transfers between devices, swap(): return lax.ppermute(values, 'narrow', [(0, 1), (1, 0)])  3.48 us
  transfers between devices with their start and end apart: 24, of which 15 were waited for; matrix products, arithmetic and copies ran while one was open for 0% of the time, Pallas kernels for 43%

profile of v3, /device:TPU:0, one launch (start us, length us, event | category | flops | bytes accessed | tf_op | source)
XLA Modules:
  0.0 157.8 jit_solution(12964723357809810539)
XLA Ops:
  1.2 3.4 %project.2 = (bf16[768,1024]{1,0:T(8,128)(2,1)S(1)}, bf16[3,1024,384]{2,1,0:T(8,128)(2,1)S(1)}) custom-call(bf16[512,768]{1,0:T(8,128)(2,1)} %refs_5_.3, f32[768]{0:T(1024)} %refs_6_.5, bf16[3,768,384]{2,1,0:T(8,128)(2,1)} %refs_3_.5), custom_call_target="tpu_custom_call" | custom-call | flops 905969664 | bytes 1572864 | tf_op jit(solution)/shard_map/project/pallas_call | solution.py:124
  5.5 1.7 %project.3 = (bf16[768,1024]{1,0:T(8,128)(2,1)S(1)}, bf16[3,1024,384]{2,1,0:T(8,128)(2,1)S(1)}) custom-call(bf16[512,768]{1,0:T(8,128)(2,1)S(1)} %collective-permute-done.rows_ref, f32[768]{0:T(1024)S(1)} %copy-done.6, bf16[3,768,384]{2,1,0:T(8,128)(2,1)S(1)} %copy-done, ...), custom_call_target="tpu_custom_call", output_to_operand_aliasing={{0}: (3, {}), {1}: (4, {})} | custom-call | flops 905969664 | bytes 1572864 | tf_op jit(solution)/shard_map/project/pallas_call | solution.py:124
  7.3 12.2 %attention.1 = (bf16[512,384]{1,0:T(8,128)(2,1)S(1)}, bf16[512,384]{1,0:T(8,128)(2,1)S(1)}, bf16[6,1024,128]{2,1,0:T(8,128)(2,1)S(1)}, bf16[1024,128]{1,0:T(8,128)(2,1)S(1)}) custom-call(bf16[3,1024,384]{2,1,0:T(8,128)(2,1)S(1)} %get-tuple-element.106.qkv_ref.refs_0_, s32[1024]{0:T(1024)S(1)} %copy-done.15, s32[1024]{0:T(1024)S(1)} %copy-done.16), custom_call_target="tpu_custom_call" | custom-call | flops 6442450944 | bytes 3932160 | tf_op jit(solution)/shard_map/attention/pallas_call | solution.py:206
  21.3 6.8 %middle.4 = (f32[512,768]{1,0:T(8,128)S(1)}, bf16[512,768]{1,0:T(8,128)(2,1)S(1)}, bf16[768,512]{1,0:T(8,128)(2,1)S(1)}, bf16[512,768]{1,0:T(8,128)(2,1)S(1)}, b...) custom-call(bf16[512,768]{1,0:T(8,128)(2,1)S(1)} %copy-done.4, ...), custom_call_target="tpu_custom_call" | custom-call | flops 7247757312 | bytes 12582912 | tf_op jit(solution)/shard_map/middle/pallas_call | solution.py:342
  28.5 5.5 %middle.5 = (f32[512,768]{1,0:T(8,128)S(1)}, f32[512,768]{1,0:T(8,128)S(1)}, bf16[16,48,1536]{2,1,0:T(8,128)(2,1)S(1)}) custom-call(bf16[512,768]{1,0:T(8,128)(2,1)S(1)} %get-tuple-element.113.refs_0_, bf16[768,512]{1,0:T(8,128)(2,1)S(1)} %get-tuple-element.114.refs_1_, bf16[512,768]{1,0:T(8,128)(2,1)S(1)} %get-tuple-element.115.refs_2_, ...), custom_call_target="tpu_custom_call" | custom-call | flops 7247757312 | bytes 12582912 | tf_op jit(solution)/shard_map/middle/pallas_call | solution.py:342
  34.2 6.0 %middle.6 = (f32[512,768]{1,0:T(8,128)S(1)}, f32[512,768]{1,0:T(8,128)S(1)}, bf16[8,48,1536]{2,1,0:T(8,128)(2,1)S(1)}, bf16[8,48,1536]{2,1,0:T(8,128)(2,1)S(1)}) custom-call(bf16[512,768]{1,0:T(8,128)(2,1)S(1)} %get-tuple-element.113.refs_0_, bf16[768,512]{1,0:T(8,128)(2,1)S(1)} %get-tuple-element.114.refs_1_, ...), custom_call_target="tpu_custom_call" | custom-call | flops 7247757312 | bytes 12582912 | tf_op jit(solution)/shard_map/middle/pallas_call | solution.py:342
  40.2 2.9 %collective-permute-start.8 = (bf16[8,48,1536]{2,1,0:T(8,128)(2,1)S(1)}, bf16[8,48,1536]{2,1,0:T(8,128)(2,1)S(1)}, u32[]{:S(2)}, u32[]{:S(2)}) collective-permute-start(bf16[8,48,1536]{2,1,0:T(8,128)(2,1)S(1)} %get-tuple-element.129), channel_id=1, source_target_pairs={{0,2},{1,5},{2,0},{3,7},{4,6},{5,1},{6,4},{7,3},{8,10},{9,13},{10,... | collective-permute-start | bytes 3538952 | tf_op jit(solution)/shard_map/ppermute | solution.py:79
  43.1 7.5 %middle.7 = (bf16[512,768]{1,0:T(8,128)(2,1)}, f32[512,768]{1,0:T(8,128)S(1)}, bf16[512,768]{1,0:T(8,128)(2,1)S(1)}, f32[1,768]{1,0:T(1,128)S(1)}, bf16[8,48,153...) custom-call(bf16[512,768]{1,0:T(8,128)(2,1)S(1)} %get-tuple-element.113.refs_0_, ...), custom_call_target="tpu_custom_call" | custom-call | flops 7247757312 | bytes 12582912 | tf_op jit(solution)/shard_map/middle/pallas_call | solution.py:342
  53.9 3.4 %collective-permute-done.8.refs_1_ = bf16[8,48,1536]{2,1,0:T(8,128)(2,1)S(1)} collective-permute-done((bf16[8,48,1536]{2,1,0:T(8,128)(2,1)S(1)}, bf16[8,48,1536]{2,1,0:T(8,128)(2,1)S(1)}, u32[]{:S(2)}, u32[]{:S(2)}) %collective-permute-start.8) | collective-permute-done | bytes 1179680 | tf_op jit(solution)/shard_map/ppermute | solution.py:79
  57.2 7.9 %attention_back.3 = (bf16[1024,384]{1,0:T(8,128)(2,1)S(1)}, bf16[8,48,1024]{2,1,0:T(8,128)(2,1)S(1)}, bf16[8,48,1024]{2,1,0:T(8,128)(2,1)S(1)}) custom-call(bf16[3,1024,384]{2,1,0:T(8,128)(2,1)S(1)} %get-tuple-element.106.qkv_ref.refs_0_, bf16[1024,384]{1,0:T(8,128)(2,1)S(1)} %get-tuple-element.151.refs_1_, ...), custom_call_target="tpu_custom_call" | custom-call | flops 6710886400 | bytes 2097152 | tf_op jit(solution)/shard_map/attention_back/pallas_call | solution.py:463
  65.2 1.8 %weights.1 = (f32[1,128]{1,0:T(1,128)S(1)}, bf16[3,48,384]{2,1,0:T(8,128)(2,1)S(1)}, bf16[48,384]{1,0:T(8,128)(2,1)S(1)}, bf16[2,48,1024]{2,1,0:T(8,128)(2,1)S(1)}, bf16[48,1024]{1,0:T(8,128)(2,1)S(1)}) custom-call(bf16[3,768,384]{2,1,0:T(8,128)(2,1)S(1)} %copy-done, bf16[384,768]{1,0:T(8,128)(2,1)S(1)} %copy-done.2, bf16[2,768,1024]{2,1,0:T(8,128)(2,1)S(1)} %copy-done.1, ...), custom_call_target="tpu_custom_call" | custom-call | flops 1048576 | bytes 7340032 | tf_op jit(solution)/shard_map/weights/pallas_call | solution.py:843
  66.9 2.9 %collective-permute-done.9.refs_3_ = bf16[8,48,1536]{2,1,0:T(8,128)(2,1)S(1)} collective-permute-done((bf16[8,48,1536]{2,1,0:T(8,128)(2,1)S(1)}, bf16[8,48,1536]{2,1,0:T(8,128)(2,1)S(1)}, u32[]{:S(2)}, u32[]{:S(2)}) %collective-permute-start.9) | collective-permute-done | bytes 1179680 | tf_op jit(solution)/shard_map/ppermute | solution.py:79
  70.2 2.1 %collective-permute-start.11 = (bf16[4,48,3072]{2,1,0:T(8,128)(2,1)S(1)}, bf16[4,48,3072]{2,1,0:T(8,128)(2,1)S(1)}, u32[]{:S(2)}, u32[]{:S(2)}) collective-permute-start(bf16[4,48,3072]{2,1,0:T(8,128)(2,1)S(1)} %turn.6), channel_id=1, source_target_pairs={{0,4},{1,9},{2,6},{3,11},{4,0},{5,13},{6,2},{7,15},{8,12},{9,1},{1... | collective-permute-start | bytes 3538952 | tf_op jit(solution)/shard_map/ppermute | solution.py:79
  72.3 7.7 %attention_back.4 = (bf16[1024,384]{1,0:T(8,128)(2,1)S(1)}, bf16[8,48,1024]{2,1,0:T(8,128)(2,1)S(1)}, bf16[8,48,1024]{2,1,0:T(8,128)(2,1)S(1)}) custom-call(bf16[3,1024,384]{2,1,0:T(8,128)(2,1)S(1)} %get-tuple-element.106.qkv_ref.refs_0_, bf16[1024,384]{1,0:T(8,128)(2,1)S(1)} %get-tuple-element.151.refs_1_, ...), custom_call_target="tpu_custom_call", output_to_operand_aliasing={{1}: (8, {}), {2}: (9, {})} | custom-call | flops 6710886400 | bytes 2097152 | tf_op jit(solution)/shard_map/attention_back/pallas_call | solution.py:463
  81.5 7.7 %attention_back.5 = (bf16[1024,384]{1,0:T(8,128)(2,1)S(1)}, bf16[8,48,512]{2,1,0:T(8,128)(2,1)S(1)}, bf16[8,48,512]{2,1,0:T(8,128)(2,1)S(1)}) custom-call(bf16[3,1024,384]{2,1,0:T(8,128)(2,1)S(1)} %get-tuple-element.106.qkv_ref.refs_0_, bf16[1024,384]{1,0:T(8,128)(2,1)S(1)} %get-tuple-element.151.refs_1_, ...), custom_call_target="tpu_custom_call" | custom-call | flops 6710886400 | bytes 2097152 | tf_op jit(solution)/shard_map/attention_back/pallas_call | solution.py:463
  91.4 3.9 %collective-permute-start.12 = (bf16[2,48,3072]{2,1,0:T(8,128)(2,1)S(1)}, bf16[2,48,3072]{2,1,0:T(8,128)(2,1)S(1)}, u32[]{:S(2)}, u32[]{:S(2)}) collective-permute-start(bf16[2,48,3072]{2,1,0:T(8,128)(2,1)S(1)} %turn.7), channel_id=1, source_target_pairs={{0,8},{1,3},{2,10},{3,1},{4,12},{5,7},{6,14},{7,5},{8,0},{9,11},{1... | collective-permute-start | bytes 1769480 | tf_op jit(solution)/shard_map/ppermute | solution.py:79
  95.3 6.0 %collective-permute-done.15.refs_3_.refs_10_ = bf16[8,48,512]{2,1,0:T(8,128)(2,1)S(1)} collective-permute-done((bf16[8,48,512]{2,1,0:T(8,128)(2,1)S(1)}, bf16[8,48,512]{2,1,0:T(8,128)(2,1)S(1)}, u32[]{:S(2)}, u32[]{:S(2)}) %collective-permute-start.15) | collective-permute-done | bytes 393248 | tf_op jit(solution)/shard_map/ppermute | solution.py:79
  104.0 7.7 %collective-permute-done.16.refs_4_.refs_11_ = bf16[4,48,1536]{2,1,0:T(8,128)(2,1)S(1)} collective-permute-done((bf16[4,48,1536]{2,1,0:T(8,128)(2,1)S(1)}, bf16[4,48,1536]{2,1,0:T(8,128)(2,1)S(1)}, u32[]{:S(2)}, u32[]{:S(2)}) %collective-permute-start.16) | collective-permute-done | bytes 589856 | tf_op jit(solution)/shard_map/ppermute | solution.py:79
  111.8 2.8 %collective-permute-start.17 = (bf16[2,48,1536]{2,1,0:T(8,128)(2,1)S(1)}, bf16[2,48,1536]{2,1,0:T(8,128)(2,1)S(1)}, u32[]{:S(2)}, u32[]{:S(2)}) collective-permute-start(bf16[2,48,1536]{2,1,0:T(8,128)(2,1)S(1)} %turn.10), channel_id=1, source_target_pairs={{0,8},{1,3},{2,10},{3,1},{4,12},{5,7},{6,14},{7,5},{8,0},{9,11},{1... | collective-permute-start | bytes 884744 | tf_op jit(solution)/shard_map/ppermute | solution.py:79
  114.6 2.4 %collective-permute-start.13 = (bf16[1,48,3072]{2,1,0:T(8,128)(2,1)S(1)}, bf16[1,48,3072]{2,1,0:T(8,128)(2,1)S(1)}, u32[]{:S(2)}, u32[]{:S(2)}) collective-permute-start(bf16[1,48,3072]{2,1,0:T(8,128)(2,1)S(1)} %turn.8), channel_id=1, source_target_pairs={{0,16},{1,17},{2,18},{3,19},{4,20},{5,21},{6,22},{7,23},{8,24},{9,... | collective-permute-start | bytes 884744 | tf_op jit(solution)/shard_map/ppermute | solution.py:79
  117.1 4.4 %collective-permute-done.17.refs_5_.refs_12_ = bf16[2,48,1536]{2,1,0:T(8,128)(2,1)S(1)} collective-permute-done((bf16[2,48,1536]{2,1,0:T(8,128)(2,1)S(1)}, bf16[2,48,1536]{2,1,0:T(8,128)(2,1)S(1)}, u32[]{:S(2)}, u32[]{:S(2)}) %collective-permute-start.17) | collective-permute-done | bytes 294944 | tf_op jit(solution)/shard_map/ppermute | solution.py:79
  121.6 3.0 %collective-permute-start.18 = (bf16[1,48,1536]{2,1,0:T(8,128)(2,1)S(1)}, bf16[1,48,1536]{2,1,0:T(8,128)(2,1)S(1)}, u32[]{:S(2)}, u32[]{:S(2)}) collective-permute-start(bf16[1,48,1536]{2,1,0:T(8,128)(2,1)S(1)} %turn.11), channel_id=1, source_target_pairs={{0,16},{1,17},{2,18},{3,19},{4,20},{5,21},{6,22},{7,23},{8,24},{9,... | collective-permute-start | bytes 442376 | tf_op jit(solution)/shard_map/ppermute | solution.py:79
  124.6 3.1 %input_grad.1 = (f32[512,768]{1,0:T(8,128)}, f32[1,768]{1,0:T(1,128)S(1)}) custom-call(bf16[1024,384]{1,0:T(8,128)(2,1)S(1)} %get-tuple-element.134.refs_0_, bf16[1024,384]{1,0:T(8,128)(2,1)S(1)} %get-tuple-element.149.refs_1_, bf16[1024,384]{1,0:T(8,128)(2,1)S(1)} %get-tuple-element.152.refs_2_, bf16[3,768,384]{2,1,0:T(8,128)(2,1)S(1)} %copy-done, ...), custom_call_target="tpu_custom_call" | custom-call | flops 905969664 | bytes 8388608 | tf_op jit(solution)/shard_map/input_grad/pallas_call | solution.py:592
  127.7 4.1 %collective-permute-done.13.refs_6_ = bf16[1,48,3072]{2,1,0:T(8,128)(2,1)S(1)} collective-permute-done((bf16[1,48,3072]{2,1,0:T(8,128)(2,1)S(1)}, bf16[1,48,3072]{2,1,0:T(8,128)(2,1)S(1)}, u32[]{:S(2)}, u32[]{:S(2)}) %collective-permute-start.13) | collective-permute-done | bytes 294944 | tf_op jit(solution)/shard_map/ppermute | solution.py:79
  131.7 1.6 %collective-permute-done.18.refs_13_ = bf16[1,48,1536]{2,1,0:T(8,128)(2,1)S(1)} collective-permute-done((bf16[1,48,1536]{2,1,0:T(8,128)(2,1)S(1)}, bf16[1,48,1536]{2,1,0:T(8,128)(2,1)S(1)}, u32[]{:S(2)}, u32[]{:S(2)}) %collective-permute-start.18) | collective-permute-done | bytes 147488 | tf_op jit(solution)/shard_map/ppermute | solution.py:79
  136.7 3.5 %collective-permute-done.20 = f32[16,1024]{1,0:T(8,128)S(1)} collective-permute-done((f32[16,1024]{1,0:T(8,128)S(1)}, f32[16,1024]{1,0:T(8,128)S(1)}, u32[]{:S(2)}, u32[]{:S(2)}) %collective-permute-start.20) | collective-permute-done | bytes 65568 | tf_op jit(solution)/shard_map/ppermute | solution.py:79
  140.2 1.6 %collective-permute-start.21 = (f32[16,1024]{1,0:T(8,128)S(1)}, f32[16,1024]{1,0:T(8,128)S(1)}, u32[]{:S(2)}, u32[]{:S(2)}) collective-permute-start(f32[16,1024]{1,0:T(8,128)S(1)} %add.12), channel_id=1, source_target_pairs={{0,4},{1,9},{2,6},{3,11},{4,0},{5,13},{6,2},{7,15},{8,12},{9,1},{1... | collective-permute-start | bytes 196616 | tf_op jit(solution)/shard_map/ppermute | solution.py:79
  141.8 2.7 %collective-permute-done.21 = f32[16,1024]{1,0:T(8,128)S(1)} collective-permute-done((f32[16,1024]{1,0:T(8,128)S(1)}, f32[16,1024]{1,0:T(8,128)S(1)}, u32[]{:S(2)}, u32[]{:S(2)}) %collective-permute-start.21) | collective-permute-done | bytes 65568 | tf_op jit(solution)/shard_map/ppermute | solution.py:79
  146.6 2.3 %collective-permute-done.22 = f32[16,1024]{1,0:T(8,128)S(1)} collective-permute-done((f32[16,1024]{1,0:T(8,128)S(1)}, f32[16,1024]{1,0:T(8,128)S(1)}, u32[]{:S(2)}, u32[]{:S(2)}) %collective-permute-start.22) | collective-permute-done | bytes 65568 | tf_op jit(solution)/shard_map/ppermute | solution.py:79
  148.9 2.5 %collective-permute-start.23 = (f32[16,1024]{1,0:T(8,128)S(1)}, f32[16,1024]{1,0:T(8,128)S(1)}, u32[]{:S(2)}, u32[]{:S(2)}) collective-permute-start(f32[16,1024]{1,0:T(8,128)S(1)} %add.14), channel_id=1, source_target_pairs={{0,16},{1,17},{2,18},{3,19},{4,20},{5,21},{6,22},{7,23},{8,24},{9,... | collective-permute-start | bytes 196616 | tf_op jit(solution)/shard_map/ppermute | solution.py:79
  151.4 3.5 %collective-permute-done.23 = f32[16,1024]{1,0:T(8,128)S(1)} collective-permute-done((f32[16,1024]{1,0:T(8,128)S(1)}, f32[16,1024]{1,0:T(8,128)S(1)}, u32[]{:S(2)}, u32[]{:S(2)}) %collective-permute-start.23) | collective-permute-done | bytes 65568 | tf_op jit(solution)/shard_map/ppermute | solution.py:79
  154.9 2.6 %update.1 = (bf16[3,48,384]{2,1,0:T(8,128)(2,1)}, bf16[48,384]{1,0:T(8,128)(2,1)}, bf16[2,48,1024]{2,1,0:T(8,128)(2,1)}, bf16[48,1024]{1,0:T(8,128)(2,1)}, f32[3...) custom-call(f32[128]{0:T(128)S(1)} %compare_select_fusion.refs_0_, ...), custom_call_target="tpu_custom_call" | custom-call | flops 1048576 | bytes 4194304 | tf_op jit(solution)/shard_map/update/pallas_call | solution.py:780
  (80 shorter events, 18.1 us)
Async XLA Ops:
  0.7 4.0 %collective-permute-start = (bf16[512,768]{1,0:T(8,128)(2,1)}, bf16[512,768]{1,0:T(8,128)(2,1)S(1)}, u32[]{:S(2)}, u32[]{:S(2)}) collective-permute-start(bf16[512,768]{1,0:T(8,128)(2,1)} %refs_5_.3), channel_id=1, source_target_pairs={{0,1},{1,0},{2,3},{3,2},{4,5},{5,4},{6,7},{7,6},{8,9},{9,8},{10,11... | collective-permute-start | bytes 2359304 | tf_op jit(solution)/shard_map/ppermute | solution.py:83
  4.7 16.5 %collective-permute-start.3 = (bf16[2,768,1024]{2,1,0:T(8,128)(2,1)}, bf16[2,768,1024]{2,1,0:T(8,128)(2,1)S(1)}, u32[]{:S(2)}, u32[]{:S(2)}) collective-permute-start(bf16[2,768,1024]{2,1,0:T(8,128)(2,1)} %gu_ref), channel_id=1, source_target_pairs={{0,1},{1,0},{2,3},{3,2},{4,5},{5,4},{6,7},{7,6},{8,9},{9,8},{10,11... | collective-permute-start | bytes 9437192 | tf_op jit(solution)/shard_map/ppermute | solution.py:83
  5.0 16.3 %collective-permute-start.4 = (bf16[1024,768]{1,0:T(8,128)(2,1)}, bf16[1024,768]{1,0:T(8,128)(2,1)S(1)}, u32[]{:S(2)}, u32[]{:S(2)}) collective-permute-start(bf16[1024,768]{1,0:T(8,128)(2,1)} %down_ref), channel_id=1, source_target_pairs={{0,1},{1,0},{2,3},{3,2},{4,5},{5,4},{6,7},{7,6},{8,9},{9,8},{10,11... | collective-permute-start | bytes 4718600 | tf_op jit(solution)/shard_map/ppermute | solution.py:83
  5.3 16.0 %collective-permute-start.2 = (bf16[384,768]{1,0:T(8,128)(2,1)S(1)}, bf16[384,768]{1,0:T(8,128)(2,1)S(1)}, u32[]{:S(2)}, u32[]{:S(2)}) collective-permute-start(bf16[384,768]{1,0:T(8,128)(2,1)S(1)} %copy-done.2), channel_id=1, source_target_pairs={{0,1},{1,0},{2,3},{3,2},{4,5},{5,4},{6,7},{7,6},{8,9},{9,8},{10,11... | collective-permute-start | bytes 1769480 | tf_op jit(solution)/shard_map/ppermute | solution.py:83
  7.2 14.0 %copy-start.4 = (bf16[512,768]{1,0:T(8,128)(2,1)S(1)}, bf16[512,768]{1,0:T(8,128)(2,1)}, u32[]{:S(2)}) copy-start(bf16[512,768]{1,0:T(8,128)(2,1)} %refs_5_.3) | copy-start | bytes 2359300
  7.3 14.0 %copy-start.14 = (bf16[512,768]{1,0:T(8,128)(2,1)S(1)}, bf16[512,768]{1,0:T(8,128)(2,1)}, u32[]{:S(2)}) copy-start(bf16[512,768]{1,0:T(8,128)(2,1)} %refs_6_.3) | copy-start | bytes 2359300
  19.5 1.8 %collective-permute-start.1 = (bf16[512,384]{1,0:T(8,128)(2,1)S(1)}, bf16[512,384]{1,0:T(8,128)(2,1)S(1)}, u32[]{:S(2)}, u32[]{:S(2)}) collective-permute-start(bf16[512,384]{1,0:T(8,128)(2,1)S(1)} %get-tuple-element.108.refs_3_), channel_id=1, source_target_pairs={{0,1},{1,0},{2,3},{3,2},{4,5},{5,4},{6,7},{7,6},{8,9},{9,8},{10,11... | collective-permute-start | bytes 1179656 | tf_op jit(solution)/shard_map/ppermute | solution.py:83
  28.1 6.1 %collective-permute-start.5 = (bf16[16,48,1536]{2,1,0:T(8,128)(2,1)S(1)}, bf16[16,48,1536]{2,1,0:T(8,128)(2,1)S(1)}, u32[]{:S(2)}, u32[]{:S(2)}) collective-permute-start(bf16[16,48,1536]{2,1,0:T(8,128)(2,1)S(1)} %get-tuple-element.121), channel_id=1, source_target_pairs={{0,1},{1,0},{2,3},{3,2},{4,5},{5,4},{6,7},{7,6},{8,9},{9,8},{10,11... | collective-permute-start | bytes 7077896 | tf_op jit(solution)/shard_map/ppermute | solution.py:83
  33.9 9.1 %collective-permute-start.6 = (bf16[16,48,1536]{2,1,0:T(8,128)(2,1)S(1)}, bf16[16,48,1536]{2,1,0:T(8,128)(2,1)S(1)}, u32[]{:S(2)}, u32[]{:S(2)}) collective-permute-start(bf16[16,48,1536]{2,1,0:T(8,128)(2,1)S(1)} %get-tuple-element.125), channel_id=1, source_target_pairs={{0,1},{1,0},{2,3},{3,2},{4,5},{5,4},{6,7},{7,6},{8,9},{9,8},{10,11... | collective-permute-start | bytes 7077896 | tf_op jit(solution)/shard_map/ppermute | solution.py:83
  40.2 17.0 %collective-permute-start.8 = (bf16[8,48,1536]{2,1,0:T(8,128)(2,1)S(1)}, bf16[8,48,1536]{2,1,0:T(8,128)(2,1)S(1)}, u32[]{:S(2)}, u32[]{:S(2)}) collective-permute-start(bf16[8,48,1536]{2,1,0:T(8,128)(2,1)S(1)} %get-tuple-element.129), channel_id=1, source_target_pairs={{0,2},{1,5},{2,0},{3,7},{4,6},{5,1},{6,4},{7,3},{8,10},{9,13},{10,... | collective-permute-start | bytes 3538952 | tf_op jit(solution)/shard_map/ppermute | solution.py:79
  50.6 2.3 %collective-permute-start.7 = (bf16[512,768]{1,0:T(8,128)(2,1)S(1)}, bf16[512,768]{1,0:T(8,128)(2,1)S(1)}, u32[]{:S(2)}, u32[]{:S(2)}) collective-permute-start(bf16[512,768]{1,0:T(8,128)(2,1)S(1)} %get-tuple-element.127.own_ref), channel_id=1, source_target_pairs={{0,1},{1,0},{2,3},{3,2},{4,5},{5,4},{6,7},{7,6},{8,9},{9,8},{10,11... | collective-permute-start | bytes 2359304 | tf_op jit(solution)/shard_map/ppermute | solution.py:83
  50.6 19.3 %collective-permute-start.9 = (bf16[8,48,1536]{2,1,0:T(8,128)(2,1)S(1)}, bf16[8,48,1536]{2,1,0:T(8,128)(2,1)S(1)}, u32[]{:S(2)}, u32[]{:S(2)}) collective-permute-start(bf16[8,48,1536]{2,1,0:T(8,128)(2,1)S(1)} %get-tuple-element.137), channel_id=1, source_target_pairs={{0,2},{1,5},{2,0},{3,7},{4,6},{5,1},{6,4},{7,3},{8,10},{9,13},{10,... | collective-permute-start | bytes 3538952 | tf_op jit(solution)/shard_map/ppermute | solution.py:79
  70.2 21.0 %collective-permute-start.11 = (bf16[4,48,3072]{2,1,0:T(8,128)(2,1)S(1)}, bf16[4,48,3072]{2,1,0:T(8,128)(2,1)S(1)}, u32[]{:S(2)}, u32[]{:S(2)}) collective-permute-start(bf16[4,48,3072]{2,1,0:T(8,128)(2,1)S(1)} %turn.6), channel_id=1, source_target_pairs={{0,4},{1,9},{2,6},{3,11},{4,0},{5,13},{6,2},{7,15},{8,12},{9,1},{1... | collective-permute-start | bytes 3538952 | tf_op jit(solution)/shard_map/ppermute | solution.py:79
  80.0 21.3 %collective-permute-start.14 = (bf16[8,48,1024]{2,1,0:T(8,128)(2,1)S(1)}, bf16[8,48,1024]{2,1,0:T(8,128)(2,1)S(1)}, u32[]{:S(2)}, u32[]{:S(2)}) collective-permute-start(bf16[8,48,1024]{2,1,0:T(8,128)(2,1)S(1)} %get-tuple-element.150), channel_id=1, source_target_pairs={{0,2},{1,5},{2,0},{3,7},{4,6},{5,1},{6,4},{7,3},{8,10},{9,13},{10,... | collective-permute-start | bytes 2359304 | tf_op jit(solution)/shard_map/ppermute | solution.py:79
  89.2 12.1 %collective-permute-start.15 = (bf16[8,48,512]{2,1,0:T(8,128)(2,1)S(1)}, bf16[8,48,512]{2,1,0:T(8,128)(2,1)S(1)}, u32[]{:S(2)}, u32[]{:S(2)}) collective-permute-start(bf16[8,48,512]{2,1,0:T(8,128)(2,1)S(1)} %get-tuple-element.157), channel_id=1, source_target_pairs={{0,2},{1,5},{2,0},{3,7},{4,6},{5,1},{6,4},{7,3},{8,10},{9,13},{10,... | collective-permute-start | bytes 1179656 | tf_op jit(solution)/shard_map/ppermute | solution.py:79
  91.4 12.4 %collective-permute-start.12 = (bf16[2,48,3072]{2,1,0:T(8,128)(2,1)S(1)}, bf16[2,48,3072]{2,1,0:T(8,128)(2,1)S(1)}, u32[]{:S(2)}, u32[]{:S(2)}) collective-permute-start(bf16[2,48,3072]{2,1,0:T(8,128)(2,1)S(1)} %turn.7), channel_id=1, source_target_pairs={{0,8},{1,3},{2,10},{3,1},{4,12},{5,7},{6,14},{7,5},{8,0},{9,11},{1... | collective-permute-start | bytes 1769480 | tf_op jit(solution)/shard_map/ppermute | solution.py:79
  101.7 9.9 %collective-permute-start.16 = (bf16[4,48,1536]{2,1,0:T(8,128)(2,1)S(1)}, bf16[4,48,1536]{2,1,0:T(8,128)(2,1)S(1)}, u32[]{:S(2)}, u32[]{:S(2)}) collective-permute-start(bf16[4,48,1536]{2,1,0:T(8,128)(2,1)S(1)} %turn.9), channel_id=1, source_target_pairs={{0,4},{1,9},{2,6},{3,11},{4,0},{5,13},{6,2},{7,15},{8,12},{9,1},{1... | collective-permute-start | bytes 1769480 | tf_op jit(solution)/shard_map/ppermute | solution.py:79
  103.7 20.9 %collective-permute-start.10 = (bf16[512,768]{1,0:T(8,128)(2,1)S(1)}, bf16[512,768]{1,0:T(8,128)(2,1)S(1)}, u32[]{:S(2)}, u32[]{:S(2)}) collective-permute-start(bf16[512,768]{1,0:T(8,128)(2,1)S(1)} %input_other.1), channel_id=1, source_target_pairs={{0,1},{1,0},{2,3},{3,2},{4,5},{5,4},{6,7},{7,6},{8,9},{9,8},{10,11... | collective-permute-start | bytes 2359304 | tf_op jit(solution)/shard_map/ppermute | solution.py:83
  111.8 9.7 %collective-permute-start.17 = (bf16[2,48,1536]{2,1,0:T(8,128)(2,1)S(1)}, bf16[2,48,1536]{2,1,0:T(8,128)(2,1)S(1)}, u32[]{:S(2)}, u32[]{:S(2)}) collective-permute-start(bf16[2,48,1536]{2,1,0:T(8,128)(2,1)S(1)} %turn.10), channel_id=1, source_target_pairs={{0,8},{1,3},{2,10},{3,1},{4,12},{5,7},{6,14},{7,5},{8,0},{9,11},{1... | collective-permute-start | bytes 884744 | tf_op jit(solution)/shard_map/ppermute | solution.py:79
  114.6 17.1 %collective-permute-start.13 = (bf16[1,48,3072]{2,1,0:T(8,128)(2,1)S(1)}, bf16[1,48,3072]{2,1,0:T(8,128)(2,1)S(1)}, u32[]{:S(2)}, u32[]{:S(2)}) collective-permute-start(bf16[1,48,3072]{2,1,0:T(8,128)(2,1)S(1)} %turn.8), channel_id=1, source_target_pairs={{0,16},{1,17},{2,18},{3,19},{4,20},{5,21},{6,22},{7,23},{8,24},{9,... | collective-permute-start | bytes 884744 | tf_op jit(solution)/shard_map/ppermute | solution.py:79
  121.6 11.7 %collective-permute-start.18 = (bf16[1,48,1536]{2,1,0:T(8,128)(2,1)S(1)}, bf16[1,48,1536]{2,1,0:T(8,128)(2,1)S(1)}, u32[]{:S(2)}, u32[]{:S(2)}) collective-permute-start(bf16[1,48,1536]{2,1,0:T(8,128)(2,1)S(1)} %turn.11), channel_id=1, source_target_pairs={{0,16},{1,17},{2,18},{3,19},{4,20},{5,21},{6,22},{7,23},{8,24},{9,... | collective-permute-start | bytes 442376 | tf_op jit(solution)/shard_map/ppermute | solution.py:79
  133.3 21.5 %copy-start.7 = (f32[3,768]{1,0:T(4,128)S(1)}, f32[3,768]{1,0:T(4,128)}, u32[]{:S(2)}) copy-start(f32[3,768]{1,0:T(4,128)} %refs_7_.5) | copy-start | bytes 27652
  133.3 21.6 %copy-start.8 = (f32[2,1024]{1,0:T(2,128)S(1)}, f32[2,1024]{1,0:T(2,128)}, u32[]{:S(2)}) copy-start(f32[2,1024]{1,0:T(2,128)} %refs_13_.1) | copy-start | bytes 24580
  133.3 21.6 %copy-start.10 = (f32[2,768]{1,0:T(2,128)S(1)}, f32[2,768]{1,0:T(2,128)}, u32[]{:S(2)}) copy-start(f32[2,768]{1,0:T(2,128)} %refs_9_.3) | copy-start | bytes 18436
  133.3 21.6 %copy-start.11 = (f32[3,384]{1,0:T(4,128)S(1)}, f32[3,384]{1,0:T(4,128)}, u32[]{:S(2)}) copy-start(f32[3,384]{1,0:T(4,128)} %refs_11_.1) | copy-start | bytes 13828
  133.3 21.6 %copy-start.12 = (f32[768]{0:T(1024)S(1)}, f32[768]{0:T(1024)}, u32[]{:S(2)}) copy-start(f32[768]{0:T(1024)} %refs_8_.3) | copy-start | bytes 9220
  133.3 21.6 %copy-start.13 = (f32[768]{0:T(1024)S(1)}, f32[768]{0:T(1024)}, u32[]{:S(2)}) copy-start(f32[768]{0:T(1024)} %refs_10_.1) | copy-start | bytes 9220
  134.6 1.2 collective-permute-start.19
  135.9 4.3 %collective-permute-start.20 = (f32[16,1024]{1,0:T(8,128)S(1)}, f32[16,1024]{1,0:T(8,128)S(1)}, u32[]{:S(2)}, u32[]{:S(2)}) collective-permute-start(f32[16,1024]{1,0:T(8,128)S(1)} %get-tuple-element.168), channel_id=1, source_target_pairs={{0,2},{1,5},{2,0},{3,7},{4,6},{5,1},{6,4},{7,3},{8,10},{9,13},{10,... | collective-permute-start | bytes 196616 | tf_op jit(solution)/shard_map/ppermute | solution.py:79
  140.2 4.3 %collective-permute-start.21 = (f32[16,1024]{1,0:T(8,128)S(1)}, f32[16,1024]{1,0:T(8,128)S(1)}, u32[]{:S(2)}, u32[]{:S(2)}) collective-permute-start(f32[16,1024]{1,0:T(8,128)S(1)} %add.12), channel_id=1, source_target_pairs={{0,4},{1,9},{2,6},{3,11},{4,0},{5,13},{6,2},{7,15},{8,12},{9,1},{1... | collective-permute-start | bytes 196616 | tf_op jit(solution)/shard_map/ppermute | solution.py:79
  144.6 4.3 %collective-permute-start.22 = (f32[16,1024]{1,0:T(8,128)S(1)}, f32[16,1024]{1,0:T(8,128)S(1)}, u32[]{:S(2)}, u32[]{:S(2)}) collective-permute-start(f32[16,1024]{1,0:T(8,128)S(1)} %add.13), channel_id=1, source_target_pairs={{0,8},{1,3},{2,10},{3,1},{4,12},{5,7},{6,14},{7,5},{8,0},{9,11},{1... | collective-permute-start | bytes 196616 | tf_op jit(solution)/shard_map/ppermute | solution.py:79
  148.9 5.9 %collective-permute-start.23 = (f32[16,1024]{1,0:T(8,128)S(1)}, f32[16,1024]{1,0:T(8,128)S(1)}, u32[]{:S(2)}, u32[]{:S(2)}) collective-permute-start(f32[16,1024]{1,0:T(8,128)S(1)} %add.14), channel_id=1, source_target_pairs={{0,16},{1,17},{2,18},{3,19},{4,20},{5,21},{6,22},{7,23},{8,24},{9,... | collective-permute-start | bytes 196616 | tf_op jit(solution)/shard_map/ppermute | solution.py:79
  (10 other events, 60.6 us)

commit v4 on v3

--- a/solution.py
+++ b/solution.py
@@ -48,30 +48,36 @@
     return high, middle, (rest - middle.astype(F32)).astype(BF16)
 
 
-def bit_orders(n_wide):
+WIDE, PAIRS = 0, 1
+
+
+def bit_orders(n_wide, kind):
     bits = n_wide.bit_length() - 1
     straight = list(range(bits))
-    turned = straight[1:-1] + straight[:1] + straight[-1:] if bits > 2 else straight
-    return straight, turned
-
-
-def slot_masks(n_wide):
+    if bits <= 2:
+        return straight, straight
+    if kind == WIDE:
+        return straight, [1, 0] + straight[2:]
+    return straight, straight[1:-1] + straight[:1] + straight[-1:]
+
+
+def slot_masks(n_wide, kind):
     bits = n_wide.bit_length() - 1
     return [
         [sum(1 << bit for stage, bit in enumerate(order) if slot >> (bits - 1 - stage) & 1) for slot in range(n_wide)]
-        for order in bit_orders(n_wide)
+        for order in bit_orders(n_wide, kind)
     ]
 
 
-def slot_row(slot, n_wide, turned):
-    masks = slot_masks(n_wide)
+def slot_row(slot, n_wide, kind, turned=0):
+    masks = slot_masks(n_wide, kind)
     wide, core = lax.axis_index("wide"), lax.axis_index("narrow")
     first, second = masks[turned][slot], masks[1 - turned][slot]
     return jnp.bitwise_xor(wide, first + (second - first) * core)
 
 
-def stage_exchange(values, stage, n_wide):
-    orders = bit_orders(n_wide)
+def stage_exchange(values, stage, n_wide, kind):
+    orders = bit_orders(n_wide, kind)
     pairs = []
     for wide in range(n_wide):
         for core in range(2):
@@ -83,24 +89,20 @@
     return lax.ppermute(values, "narrow", [(0, 1), (1, 0)])
 
 
-def write_slots(turned, n_wide, held_ref, targets, rows_each, more_ref=None):
+def write_slots(kind, turned, n_wide, held_ref, targets, rows_each):
     if targets[0].ndim == 2:
-        more = 0.0 if more_ref is None else more_ref[...].astype(F32)
-        targets[0][...] = (held_ref[...] + more).astype(BF16)
+        targets[0][...] = held_ref[...].astype(BF16)
         return
     slot = 0
     for target in targets:
         for at in range(target.shape[0]):
-            start = pl.multiple_of(slot_row(slot, n_wide, turned) * rows_each, 16)
-            value = held_ref[pl.ds(start, rows_each), :]
-            if more_ref is not None:
-                value = value + more_ref[slot].astype(F32)
-            target[at] = value.astype(BF16)
+            start = pl.multiple_of(slot_row(slot, n_wide, kind, turned) * rows_each, 16)
+            target[at] = held_ref[pl.ds(start, rows_each), :].astype(BF16)
             slot += 1
 
 
-def in_slots(part, n_wide):
-    rows = jnp.stack([slot_row(slot, n_wide, 0) for slot in range(n_wide)])
+def in_slots(part, n_wide, kind):
+    rows = jnp.stack([slot_row(slot, n_wide, kind) for slot in range(n_wide)])
     return jnp.take(part.reshape(n_wide, -1, part.shape[-1]), rows, axis=0)
 
 
@@ -240,7 +242,6 @@
         if last:
             (middle_ref, gain_ref) = take(2)
     (gu_ref, down_ref) = take(2)
-    part_in = None if last is None else take(1)[0]
     if first:
         (middle_ref, normed, normed_t, seed, seed_t) = take(5)
     if last:
@@ -288,7 +289,7 @@
     held[:, 0:chunk] = mm(normed_t[...], gate_grad)
     held[:, chunk : 2 * chunk] = mm(normed_t[...], up_grad)
     held[:, 2 * chunk : 3 * chunk] = mm(seed_t[...], hidden)
-    write_slots(int(last is None), n_wide, held, part_refs, rows_each, part_in)
+    write_slots(WIDE, int(last is None), n_wide, held, part_refs, rows_each)
 
     if last:
 
@@ -306,16 +307,15 @@
             gain_part_ref[...] = jnp.sum(back * middle * factor, axis=0, keepdims=True)
 
 
-def middle_call(first, last, inputs, w_gu, w_down, at, steps, part_in, n_wide, chunk):
+def middle_call(first, last, inputs, w_gu, w_down, at, steps, n_wide, chunk):
     count, width = inputs[0].shape
     rows_each = width // n_wide
     tall = rows_each % 16 == 0
     rows, turned = (count, width), (width, count)
     columns = 3 * chunk * steps
     if tall:
-        slots = [n_wide] if last is None else [n_wide // 2] * 2
-        part_specs = [pl.BlockSpec((n, rows_each, 3 * chunk), lambda j, *_: (0, 0, j)) for n in slots]
-        part_shapes = [jax.ShapeDtypeStruct((n, rows_each, columns), BF16) for n in slots]
+        part_specs = [pl.BlockSpec((n_wide, rows_each, 3 * chunk), lambda j, *_: (0, 0, j))]
+        part_shapes = [jax.ShapeDtypeStruct((n_wide, rows_each, columns), BF16)]
     else:
         part_specs = [pl.BlockSpec((width, 3 * chunk), lambda j, *_: (0, j))]
         part_shapes = [jax.ShapeDtypeStruct((width, columns), BF16)]
@@ -324,11 +324,6 @@
         pl.BlockSpec((chunk, width), lambda j, *_: (at + j, 0)),
     ]
     inputs = [*inputs, w_gu, w_down]
-    if last is not None:
-        inputs.append(part_in)
-        in_specs.append(
-            pl.BlockSpec((n_wide, rows_each, 3 * chunk), lambda j, *_: (0, 0, j)) if tall else part_specs[0]
-        )
     shape = jax.ShapeDtypeStruct
     scratch = [pltpu.VMEM((width, 3 * chunk), F32)]
     out_shape = []
@@ -347,14 +342,14 @@
         scratch_shapes=scratch,
         out_shape=out_shape + part_shapes,
         compiler_params=pltpu.CompilerParams(vmem_limit_bytes=(20 if last else 14) * MIB),
-        cost_estimate=cost(36 * count * width * chunk * steps, 32 * width * chunk * steps),
+        cost_estimate=cost((1 if last else 36) * count * width * chunk * steps, width * chunk * steps),
         name="middle",
     )(*inputs)
-    parts = outs[len(out_shape) :]
-    if not tall and last is not None:
-        slots = in_slots(parts[0], n_wide)
-        parts = [slots[: n_wide // 2], slots[n_wide // 2 :]]
-    return outs[: len(out_shape)], parts
+    return outs[: len(out_shape)], outs[-1]
+
+
+def slotted(part, n_wide):
+    return part if part.ndim == 3 else in_slots(part, n_wide, WIDE)
 
 
 def seeds_kernel(own_ref, other_ref, w_ref, grad_ref, seed_t_ref):
@@ -374,7 +369,7 @@
             jax.ShapeDtypeStruct((2 * count, out), BF16),
             jax.ShapeDtypeStruct((width, 2 * count), BF16),
         ],
-        cost_estimate=cost(count * width, 8 * count),
+        cost_estimate=cost(16 * count * width * width, 8 * count),
         compiler_params=pltpu.CompilerParams(vmem_limit_bytes=4 * MIB),
         name="seeds",
     )(own, other, w_out)
@@ -432,7 +427,7 @@
     pieces[:, 0:LANES] = query_total[...].T.astype(BF16)
     held[:, 0 : 3 * LANES] = mm(normed_t_ref[...], pieces[...])
     held[:, 3 * LANES : 4 * LANES] = mm(seed_t_ref[...], mixed[...])
-    write_slots(0, n_wide, held, part_refs, rows_each)
+    write_slots(PAIRS, 0, n_wide, held, part_refs, rows_each)
 
 
 def attention_back(pair, at, total, carried, qkv, grad, mixed_own, mixed_other, kept, keys, normed_t, seed_t, n_wide, block=512):
@@ -484,7 +479,7 @@
 def kept_and_sent(parts, n_wide):
     if len(parts) == 2:
         return parts
-    slots = in_slots(parts[0], n_wide)
+    slots = in_slots(parts[0], n_wide, PAIRS)
     return slots[: n_wide // 2], slots[n_wide // 2 :]
 
 
@@ -509,8 +504,8 @@
 
 
 class Scatter:
-    def __init__(self, groups, n_wide):
-        self.groups, self.joint, self.n_wide, self.stage, self.slots = groups, [], n_wide, 1, n_wide // 2
+    def __init__(self, kind, groups, n_wide, stage):
+        self.kind, self.groups, self.joint, self.n_wide, self.stage, self.slots = kind, groups, [], n_wide, stage, n_wide >> stage
 
     def turn(self, *earlier):
         self.slots //= 2
@@ -532,7 +527,7 @@
         return self.send
 
     def go(self):
-        self.joint.append(stage_exchange(self.send, self.stage, self.n_wide))
+        self.joint.append(stage_exchange(self.send, self.stage, self.n_wide, self.kind))
         self.stage += 1
 
     def finish(self, other):
@@ -684,23 +679,32 @@
     )(*pieces, *lines)
 
 
-def combine_kernel(rows, width, columns_ref, own_ref, recv_ref, summed_ref, pair_ref):
+def sum_place(i, narrow, count):
+    if i < 4:
+        return slice(3 + i // 2, 4 + i // 2), slice(i % 2 * narrow, (i % 2 + 1) * narrow)
+    return slice(i - 4, i - 3), slice(0, count)
+
+
+def combine_kernel(rows, width, narrow, columns_ref, own_ref, recv_ref, summed_ref, pair_ref):
     pair = own_ref[...] + recv_ref[...]
     pair_ref[...] = pair
     summed_ref[...] = jnp.zeros_like(summed_ref)
-    summed_ref[0:8, :] = columns_ref[...]
-    summed_ref[7:8, 0:LANES] = jnp.sum(pair[0:rows, :], axis=0, keepdims=True)
+    summed_ref[0:3, :] = columns_ref[4:7, :]
+    for i in range(4):
+        place = sum_place(i, narrow, 0)
+        summed_ref[place] = columns_ref[i : i + 1, 0:narrow]
+    summed_ref[3:4, 2 * narrow : 2 * narrow + LANES] = jnp.sum(pair[0:rows, :], axis=0, keepdims=True)
     at = padded(rows)
-    for line in (8, 9):
+    for line in (5, 6):
         for i in range(0, width, LANES):
             summed_ref[line : line + 1, i : i + LANES] = pair[at : at + 1, :]
             at += 1
 
 
-def combine(columns, own, recv, rows, width):
-    shapes = [(16, columns.shape[1]), own.shape]
+def combine(columns, own, recv, rows, width, narrow):
+    shapes = [columns.shape, own.shape]
     return pl.pallas_call(
-        functools.partial(combine_kernel, rows, width),
+        functools.partial(combine_kernel, rows, width, narrow),
         out_shape=[jax.ShapeDtypeStruct(s, F32) for s in shapes],
         compiler_params=pltpu.CompilerParams(vmem_limit_bytes=4 * MIB),
         name="combine",
@@ -730,11 +734,12 @@
     turned[...] = jnp.zeros_like(turned)
     turned[0:8, :] = own
     prior_columns = turned[...].T
-    gains = pltpu.roll(summed_ref[8:16, 0:width], start, 1)
-    attn_gain_ref[...] = jnp.reshape(gains[0:1, 0:rows], (rows,))
-    mlp_gain_ref[...] = jnp.reshape(gains[1:2, 0:rows], (rows,))
+    gains = pltpu.roll(summed_ref[:, 0:width], start, 1)
+    attn_gain_ref[...] = jnp.reshape(gains[5:6, 0:rows], (rows,))
+    mlp_gain_ref[...] = jnp.reshape(gains[6:7, 0:rows], (rows,))
     sums = pair_ref[pl.ds(padded(rows) + 2 * width // LANES, 1), :]
-    totals = summed_ref[7:8, 0:LANES]
+    narrow = out_ref.shape[1]
+    totals = summed_ref[3:4, 2 * narrow : 2 * narrow + LANES]
     all_rows = jnp.zeros((rows, LANES), F32)
     priors = [qkv_cols[0:1], qkv_cols[1:2], qkv_cols[2:3], as_line(out_rows), gu_cols[0:1], gu_cols[1:2], as_line(down_rows)]
     for i in range(7):
@@ -742,7 +747,7 @@
         entries = float(across * width)
         row_new = beta * prior_columns[0:rows, i : i + 1] + fresh * (pair_ref[0:rows, i : i + 1] / across + TINIEST)
         count = priors[i].shape[1]
-        col_new = beta * priors[i] + fresh * (summed_ref[i : i + 1, 0:count] / width + TINIEST)
+        col_new = beta * priors[i] + fresh * (summed_ref[sum_place(i, narrow, count)] / width + TINIEST)
         all_rows = jnp.where(lane == i, row_new, all_rows)
         if i in (3, 6):
             at = 7 + (i == 6)
@@ -915,35 +920,28 @@
     mixed_recv = swap(mixed_other)
     steps = units // chunk // 2
 
-    (middle, *handed), (part_other,) = middle_call(
-        True,
-        None,
-        [tokens, mixed_own, mixed_recv, w_out, w_out_other, gain_mlp, cotangent, keys],
-        w_gu_other,
-        w_down_other,
-        0,
-        steps,
-        None,
-        n_wide,
-        chunk,
-    )
-    part_first = swap(part_other)
-    totals, (part_other,) = middle_call(
-        False, None, handed, w_gu_other, w_down_other, steps, steps, None, n_wide, chunk
-    )
-    part_second = swap(part_other)
-    handed = [*handed[:4], *totals]
-    totals, parts = middle_call(
-        False, False, handed, w_gu, w_down, 0, steps, part_first, n_wide, chunk
-    )
-    wide_a = [parts[0], stage_exchange(parts[1], 0, n_wide)]
-    handed = [*handed[:4], *totals]
-    (mixed_out, middle_grad, attn_seed, mlp_gain_part), parts = middle_call(
-        False, True, [*handed, middle, gain_mlp], w_gu, w_down, steps, steps, part_second, n_wide, chunk
-    )
-    wide_b = [parts[0], stage_exchange(parts[1], 0, n_wide)]
-    mixed_grad, seed_t = seeds_call(attn_seed, swap(attn_seed), w_out)
-    mixed_grad = after(mixed_grad, wide_a[1])
+    inputs = [tokens, mixed_own, mixed_recv, w_out, w_out_other, gain_mlp, cotangent, keys]
+    wide_parts = []
+    for i in range(2):
+        at = i * steps
+        outs, part_other = middle_call(i == 0, None, inputs, w_gu_other, w_down_other, at, steps, n_wide, chunk)
+        if i == 0:
+            middle, *inputs = outs
+        else:
+            inputs = [*inputs[:4], *outs, middle, gain_mlp]
+        outs, part = middle_call(False, i == 1, inputs, w_gu, w_down, at, steps, n_wide, chunk)
+        one = Scatter(WIDE, [[slotted(part, n_wide), slotted(swap(part_other), n_wide)]], n_wide, 0)
+        wide_parts.append(one)
+        if i == 1:
+            mixed_out, middle_grad, attn_seed, mlp_gain_part = outs
+            attn_seed = after(attn_seed, wide_parts[0].turn())
+            wide_parts[0].go()
+            mixed_grad, seed_t = seeds_call(attn_seed, swap(attn_seed), w_out)
+            mixed_grad = after(mixed_grad, one.turn(mixed_grad))
+        else:
+            one.turn()
+        one.go()
+        inputs = [after(inputs[0], one.send), *inputs[1:4], *outs[:2]]
 
     pairs = heads_width // LANES
     back = functools.partial(
@@ -962,20 +960,20 @@
     pieces.append(piece)
     weights = after((w_qkv, w_out, w_gu, w_down, out_rows, down_rows), piece)
     local_sums, own_weights = weights_call(*weights, n_wide)
-    wide_batch = Scatter([wide_a, wide_b], n_wide)
-    mixed_grad = after(mixed_grad, wide_batch.turn(piece, local_sums))
-    wide_batch.go()
+    mixed_grad = after(mixed_grad, local_sums)
     for pair in range(1, pairs - 1):
         piece, carried = back(pair, pair, pairs - 1, carried, grad=mixed_grad)
         pieces.append(piece)
     keep, send = kept_and_sent(carried, n_wide)
-    first = [keep, stage_exchange(send, 0, n_wide)]
-    mixed_grad = after(mixed_grad, send)
+    first = [keep, stage_exchange(send, 0, n_wide, PAIRS)]
+    mixed_grad = after(mixed_grad, send, wide_parts[1].turn(piece))
+    wide_parts[1].go()
     piece, carried = back(pairs - 1, 0, 1, [], grad=mixed_grad)
     pieces.append(piece)
     keep, send = kept_and_sent(carried, n_wide)
-    last = [keep, stage_exchange(send, 0, n_wide)]
-    pair_batch = Scatter([first, last], n_wide)
+    last = [keep, stage_exchange(send, 0, n_wide, PAIRS)]
+    pair_batch = Scatter(PAIRS, [first, last], n_wide, 1)
+    wide_batch = Scatter(WIDE, [one.groups[0] + one.joint for one in wide_parts], n_wide, 2)
     batches = wide_batch.finish(pair_batch)
     back_other = swap(input_other(pieces, w_qkv))
     tokens_grad, attn_gain_part = input_grad(pieces, w_qkv, back_other, tokens, gain_attn, middle_grad)
@@ -983,9 +981,9 @@
     *grads, columns, pair = gather_own(
         batches, attn_gain_part, mlp_gain_part, local_sums, heads_width, units, chunk
     )
-    summed, pair = combine(columns, pair, swap(pair), rows_each, width)
+    summed, pair = combine(columns, pair, swap(pair), rows_each, width, heads_width)
     for stage in range(n_wide.bit_length() - 1):
-        summed = summed + stage_exchange(summed, stage, n_wide)
+        summed = summed + stage_exchange(summed, stage, n_wide, PAIRS)
     outs = update(
         step_count,
         learn_rate,

time: 161 us -> 158 us (0.981)
  waiting for transfers between devices: 46.8 us -> 44 us
    ppermute x10, starting transfers between devices: 2.41 us -> 4.93 us  [swap(): return lax.ppermute(values, 'narrow', [(0, 1), (1, 0)])]
    ppermute x14 -> x15, starting transfers between devices: 26.9 us -> 24.5 us  [stage_exchange(): return lax.ppermute(values, ('wide', 'narrow'), pairs)]
    ppermute x14 -> x15, waiting for transfers between devices: 43.4 us -> 41.6 us  [stage_exchange(): return lax.ppermute(values, ('wide', 'narrow'), pairs)]
  transfers between devices with their start and end apart: 24 -> 25, of which waited for: 15 -> 14; matrix products, arithmetic and copies ran while one was open for 0% -> 0% of each run, Pallas kernels for 43% -> 44%
where the time goes in v4:
time: 158 us; the launch traced here: 155 us
  Pallas kernels  79.2 us (50%)
  waiting for transfers between devices  44 us (28%)
  starting transfers between devices  29.4 us (19%)
  between operations  2.67 us (2%)
    ppermute x15, waiting for transfers between devices, stage_exchange(): return lax.ppermute(values, ('wide', 'narrow'), pairs)  41.6 us
    pallas_call x4, Pallas kernels, middle_call(): pl.pallas_call(functools.partial(middle_kernel, first, last, rows_each, n...  25.1 us
    ppermute x15, starting transfers between devices, stage_exchange(): return lax.ppermute(values, ('wide', 'narrow'), pairs)  24.5 us
    pallas_call x3, Pallas kernels, attention_back(): pl.pallas_call(functools.partial(attention_back_kernel, block, rows_each,...  23.4 us
    pallas_call x1, Pallas kernels, attention(): pl.pallas_call(functools.partial(attention_kernel, block=block), grid=(pa...  12.1 us
    pallas_call x2, Pallas kernels, project(): pl.pallas_call(functools.partial(project_kernel, len(carried)), grid=(1,)...  5.26 us
    ppermute x10, starting transfers between devices, swap(): return lax.ppermute(values, 'narrow', [(0, 1), (1, 0)])  4.93 us
  transfers between devices with their start and end apart: 25, of which 14 were waited for; matrix products, arithmetic and copies ran while one was open for 0% of the time, Pallas kernels for 44%

profile of v4, /device:TPU:0, one launch (start us, length us, event | category | flops | bytes accessed | tf_op | source)
XLA Modules:
  0.0 155.5 jit_solution(2300437173938588754)
XLA Ops:
  1.2 3.5 %project.2 = (bf16[768,1024]{1,0:T(8,128)(2,1)S(1)}, bf16[3,1024,384]{2,1,0:T(8,128)(2,1)S(1)}) custom-call(bf16[512,768]{1,0:T(8,128)(2,1)} %refs_5_.3, f32[768]{0:T(1024)} %refs_6_.5, bf16[3,768,384]{2,1,0:T(8,128)(2,1)} %refs_3_.5), custom_call_target="tpu_custom_call" | custom-call | flops 905969664 | bytes 1572864 | tf_op jit(solution)/shard_map/project/pallas_call | solution.py:126
  5.5 1.7 %project.3 = (bf16[768,1024]{1,0:T(8,128)(2,1)S(1)}, bf16[3,1024,384]{2,1,0:T(8,128)(2,1)S(1)}) custom-call(bf16[512,768]{1,0:T(8,128)(2,1)S(1)} %collective-permute-done.rows_ref, f32[768]{0:T(1024)S(1)} %copy-done.6, bf16[3,768,384]{2,1,0:T(8,128)(2,1)S(1)} %copy-done, ...), custom_call_target="tpu_custom_call", output_to_operand_aliasing={{0}: (3, {}), {1}: (4, {})} | custom-call | flops 905969664 | bytes 1572864 | tf_op jit(solution)/shard_map/project/pallas_call | solution.py:126
  7.3 12.1 %attention.1 = (bf16[512,384]{1,0:T(8,128)(2,1)S(1)}, bf16[512,384]{1,0:T(8,128)(2,1)S(1)}, bf16[6,1024,128]{2,1,0:T(8,128)(2,1)S(1)}, bf16[1024,128]{1,0:T(8,128)(2,1)S(1)}) custom-call(bf16[3,1024,384]{2,1,0:T(8,128)(2,1)S(1)} %get-tuple-element.107.qkv_ref.refs_0_, s32[1024]{0:T(1024)S(1)} %copy-done.16, s32[1024]{0:T(1024)S(1)} %copy-done.17), custom_call_target="tpu_custom_call" | custom-call | flops 6442450944 | bytes 3932160 | tf_op jit(solution)/shard_map/attention/pallas_call | solution.py:208
  21.3 6.7 %middle.4 = (f32[512,768]{1,0:T(8,128)S(1)}, bf16[512,768]{1,0:T(8,128)(2,1)S(1)}, bf16[768,512]{1,0:T(8,128)(2,1)S(1)}, bf16[512,768]{1,0:T(8,128)(2,1)S(1)}, b...) custom-call(bf16[512,768]{1,0:T(8,128)(2,1)S(1)} %copy-done.3, ...), custom_call_target="tpu_custom_call" | custom-call | flops 7247757312 | bytes 393216 | tf_op jit(solution)/shard_map/middle/pallas_call | solution.py:337
  28.5 5.5 %middle.5 = (f32[512,768]{1,0:T(8,128)S(1)}, f32[512,768]{1,0:T(8,128)S(1)}, bf16[16,48,1536]{2,1,0:T(8,128)(2,1)S(1)}) custom-call(bf16[512,768]{1,0:T(8,128)(2,1)S(1)} %get-tuple-element.122.refs_0_, bf16[768,512]{1,0:T(8,128)(2,1)S(1)} %get-tuple-element.115.refs_1_, bf16[512,768]{1,0:T(8,128)(2,1)S(1)} %get-tuple-element.116.refs_2_, ...), custom_call_target="tpu_custom_call" | custom-call | flops 7247757312 | bytes 393216 | tf_op jit(solution)/shard_map/middle/pallas_call | solution.py:337
  34.4 2.6 %collective-permute-start.6 = (bf16[8,48,1536]{2,1,0:T(8,128)(2,1)S(1)}, bf16[8,48,1536]{2,1,0:T(8,128)(2,1)S(1)}, u32[]{:S(2)}, u32[]{:S(2)}) collective-permute-start(bf16[8,48,1536]{2,1,0:T(8,128)(2,1)S(1)} %turn.9), channel_id=1, source_target_pairs={{0,2},{1,5},{2,0},{3,7},{4,6},{5,1},{6,4},{7,3},{8,10},{9,13},{10,... | collective-permute-start | bytes 3538952 | tf_op jit(solution)/shard_map/ppermute | solution.py:85
  37.0 5.7 %middle.6 = (f32[512,768]{1,0:T(8,128)S(1)}, f32[512,768]{1,0:T(8,128)S(1)}, bf16[16,48,1536]{2,1,0:T(8,128)(2,1)S(1)}) custom-call(bf16[512,768]{1,0:T(8,128)(2,1)S(1)} %get-tuple-element.122.refs_0_, bf16[768,512]{1,0:T(8,128)(2,1)S(1)} %get-tuple-element.115.refs_1_, bf16[512,768]{1,0:T(8,128)(2,1)S(1)} %get-tuple-element.116.refs_2_, ...), custom_call_target="tpu_custom_call" | custom-call | flops 7247757312 | bytes 393216 | tf_op jit(solution)/shard_map/middle/pallas_call | solution.py:337
  42.8 7.1 %middle.7 = (bf16[512,768]{1,0:T(8,128)(2,1)}, f32[512,768]{1,0:T(8,128)S(1)}, bf16[512,768]{1,0:T(8,128)(2,1)S(1)}, f32[1,768]{1,0:T(1,128)S(1)}, bf16[16,48,1536]{2,1,0:T(8,128)(2,1)S(1)}) custom-call(bf16[512,768]{1,0:T(8,128)(2,1)S(1)} %get-tuple-element.122.refs_0_, bf16[768,512]{1,0:T(8,128)(2,1)S(1)} %get-tuple-element.115.refs_1_, ...), custom_call_target="tpu_custom_call" | custom-call | flops 201326592 | bytes 393216 | tf_op jit(solution)/shard_map/middle/pallas_call | solution.py:337
  51.5 2.1 %collective-permute-start.11 = (bf16[4,48,1536]{2,1,0:T(8,128)(2,1)S(1)}, bf16[4,48,1536]{2,1,0:T(8,128)(2,1)S(1)}, u32[]{:S(2)}, u32[]{:S(2)}) collective-permute-start(bf16[4,48,1536]{2,1,0:T(8,128)(2,1)S(1)} %turn.10), channel_id=1, source_target_pairs={{0,4},{1,3},{2,6},{3,1},{4,0},{5,7},{6,2},{7,5},{8,12},{9,11},{10,... | collective-permute-start | bytes 1769480 | tf_op jit(solution)/shard_map/ppermute | solution.py:85
  55.1 2.1 %collective-permute-start.9 = (bf16[8,48,1536]{2,1,0:T(8,128)(2,1)S(1)}, bf16[8,48,1536]{2,1,0:T(8,128)(2,1)S(1)}, u32[]{:S(2)}, u32[]{:S(2)}) collective-permute-start(bf16[8,48,1536]{2,1,0:T(8,128)(2,1)S(1)} %turn.11), channel_id=1, source_target_pairs={{0,2},{1,5},{2,0},{3,7},{4,6},{5,1},{6,4},{7,3},{8,10},{9,13},{10,... | collective-permute-start | bytes 3538952 | tf_op jit(solution)/shard_map/ppermute | solution.py:85
  57.2 7.9 %attention_back.3 = (bf16[1024,384]{1,0:T(8,128)(2,1)S(1)}, bf16[8,48,1024]{2,1,0:T(8,128)(2,1)S(1)}, bf16[8,48,1024]{2,1,0:T(8,128)(2,1)S(1)}) custom-call(bf16[3,1024,384]{2,1,0:T(8,128)(2,1)S(1)} %get-tuple-element.107.qkv_ref.refs_0_, bf16[1024,384]{1,0:T(8,128)(2,1)S(1)} %get-tuple-element.153.refs_1_, ...), custom_call_target="tpu_custom_call" | custom-call | flops 6710886400 | bytes 2097152 | tf_op jit(solution)/shard_map/attention_back/pallas_call | solution.py:458
  65.2 1.8 %weights.1 = (f32[1,128]{1,0:T(1,128)S(1)}, bf16[3,48,384]{2,1,0:T(8,128)(2,1)S(1)}, bf16[48,384]{1,0:T(8,128)(2,1)S(1)}, bf16[2,48,1024]{2,1,0:T(8,128)(2,1)S(1)}, bf16[48,1024]{1,0:T(8,128)(2,1)S(1)}) custom-call(bf16[3,768,384]{2,1,0:T(8,128)(2,1)S(1)} %copy-done, bf16[384,768]{1,0:T(8,128)(2,1)S(1)} %copy-done.4, bf16[2,768,1024]{2,1,0:T(8,128)(2,1)S(1)} %copy-done.1, ...), custom_call_target="tpu_custom_call" | custom-call | flops 1048576 | bytes 7340032 | tf_op jit(solution)/shard_map/weights/pallas_call | solution.py:848
  66.9 7.7 %attention_back.4 = (bf16[1024,384]{1,0:T(8,128)(2,1)S(1)}, bf16[8,48,1024]{2,1,0:T(8,128)(2,1)S(1)}, bf16[8,48,1024]{2,1,0:T(8,128)(2,1)S(1)}) custom-call(bf16[3,1024,384]{2,1,0:T(8,128)(2,1)S(1)} %get-tuple-element.107.qkv_ref.refs_0_, bf16[1024,384]{1,0:T(8,128)(2,1)S(1)} %get-tuple-element.153.refs_1_, ...), custom_call_target="tpu_custom_call", output_to_operand_aliasing={{1}: (8, {}), {2}: (9, {})} | custom-call | flops 6710886400 | bytes 2097152 | tf_op jit(solution)/shard_map/attention_back/pallas_call | solution.py:458
  75.0 2.1 %collective-permute-start.12 = (bf16[4,48,1536]{2,1,0:T(8,128)(2,1)S(1)}, bf16[4,48,1536]{2,1,0:T(8,128)(2,1)S(1)}, u32[]{:S(2)}, u32[]{:S(2)}) collective-permute-start(bf16[4,48,1536]{2,1,0:T(8,128)(2,1)S(1)} %turn.12), channel_id=1, source_target_pairs={{0,4},{1,3},{2,6},{3,1},{4,0},{5,7},{6,2},{7,5},{8,12},{9,11},{10,... | collective-permute-start | bytes 1769480 | tf_op jit(solution)/shard_map/ppermute | solution.py:85
  77.1 7.7 %attention_back.5 = (bf16[1024,384]{1,0:T(8,128)(2,1)S(1)}, bf16[8,48,512]{2,1,0:T(8,128)(2,1)S(1)}, bf16[8,48,512]{2,1,0:T(8,128)(2,1)S(1)}) custom-call(bf16[3,1024,384]{2,1,0:T(8,128)(2,1)S(1)} %get-tuple-element.107.qkv_ref.refs_0_, bf16[1024,384]{1,0:T(8,128)(2,1)S(1)} %get-tuple-element.153.refs_1_, ...), custom_call_target="tpu_custom_call" | custom-call | flops 6710886400 | bytes 2097152 | tf_op jit(solution)/shard_map/attention_back/pallas_call | solution.py:458
  86.4 4.9 %collective-permute-done.12.refs_7_ = bf16[4,48,1536]{2,1,0:T(8,128)(2,1)S(1)} collective-permute-done((bf16[4,48,1536]{2,1,0:T(8,128)(2,1)S(1)}, bf16[4,48,1536]{2,1,0:T(8,128)(2,1)S(1)}, u32[]{:S(2)}, u32[]{:S(2)}) %collective-permute-start.12) | collective-permute-done | bytes 589856 | tf_op jit(solution)/shard_map/ppermute | solution.py:85
  91.6 2.1 %collective-permute-start.13 = (bf16[2,48,3072]{2,1,0:T(8,128)(2,1)S(1)}, bf16[2,48,3072]{2,1,0:T(8,128)(2,1)S(1)}, u32[]{:S(2)}, u32[]{:S(2)}) collective-permute-start(bf16[2,48,3072]{2,1,0:T(8,128)(2,1)S(1)} %turn.13), channel_id=1, source_target_pairs={{0,8},{1,9},{2,10},{3,11},{4,12},{5,13},{6,14},{7,15},{8,0},{9,1},... | collective-permute-start | bytes 1769480 | tf_op jit(solution)/shard_map/ppermute | solution.py:85
  93.7 2.8 %collective-permute-done.16.refs_3_.refs_13_ = bf16[8,48,512]{2,1,0:T(8,128)(2,1)S(1)} collective-permute-done((bf16[8,48,512]{2,1,0:T(8,128)(2,1)S(1)}, bf16[8,48,512]{2,1,0:T(8,128)(2,1)S(1)}, u32[]{:S(2)}, u32[]{:S(2)}) %collective-permute-start.16) | collective-permute-done | bytes 393248 | tf_op jit(solution)/shard_map/ppermute | solution.py:85
  96.9 1.8 %collective-permute-start.17 = (bf16[4,48,1536]{2,1,0:T(8,128)(2,1)S(1)}, bf16[4,48,1536]{2,1,0:T(8,128)(2,1)S(1)}, u32[]{:S(2)}, u32[]{:S(2)}) collective-permute-start(bf16[4,48,1536]{2,1,0:T(8,128)(2,1)S(1)} %turn.15), channel_id=1, source_target_pairs={{0,4},{1,9},{2,6},{3,11},{4,0},{5,13},{6,2},{7,15},{8,12},{9,1},{1... | collective-permute-start | bytes 1769480 | tf_op jit(solution)/shard_map/ppermute | solution.py:85
  100.2 7.7 %collective-permute-done.13.refs_8_ = bf16[2,48,3072]{2,1,0:T(8,128)(2,1)S(1)} collective-permute-done((bf16[2,48,3072]{2,1,0:T(8,128)(2,1)S(1)}, bf16[2,48,3072]{2,1,0:T(8,128)(2,1)S(1)}, u32[]{:S(2)}, u32[]{:S(2)}) %collective-permute-start.13) | collective-permute-done | bytes 589856 | tf_op jit(solution)/shard_map/ppermute | solution.py:85
  108.2 2.1 %collective-permute-start.18 = (bf16[2,48,1536]{2,1,0:T(8,128)(2,1)S(1)}, bf16[2,48,1536]{2,1,0:T(8,128)(2,1)S(1)}, u32[]{:S(2)}, u32[]{:S(2)}) collective-permute-start(bf16[2,48,1536]{2,1,0:T(8,128)(2,1)S(1)} %turn.16), channel_id=1, source_target_pairs={{0,8},{1,3},{2,10},{3,1},{4,12},{5,7},{6,14},{7,5},{8,0},{9,11},{1... | collective-permute-start | bytes 884744 | tf_op jit(solution)/shard_map/ppermute | solution.py:85
  110.3 2.6 %collective-permute-start.14 = (bf16[1,48,3072]{2,1,0:T(8,128)(2,1)S(1)}, bf16[1,48,3072]{2,1,0:T(8,128)(2,1)S(1)}, u32[]{:S(2)}, u32[]{:S(2)}) collective-permute-start(bf16[1,48,3072]{2,1,0:T(8,128)(2,1)S(1)} %turn.14), channel_id=1, source_target_pairs={{0,16},{1,17},{2,18},{3,19},{4,20},{5,21},{6,22},{7,23},{8,24},{9,... | collective-permute-start | bytes 884744 | tf_op jit(solution)/shard_map/ppermute | solution.py:85
  112.9 4.9 %collective-permute-done.18.refs_5_.refs_15_ = bf16[2,48,1536]{2,1,0:T(8,128)(2,1)S(1)} collective-permute-done((bf16[2,48,1536]{2,1,0:T(8,128)(2,1)S(1)}, bf16[2,48,1536]{2,1,0:T(8,128)(2,1)S(1)}, u32[]{:S(2)}, u32[]{:S(2)}) %collective-permute-start.18) | collective-permute-done | bytes 294944 | tf_op jit(solution)/shard_map/ppermute | solution.py:85
  118.9 3.1 %input_grad.1 = (f32[512,768]{1,0:T(8,128)}, f32[1,768]{1,0:T(1,128)S(1)}) custom-call(bf16[1024,384]{1,0:T(8,128)(2,1)S(1)} %get-tuple-element.139.refs_0_, bf16[1024,384]{1,0:T(8,128)(2,1)S(1)} %get-tuple-element.150.refs_1_, bf16[1024,384]{1,0:T(8,128)(2,1)S(1)} %get-tuple-element.154.refs_2_, bf16[3,768,384]{2,1,0:T(8,128)(2,1)S(1)} %copy-done, ...), custom_call_target="tpu_custom_call" | custom-call | flops 905969664 | bytes 8388608 | tf_op jit(solution)/shard_map/input_grad/pallas_call | solution.py:587
  122.0 5.9 %collective-permute-done.14.refs_9_ = bf16[1,48,3072]{2,1,0:T(8,128)(2,1)S(1)} collective-permute-done((bf16[1,48,3072]{2,1,0:T(8,128)(2,1)S(1)}, bf16[1,48,3072]{2,1,0:T(8,128)(2,1)S(1)}, u32[]{:S(2)}, u32[]{:S(2)}) %collective-permute-start.14) | collective-permute-done | bytes 294944 | tf_op jit(solution)/shard_map/ppermute | solution.py:85
  127.9 3.2 %collective-permute-done.19.refs_16_ = bf16[1,48,1536]{2,1,0:T(8,128)(2,1)S(1)} collective-permute-done((bf16[1,48,1536]{2,1,0:T(8,128)(2,1)S(1)}, bf16[1,48,1536]{2,1,0:T(8,128)(2,1)S(1)}, u32[]{:S(2)}, u32[]{:S(2)}) %collective-permute-start.19) | collective-permute-done | bytes 147488 | tf_op jit(solution)/shard_map/ppermute | solution.py:85
  132.5 2.5 %collective-permute-start.20 = (f32[64,128]{1,0:T(8,128)S(1)}, f32[64,128]{1,0:T(8,128)S(1)}, u32[]{:S(2)}, u32[]{:S(2)}) collective-permute-start(f32[64,128]{1,0:T(8,128)S(1)} %get-tuple-element.169.own_ref), channel_id=1, source_target_pairs={{0,1},{1,0},{2,3},{3,2},{4,5},{5,4},{6,7},{7,6},{8,9},{9,8},{10,11... | collective-permute-start | bytes 98312 | tf_op jit(solution)/shard_map/ppermute | solution.py:89
  137.4 2.4 %collective-permute-done.21 = f32[8,1024]{1,0:T(8,128)S(1)} collective-permute-done((f32[8,1024]{1,0:T(8,128)S(1)}, f32[8,1024]{1,0:T(8,128)S(1)}, u32[]{:S(2)}, u32[]{:S(2)}) %collective-permute-start.21) | collective-permute-done | bytes 32800 | tf_op jit(solution)/shard_map/ppermute | solution.py:85
  141.4 2.4 %collective-permute-done.22 = f32[8,1024]{1,0:T(8,128)S(1)} collective-permute-done((f32[8,1024]{1,0:T(8,128)S(1)}, f32[8,1024]{1,0:T(8,128)S(1)}, u32[]{:S(2)}, u32[]{:S(2)}) %collective-permute-start.22) | collective-permute-done | bytes 32800 | tf_op jit(solution)/shard_map/ppermute | solution.py:85
  145.1 2.6 %collective-permute-done.23 = f32[8,1024]{1,0:T(8,128)S(1)} collective-permute-done((f32[8,1024]{1,0:T(8,128)S(1)}, f32[8,1024]{1,0:T(8,128)S(1)}, u32[]{:S(2)}, u32[]{:S(2)}) %collective-permute-start.23) | collective-permute-done | bytes 32800 | tf_op jit(solution)/shard_map/ppermute | solution.py:85
  148.9 3.6 %collective-permute-done.24 = f32[8,1024]{1,0:T(8,128)S(1)} collective-permute-done((f32[8,1024]{1,0:T(8,128)S(1)}, f32[8,1024]{1,0:T(8,128)S(1)}, u32[]{:S(2)}, u32[]{:S(2)}) %collective-permute-start.24) | collective-permute-done | bytes 32800 | tf_op jit(solution)/shard_map/ppermute | solution.py:85
  152.6 2.6 %update.1 = (bf16[3,48,384]{2,1,0:T(8,128)(2,1)}, bf16[48,384]{1,0:T(8,128)(2,1)}, bf16[2,48,1024]{2,1,0:T(8,128)(2,1)}, bf16[48,1024]{1,0:T(8,128)(2,1)}, f32[3...) custom-call(f32[128]{0:T(128)S(1)} %compare_select_fusion.refs_0_, ...), custom_call_target="tpu_custom_call" | custom-call | flops 1048576 | bytes 4194304 | tf_op jit(solution)/shard_map/update/pallas_call | solution.py:785
  (85 shorter events, 19.1 us)
Async XLA Ops:
  0.7 4.1 %collective-permute-start = (bf16[512,768]{1,0:T(8,128)(2,1)}, bf16[512,768]{1,0:T(8,128)(2,1)S(1)}, u32[]{:S(2)}, u32[]{:S(2)}) collective-permute-start(bf16[512,768]{1,0:T(8,128)(2,1)} %refs_5_.3), channel_id=1, source_target_pairs={{0,1},{1,0},{2,3},{3,2},{4,5},{5,4},{6,7},{7,6},{8,9},{9,8},{10,11... | collective-permute-start | bytes 2359304 | tf_op jit(solution)/shard_map/ppermute | solution.py:89
  4.8 16.4 %collective-permute-start.3 = (bf16[2,768,1024]{2,1,0:T(8,128)(2,1)}, bf16[2,768,1024]{2,1,0:T(8,128)(2,1)S(1)}, u32[]{:S(2)}, u32[]{:S(2)}) collective-permute-start(bf16[2,768,1024]{2,1,0:T(8,128)(2,1)} %gu_ref), channel_id=1, source_target_pairs={{0,1},{1,0},{2,3},{3,2},{4,5},{5,4},{6,7},{7,6},{8,9},{9,8},{10,11... | collective-permute-start | bytes 9437192 | tf_op jit(solution)/shard_map/ppermute | solution.py:89
  5.0 16.3 %collective-permute-start.4 = (bf16[1024,768]{1,0:T(8,128)(2,1)S(1)}, bf16[1024,768]{1,0:T(8,128)(2,1)S(1)}, u32[]{:S(2)}, u32[]{:S(2)}) collective-permute-start(bf16[1024,768]{1,0:T(8,128)(2,1)S(1)} %copy-done.2), channel_id=1, source_target_pairs={{0,1},{1,0},{2,3},{3,2},{4,5},{5,4},{6,7},{7,6},{8,9},{9,8},{10,11... | collective-permute-start | bytes 4718600 | tf_op jit(solution)/shard_map/ppermute | solution.py:89
  5.4 15.9 %collective-permute-start.2 = (bf16[384,768]{1,0:T(8,128)(2,1)}, bf16[384,768]{1,0:T(8,128)(2,1)S(1)}, u32[]{:S(2)}, u32[]{:S(2)}) collective-permute-start(bf16[384,768]{1,0:T(8,128)(2,1)} %out_ref), channel_id=1, source_target_pairs={{0,1},{1,0},{2,3},{3,2},{4,5},{5,4},{6,7},{7,6},{8,9},{9,8},{10,11... | collective-permute-start | bytes 1769480 | tf_op jit(solution)/shard_map/ppermute | solution.py:89
  7.2 14.0 %copy-start.3 = (bf16[512,768]{1,0:T(8,128)(2,1)S(1)}, bf16[512,768]{1,0:T(8,128)(2,1)}, u32[]{:S(2)}) copy-start(bf16[512,768]{1,0:T(8,128)(2,1)} %refs_5_.3) | copy-start | bytes 2359300
  19.4 1.8 %collective-permute-start.1 = (bf16[512,384]{1,0:T(8,128)(2,1)S(1)}, bf16[512,384]{1,0:T(8,128)(2,1)S(1)}, u32[]{:S(2)}, u32[]{:S(2)}) collective-permute-start(bf16[512,384]{1,0:T(8,128)(2,1)S(1)} %get-tuple-element.109.refs_3_), channel_id=1, source_target_pairs={{0,1},{1,0},{2,3},{3,2},{4,5},{5,4},{6,7},{7,6},{8,9},{9,8},{10,11... | collective-permute-start | bytes 1179656 | tf_op jit(solution)/shard_map/ppermute | solution.py:89
  28.1 6.0 %collective-permute-start.5 = (bf16[16,48,1536]{2,1,0:T(8,128)(2,1)S(1)}, bf16[16,48,1536]{2,1,0:T(8,128)(2,1)S(1)}, u32[]{:S(2)}, u32[]{:S(2)}) collective-permute-start(bf16[16,48,1536]{2,1,0:T(8,128)(2,1)S(1)} %get-tuple-element.121), channel_id=1, source_target_pairs={{0,1},{1,0},{2,3},{3,2},{4,5},{5,4},{6,7},{7,6},{8,9},{9,8},{10,11... | collective-permute-start | bytes 7077896 | tf_op jit(solution)/shard_map/ppermute | solution.py:89
  34.4 16.8 %collective-permute-start.6 = (bf16[8,48,1536]{2,1,0:T(8,128)(2,1)S(1)}, bf16[8,48,1536]{2,1,0:T(8,128)(2,1)S(1)}, u32[]{:S(2)}, u32[]{:S(2)}) collective-permute-start(bf16[8,48,1536]{2,1,0:T(8,128)(2,1)S(1)} %turn.9), channel_id=1, source_target_pairs={{0,2},{1,5},{2,0},{3,7},{4,6},{5,1},{6,4},{7,3},{8,10},{9,13},{10,... | collective-permute-start | bytes 3538952 | tf_op jit(solution)/shard_map/ppermute | solution.py:85
  42.7 12.1 %collective-permute-start.8 = (bf16[16,48,1536]{2,1,0:T(8,128)(2,1)S(1)}, bf16[16,48,1536]{2,1,0:T(8,128)(2,1)S(1)}, u32[]{:S(2)}, u32[]{:S(2)}) collective-permute-start(bf16[16,48,1536]{2,1,0:T(8,128)(2,1)S(1)} %get-tuple-element.133), channel_id=1, source_target_pairs={{0,1},{1,0},{2,3},{3,2},{4,5},{5,4},{6,7},{7,6},{8,9},{9,8},{10,11... | collective-permute-start | bytes 7077896 | tf_op jit(solution)/shard_map/ppermute | solution.py:89
  51.4 2.4 %collective-permute-start.7 = (bf16[512,768]{1,0:T(8,128)(2,1)S(1)}, bf16[512,768]{1,0:T(8,128)(2,1)S(1)}, u32[]{:S(2)}, u32[]{:S(2)}) collective-permute-start(bf16[512,768]{1,0:T(8,128)(2,1)S(1)} %get-tuple-element.130.own_ref), channel_id=1, source_target_pairs={{0,1},{1,0},{2,3},{3,2},{4,5},{5,4},{6,7},{7,6},{8,9},{9,8},{10,11... | collective-permute-start | bytes 2359304 | tf_op jit(solution)/shard_map/ppermute | solution.py:89
  51.5 34.9 %collective-permute-start.11 = (bf16[4,48,1536]{2,1,0:T(8,128)(2,1)S(1)}, bf16[4,48,1536]{2,1,0:T(8,128)(2,1)S(1)}, u32[]{:S(2)}, u32[]{:S(2)}) collective-permute-start(bf16[4,48,1536]{2,1,0:T(8,128)(2,1)S(1)} %turn.10), channel_id=1, source_target_pairs={{0,4},{1,3},{2,6},{3,1},{4,0},{5,7},{6,2},{7,5},{8,12},{9,11},{10,... | collective-permute-start | bytes 1769480 | tf_op jit(solution)/shard_map/ppermute | solution.py:85
  55.1 19.7 %collective-permute-start.9 = (bf16[8,48,1536]{2,1,0:T(8,128)(2,1)S(1)}, bf16[8,48,1536]{2,1,0:T(8,128)(2,1)S(1)}, u32[]{:S(2)}, u32[]{:S(2)}) collective-permute-start(bf16[8,48,1536]{2,1,0:T(8,128)(2,1)S(1)} %turn.11), channel_id=1, source_target_pairs={{0,2},{1,5},{2,0},{3,7},{4,6},{5,1},{6,4},{7,3},{8,10},{9,13},{10,... | collective-permute-start | bytes 3538952 | tf_op jit(solution)/shard_map/ppermute | solution.py:85
  74.7 21.8 %collective-permute-start.15 = (bf16[8,48,1024]{2,1,0:T(8,128)(2,1)S(1)}, bf16[8,48,1024]{2,1,0:T(8,128)(2,1)S(1)}, u32[]{:S(2)}, u32[]{:S(2)}) collective-permute-start(bf16[8,48,1024]{2,1,0:T(8,128)(2,1)S(1)} %get-tuple-element.151), channel_id=1, source_target_pairs={{0,2},{1,5},{2,0},{3,7},{4,6},{5,1},{6,4},{7,3},{8,10},{9,13},{10,... | collective-permute-start | bytes 2359304 | tf_op jit(solution)/shard_map/ppermute | solution.py:85
  75.0 16.3 %collective-permute-start.12 = (bf16[4,48,1536]{2,1,0:T(8,128)(2,1)S(1)}, bf16[4,48,1536]{2,1,0:T(8,128)(2,1)S(1)}, u32[]{:S(2)}, u32[]{:S(2)}) collective-permute-start(bf16[4,48,1536]{2,1,0:T(8,128)(2,1)S(1)} %turn.12), channel_id=1, source_target_pairs={{0,4},{1,3},{2,6},{3,1},{4,0},{5,7},{6,2},{7,5},{8,12},{9,11},{10,... | collective-permute-start | bytes 1769480 | tf_op jit(solution)/shard_map/ppermute | solution.py:85
  84.8 11.7 %collective-permute-start.16 = (bf16[8,48,512]{2,1,0:T(8,128)(2,1)S(1)}, bf16[8,48,512]{2,1,0:T(8,128)(2,1)S(1)}, u32[]{:S(2)}, u32[]{:S(2)}) collective-permute-start(bf16[8,48,512]{2,1,0:T(8,128)(2,1)S(1)} %get-tuple-element.159), channel_id=1, source_target_pairs={{0,2},{1,5},{2,0},{3,7},{4,6},{5,1},{6,4},{7,3},{8,10},{9,13},{10,... | collective-permute-start | bytes 1179656 | tf_op jit(solution)/shard_map/ppermute | solution.py:85
  91.6 16.3 %collective-permute-start.13 = (bf16[2,48,3072]{2,1,0:T(8,128)(2,1)S(1)}, bf16[2,48,3072]{2,1,0:T(8,128)(2,1)S(1)}, u32[]{:S(2)}, u32[]{:S(2)}) collective-permute-start(bf16[2,48,3072]{2,1,0:T(8,128)(2,1)S(1)} %turn.13), channel_id=1, source_target_pairs={{0,8},{1,9},{2,10},{3,11},{4,12},{5,13},{6,14},{7,15},{8,0},{9,1},... | collective-permute-start | bytes 1769480 | tf_op jit(solution)/shard_map/ppermute | solution.py:85
  96.9 11.2 %collective-permute-start.17 = (bf16[4,48,1536]{2,1,0:T(8,128)(2,1)S(1)}, bf16[4,48,1536]{2,1,0:T(8,128)(2,1)S(1)}, u32[]{:S(2)}, u32[]{:S(2)}) collective-permute-start(bf16[4,48,1536]{2,1,0:T(8,128)(2,1)S(1)} %turn.15), channel_id=1, source_target_pairs={{0,4},{1,9},{2,6},{3,11},{4,0},{5,13},{6,2},{7,15},{8,12},{9,1},{1... | collective-permute-start | bytes 1769480 | tf_op jit(solution)/shard_map/ppermute | solution.py:85
  100.1 18.8 %collective-permute-start.10 = (bf16[512,768]{1,0:T(8,128)(2,1)S(1)}, bf16[512,768]{1,0:T(8,128)(2,1)S(1)}, u32[]{:S(2)}, u32[]{:S(2)}) collective-permute-start(bf16[512,768]{1,0:T(8,128)(2,1)S(1)} %input_other.1), channel_id=1, source_target_pairs={{0,1},{1,0},{2,3},{3,2},{4,5},{5,4},{6,7},{7,6},{8,9},{9,8},{10,11... | collective-permute-start | bytes 2359304 | tf_op jit(solution)/shard_map/ppermute | solution.py:89
  108.2 9.5 %collective-permute-start.18 = (bf16[2,48,1536]{2,1,0:T(8,128)(2,1)S(1)}, bf16[2,48,1536]{2,1,0:T(8,128)(2,1)S(1)}, u32[]{:S(2)}, u32[]{:S(2)}) collective-permute-start(bf16[2,48,1536]{2,1,0:T(8,128)(2,1)S(1)} %turn.16), channel_id=1, source_target_pairs={{0,8},{1,3},{2,10},{3,1},{4,12},{5,7},{6,14},{7,5},{8,0},{9,11},{1... | collective-permute-start | bytes 884744 | tf_op jit(solution)/shard_map/ppermute | solution.py:85
  110.3 17.6 %collective-permute-start.14 = (bf16[1,48,3072]{2,1,0:T(8,128)(2,1)S(1)}, bf16[1,48,3072]{2,1,0:T(8,128)(2,1)S(1)}, u32[]{:S(2)}, u32[]{:S(2)}) collective-permute-start(bf16[1,48,3072]{2,1,0:T(8,128)(2,1)S(1)} %turn.14), channel_id=1, source_target_pairs={{0,16},{1,17},{2,18},{3,19},{4,20},{5,21},{6,22},{7,23},{8,24},{9,... | collective-permute-start | bytes 884744 | tf_op jit(solution)/shard_map/ppermute | solution.py:85
  117.9 13.2 %collective-permute-start.19 = (bf16[1,48,1536]{2,1,0:T(8,128)(2,1)S(1)}, bf16[1,48,1536]{2,1,0:T(8,128)(2,1)S(1)}, u32[]{:S(2)}, u32[]{:S(2)}) collective-permute-start(bf16[1,48,1536]{2,1,0:T(8,128)(2,1)S(1)} %turn.17), channel_id=1, source_target_pairs={{0,16},{1,17},{2,18},{3,19},{4,20},{5,21},{6,22},{7,23},{8,24},{9,... | collective-permute-start | bytes 442376 | tf_op jit(solution)/shard_map/ppermute | solution.py:85
  131.1 21.4 %copy-start.7 = (f32[3,768]{1,0:T(4,128)S(1)}, f32[3,768]{1,0:T(4,128)}, u32[]{:S(2)}) copy-start(f32[3,768]{1,0:T(4,128)} %refs_7_.5) | copy-start | bytes 27652
  131.1 21.4 %copy-start.8 = (f32[2,1024]{1,0:T(2,128)S(1)}, f32[2,1024]{1,0:T(2,128)}, u32[]{:S(2)}) copy-start(f32[2,1024]{1,0:T(2,128)} %refs_13_.1) | copy-start | bytes 24580
  131.1 21.4 %copy-start.10 = (f32[2,768]{1,0:T(2,128)S(1)}, f32[2,768]{1,0:T(2,128)}, u32[]{:S(2)}) copy-start(f32[2,768]{1,0:T(2,128)} %refs_9_.3) | copy-start | bytes 18436
  131.1 21.4 %copy-start.11 = (f32[3,384]{1,0:T(4,128)S(1)}, f32[3,384]{1,0:T(4,128)}, u32[]{:S(2)}) copy-start(f32[3,384]{1,0:T(4,128)} %refs_11_.1) | copy-start | bytes 13828
  131.1 21.4 %copy-start.13 = (f32[768]{0:T(1024)S(1)}, f32[768]{0:T(1024)}, u32[]{:S(2)}) copy-start(f32[768]{0:T(1024)} %refs_8_.3) | copy-start | bytes 9220
  131.1 21.4 %copy-start.14 = (f32[768]{0:T(1024)S(1)}, f32[768]{0:T(1024)}, u32[]{:S(2)}) copy-start(f32[768]{0:T(1024)} %refs_10_.1) | copy-start | bytes 9220
  132.5 3.4 %collective-permute-start.20 = (f32[64,128]{1,0:T(8,128)S(1)}, f32[64,128]{1,0:T(8,128)S(1)}, u32[]{:S(2)}, u32[]{:S(2)}) collective-permute-start(f32[64,128]{1,0:T(8,128)S(1)} %get-tuple-element.169.own_ref), channel_id=1, source_target_pairs={{0,1},{1,0},{2,3},{3,2},{4,5},{5,4},{6,7},{7,6},{8,9},{9,8},{10,11... | collective-permute-start | bytes 98312 | tf_op jit(solution)/shard_map/ppermute | solution.py:89
  135.9 4.0 %collective-permute-start.21 = (f32[8,1024]{1,0:T(8,128)S(1)}, f32[8,1024]{1,0:T(8,128)S(1)}, u32[]{:S(2)}, u32[]{:S(2)}) collective-permute-start(f32[8,1024]{1,0:T(8,128)S(1)} %get-tuple-element.170), channel_id=1, source_target_pairs={{0,2},{1,5},{2,0},{3,7},{4,6},{5,1},{6,4},{7,3},{8,10},{9,13},{10,... | collective-permute-start | bytes 98312 | tf_op jit(solution)/shard_map/ppermute | solution.py:85
  139.8 3.9 %collective-permute-start.22 = (f32[8,1024]{1,0:T(8,128)S(1)}, f32[8,1024]{1,0:T(8,128)S(1)}, u32[]{:S(2)}, u32[]{:S(2)}) collective-permute-start(f32[8,1024]{1,0:T(8,128)S(1)} %add.12), channel_id=1, source_target_pairs={{0,4},{1,9},{2,6},{3,11},{4,0},{5,13},{6,2},{7,15},{8,12},{9,1},{1... | collective-permute-start | bytes 98312 | tf_op jit(solution)/shard_map/ppermute | solution.py:85
  143.8 3.9 %collective-permute-start.23 = (f32[8,1024]{1,0:T(8,128)S(1)}, f32[8,1024]{1,0:T(8,128)S(1)}, u32[]{:S(2)}, u32[]{:S(2)}) collective-permute-start(f32[8,1024]{1,0:T(8,128)S(1)} %add.13), channel_id=1, source_target_pairs={{0,8},{1,3},{2,10},{3,1},{4,12},{5,7},{6,14},{7,5},{8,0},{9,11},{1... | collective-permute-start | bytes 98312 | tf_op jit(solution)/shard_map/ppermute | solution.py:85
  147.7 4.8 %collective-permute-start.24 = (f32[8,1024]{1,0:T(8,128)S(1)}, f32[8,1024]{1,0:T(8,128)S(1)}, u32[]{:S(2)}, u32[]{:S(2)}) collective-permute-start(f32[8,1024]{1,0:T(8,128)S(1)} %add.14), channel_id=1, source_target_pairs={{0,16},{1,17},{2,18},{3,19},{4,20},{5,21},{6,22},{7,23},{8,24},{9,... | collective-permute-start | bytes 98312 | tf_op jit(solution)/shard_map/ppermute | solution.py:85
  (11 other events, 84.0 us)

commit v5 on v4

--- a/solution.py
+++ b/solution.py
@@ -965,9 +965,10 @@
         piece, carried = back(pair, pair, pairs - 1, carried, grad=mixed_grad)
         pieces.append(piece)
     keep, send = kept_and_sent(carried, n_wide)
+    send = after(send, wide_parts[1].turn(piece))
+    wide_parts[1].go()
     first = [keep, stage_exchange(send, 0, n_wide, PAIRS)]
-    mixed_grad = after(mixed_grad, send, wide_parts[1].turn(piece))
-    wide_parts[1].go()
+    mixed_grad = after(mixed_grad, send)
     piece, carried = back(pairs - 1, 0, 1, [], grad=mixed_grad)
     pieces.append(piece)
     keep, send = kept_and_sent(carried, n_wide)

time: 158 us -> 157 us (level)
  transfers between devices with their start and end apart: 25 -> 25, of which waited for: 14 -> 15; matrix products, arithmetic and copies ran while one was open for 0% -> 0% of each run, Pallas kernels for 44% -> 44%
where the time goes in v5:
time: 157 us; the launch traced here: 154 us
  Pallas kernels  79.3 us (51%)
  waiting for transfers between devices  43.6 us (28%)
  starting transfers between devices  28.4 us (18%)
  between operations  2.66 us (2%)
    ppermute x15, waiting for transfers between devices, stage_exchange(): return lax.ppermute(values, ('wide', 'narrow'), pairs)  41.2 us
    pallas_call x4, Pallas kernels, middle_call(): pl.pallas_call(functools.partial(middle_kernel, first, last, rows_each, n...  25.1 us
    pallas_call x3, Pallas kernels, attention_back(): pl.pallas_call(functools.partial(attention_back_kernel, block, rows_each,...  23.4 us
    ppermute x15, starting transfers between devices, stage_exchange(): return lax.ppermute(values, ('wide', 'narrow'), pairs)  23.2 us
    pallas_call x1, Pallas kernels, attention(): pl.pallas_call(functools.partial(attention_kernel, block=block), grid=(pa...  12.1 us
    pallas_call x2, Pallas kernels, project(): pl.pallas_call(functools.partial(project_kernel, len(carried)), grid=(1,)...  5.26 us
    ppermute x10, starting transfers between devices, swap(): return lax.ppermute(values, 'narrow', [(0, 1), (1, 0)])  5.2 us
  transfers between devices with their start and end apart: 25, of which 15 were waited for; matrix products, arithmetic and copies ran while one was open for 0% of the time, Pallas kernels for 44%

profile of v5, /device:TPU:0, one launch (start us, length us, event | category | flops | bytes accessed | tf_op | source)
XLA Modules:
  0.0 154.0 jit_solution(17640607030726739296)
XLA Ops:
  1.2 3.5 %project.2 = (bf16[768,1024]{1,0:T(8,128)(2,1)S(1)}, bf16[3,1024,384]{2,1,0:T(8,128)(2,1)S(1)}) custom-call(bf16[512,768]{1,0:T(8,128)(2,1)} %refs_5_.3, f32[768]{0:T(1024)} %refs_6_.5, bf16[3,768,384]{2,1,0:T(8,128)(2,1)} %refs_3_.5), custom_call_target="tpu_custom_call" | custom-call | flops 905969664 | bytes 1572864 | tf_op jit(solution)/shard_map/project/pallas_call | solution.py:126
  5.5 1.7 %project.3 = (bf16[768,1024]{1,0:T(8,128)(2,1)S(1)}, bf16[3,1024,384]{2,1,0:T(8,128)(2,1)S(1)}) custom-call(bf16[512,768]{1,0:T(8,128)(2,1)S(1)} %collective-permute-done.rows_ref, f32[768]{0:T(1024)S(1)} %copy-done.6, bf16[3,768,384]{2,1,0:T(8,128)(2,1)S(1)} %copy-done, ...), custom_call_target="tpu_custom_call", output_to_operand_aliasing={{0}: (3, {}), {1}: (4, {})} | custom-call | flops 905969664 | bytes 1572864 | tf_op jit(solution)/shard_map/project/pallas_call | solution.py:126
  7.3 12.1 %attention.1 = (bf16[512,384]{1,0:T(8,128)(2,1)S(1)}, bf16[512,384]{1,0:T(8,128)(2,1)S(1)}, bf16[6,1024,128]{2,1,0:T(8,128)(2,1)S(1)}, bf16[1024,128]{1,0:T(8,128)(2,1)S(1)}) custom-call(bf16[3,1024,384]{2,1,0:T(8,128)(2,1)S(1)} %get-tuple-element.108.qkv_ref.refs_0_, s32[1024]{0:T(1024)S(1)} %copy-done.16, s32[1024]{0:T(1024)S(1)} %copy-done.17), custom_call_target="tpu_custom_call" | custom-call | flops 6442450944 | bytes 3932160 | tf_op jit(solution)/shard_map/attention/pallas_call | solution.py:208
  21.3 6.7 %middle.4 = (f32[512,768]{1,0:T(8,128)S(1)}, bf16[512,768]{1,0:T(8,128)(2,1)S(1)}, bf16[768,512]{1,0:T(8,128)(2,1)S(1)}, bf16[512,768]{1,0:T(8,128)(2,1)S(1)}, b...) custom-call(bf16[512,768]{1,0:T(8,128)(2,1)S(1)} %copy-done.3, ...), custom_call_target="tpu_custom_call" | custom-call | flops 7247757312 | bytes 393216 | tf_op jit(solution)/shard_map/middle/pallas_call | solution.py:337
  28.5 5.5 %middle.5 = (f32[512,768]{1,0:T(8,128)S(1)}, f32[512,768]{1,0:T(8,128)S(1)}, bf16[16,48,1536]{2,1,0:T(8,128)(2,1)S(1)}) custom-call(bf16[512,768]{1,0:T(8,128)(2,1)S(1)} %get-tuple-element.123.refs_0_, bf16[768,512]{1,0:T(8,128)(2,1)S(1)} %get-tuple-element.116.refs_1_, bf16[512,768]{1,0:T(8,128)(2,1)S(1)} %get-tuple-element.117.refs_2_, ...), custom_call_target="tpu_custom_call" | custom-call | flops 7247757312 | bytes 393216 | tf_op jit(solution)/shard_map/middle/pallas_call | solution.py:337
  34.4 2.6 %collective-permute-start.6 = (bf16[8,48,1536]{2,1,0:T(8,128)(2,1)S(1)}, bf16[8,48,1536]{2,1,0:T(8,128)(2,1)S(1)}, u32[]{:S(2)}, u32[]{:S(2)}) collective-permute-start(bf16[8,48,1536]{2,1,0:T(8,128)(2,1)S(1)} %turn.9), channel_id=1, source_target_pairs={{0,2},{1,5},{2,0},{3,7},{4,6},{5,1},{6,4},{7,3},{8,10},{9,13},{10,... | collective-permute-start | bytes 3538952 | tf_op jit(solution)/shard_map/ppermute | solution.py:85
  37.0 5.7 %middle.6 = (f32[512,768]{1,0:T(8,128)S(1)}, f32[512,768]{1,0:T(8,128)S(1)}, bf16[16,48,1536]{2,1,0:T(8,128)(2,1)S(1)}) custom-call(bf16[512,768]{1,0:T(8,128)(2,1)S(1)} %get-tuple-element.123.refs_0_, bf16[768,512]{1,0:T(8,128)(2,1)S(1)} %get-tuple-element.116.refs_1_, bf16[512,768]{1,0:T(8,128)(2,1)S(1)} %get-tuple-element.117.refs_2_, ...), custom_call_target="tpu_custom_call" | custom-call | flops 7247757312 | bytes 393216 | tf_op jit(solution)/shard_map/middle/pallas_call | solution.py:337
  42.8 7.1 %middle.7 = (bf16[512,768]{1,0:T(8,128)(2,1)}, f32[512,768]{1,0:T(8,128)S(1)}, bf16[512,768]{1,0:T(8,128)(2,1)S(1)}, f32[1,768]{1,0:T(1,128)S(1)}, bf16[16,48,1536]{2,1,0:T(8,128)(2,1)S(1)}) custom-call(bf16[512,768]{1,0:T(8,128)(2,1)S(1)} %get-tuple-element.123.refs_0_, bf16[768,512]{1,0:T(8,128)(2,1)S(1)} %get-tuple-element.116.refs_1_, ...), custom_call_target="tpu_custom_call" | custom-call | flops 201326592 | bytes 393216 | tf_op jit(solution)/shard_map/middle/pallas_call | solution.py:337
  51.5 2.1 %collective-permute-start.11 = (bf16[4,48,1536]{2,1,0:T(8,128)(2,1)S(1)}, bf16[4,48,1536]{2,1,0:T(8,128)(2,1)S(1)}, u32[]{:S(2)}, u32[]{:S(2)}) collective-permute-start(bf16[4,48,1536]{2,1,0:T(8,128)(2,1)S(1)} %turn.10), channel_id=1, source_target_pairs={{0,4},{1,3},{2,6},{3,1},{4,0},{5,7},{6,2},{7,5},{8,12},{9,11},{10,... | collective-permute-start | bytes 1769480 | tf_op jit(solution)/shard_map/ppermute | solution.py:85
  55.1 2.1 %collective-permute-start.9 = (bf16[8,48,1536]{2,1,0:T(8,128)(2,1)S(1)}, bf16[8,48,1536]{2,1,0:T(8,128)(2,1)S(1)}, u32[]{:S(2)}, u32[]{:S(2)}) collective-permute-start(bf16[8,48,1536]{2,1,0:T(8,128)(2,1)S(1)} %turn.11), channel_id=1, source_target_pairs={{0,2},{1,5},{2,0},{3,7},{4,6},{5,1},{6,4},{7,3},{8,10},{9,13},{10,... | collective-permute-start | bytes 3538952 | tf_op jit(solution)/shard_map/ppermute | solution.py:85
  57.2 7.9 %attention_back.3 = (bf16[1024,384]{1,0:T(8,128)(2,1)S(1)}, bf16[8,48,1024]{2,1,0:T(8,128)(2,1)S(1)}, bf16[8,48,1024]{2,1,0:T(8,128)(2,1)S(1)}) custom-call(bf16[3,1024,384]{2,1,0:T(8,128)(2,1)S(1)} %get-tuple-element.108.qkv_ref.refs_0_, bf16[1024,384]{1,0:T(8,128)(2,1)S(1)} %get-tuple-element.155.refs_1_, ...), custom_call_target="tpu_custom_call" | custom-call | flops 6710886400 | bytes 2097152 | tf_op jit(solution)/shard_map/attention_back/pallas_call | solution.py:458
  65.2 1.8 %weights.1 = (f32[1,128]{1,0:T(1,128)S(1)}, bf16[3,48,384]{2,1,0:T(8,128)(2,1)S(1)}, bf16[48,384]{1,0:T(8,128)(2,1)S(1)}, bf16[2,48,1024]{2,1,0:T(8,128)(2,1)S(1)}, bf16[48,1024]{1,0:T(8,128)(2,1)S(1)}) custom-call(bf16[3,768,384]{2,1,0:T(8,128)(2,1)S(1)} %copy-done, bf16[384,768]{1,0:T(8,128)(2,1)S(1)} %copy-done.4, bf16[2,768,1024]{2,1,0:T(8,128)(2,1)S(1)} %copy-done.1, ...), custom_call_target="tpu_custom_call" | custom-call | flops 1048576 | bytes 7340032 | tf_op jit(solution)/shard_map/weights/pallas_call | solution.py:848
  66.9 7.7 %attention_back.4 = (bf16[1024,384]{1,0:T(8,128)(2,1)S(1)}, bf16[8,48,1024]{2,1,0:T(8,128)(2,1)S(1)}, bf16[8,48,1024]{2,1,0:T(8,128)(2,1)S(1)}) custom-call(bf16[3,1024,384]{2,1,0:T(8,128)(2,1)S(1)} %get-tuple-element.108.qkv_ref.refs_0_, bf16[1024,384]{1,0:T(8,128)(2,1)S(1)} %get-tuple-element.155.refs_1_, ...), custom_call_target="tpu_custom_call", output_to_operand_aliasing={{1}: (8, {}), {2}: (9, {})} | custom-call | flops 6710886400 | bytes 2097152 | tf_op jit(solution)/shard_map/attention_back/pallas_call | solution.py:458
  77.4 7.7 %attention_back.5 = (bf16[1024,384]{1,0:T(8,128)(2,1)S(1)}, bf16[8,48,512]{2,1,0:T(8,128)(2,1)S(1)}, bf16[8,48,512]{2,1,0:T(8,128)(2,1)S(1)}) custom-call(bf16[3,1024,384]{2,1,0:T(8,128)(2,1)S(1)} %get-tuple-element.108.qkv_ref.refs_0_, bf16[1024,384]{1,0:T(8,128)(2,1)S(1)} %get-tuple-element.155.refs_1_, ...), custom_call_target="tpu_custom_call" | custom-call | flops 6710886400 | bytes 2097152 | tf_op jit(solution)/shard_map/attention_back/pallas_call | solution.py:458
  86.4 4.7 %collective-permute-done.12.refs_7_ = bf16[4,48,1536]{2,1,0:T(8,128)(2,1)S(1)} collective-permute-done((bf16[4,48,1536]{2,1,0:T(8,128)(2,1)S(1)}, bf16[4,48,1536]{2,1,0:T(8,128)(2,1)S(1)}, u32[]{:S(2)}, u32[]{:S(2)}) %collective-permute-start.12) | collective-permute-done | bytes 589856 | tf_op jit(solution)/shard_map/ppermute | solution.py:85
  91.4 1.6 %collective-permute-start.13 = (bf16[2,48,3072]{2,1,0:T(8,128)(2,1)S(1)}, bf16[2,48,3072]{2,1,0:T(8,128)(2,1)S(1)}, u32[]{:S(2)}, u32[]{:S(2)}) collective-permute-start(bf16[2,48,3072]{2,1,0:T(8,128)(2,1)S(1)} %turn.13), channel_id=1, source_target_pairs={{0,8},{1,9},{2,10},{3,11},{4,12},{5,13},{6,14},{7,15},{8,0},{9,1},... | collective-permute-start | bytes 1769480 | tf_op jit(solution)/shard_map/ppermute | solution.py:85
  93.0 3.4 %collective-permute-done.16.refs_3_.refs_13_ = bf16[8,48,512]{2,1,0:T(8,128)(2,1)S(1)} collective-permute-done((bf16[8,48,512]{2,1,0:T(8,128)(2,1)S(1)}, bf16[8,48,512]{2,1,0:T(8,128)(2,1)S(1)}, u32[]{:S(2)}, u32[]{:S(2)}) %collective-permute-start.16) | collective-permute-done | bytes 393248 | tf_op jit(solution)/shard_map/ppermute | solution.py:85
  100.9 4.8 %collective-permute-done.13.refs_8_ = bf16[2,48,3072]{2,1,0:T(8,128)(2,1)S(1)} collective-permute-done((bf16[2,48,3072]{2,1,0:T(8,128)(2,1)S(1)}, bf16[2,48,3072]{2,1,0:T(8,128)(2,1)S(1)}, u32[]{:S(2)}, u32[]{:S(2)}) %collective-permute-start.13) | collective-permute-done | bytes 589856 | tf_op jit(solution)/shard_map/ppermute | solution.py:85
  106.9 1.6 %collective-permute-start.18 = (bf16[2,48,1536]{2,1,0:T(8,128)(2,1)S(1)}, bf16[2,48,1536]{2,1,0:T(8,128)(2,1)S(1)}, u32[]{:S(2)}, u32[]{:S(2)}) collective-permute-start(bf16[2,48,1536]{2,1,0:T(8,128)(2,1)S(1)} %turn.16), channel_id=1, source_target_pairs={{0,8},{1,3},{2,10},{3,1},{4,12},{5,7},{6,14},{7,5},{8,0},{9,11},{1... | collective-permute-start | bytes 884744 | tf_op jit(solution)/shard_map/ppermute | solution.py:85
  108.6 2.6 %collective-permute-start.14 = (bf16[1,48,3072]{2,1,0:T(8,128)(2,1)S(1)}, bf16[1,48,3072]{2,1,0:T(8,128)(2,1)S(1)}, u32[]{:S(2)}, u32[]{:S(2)}) collective-permute-start(bf16[1,48,3072]{2,1,0:T(8,128)(2,1)S(1)} %turn.14), channel_id=1, source_target_pairs={{0,16},{1,17},{2,18},{3,19},{4,20},{5,21},{6,22},{7,23},{8,24},{9,... | collective-permute-start | bytes 884744 | tf_op jit(solution)/shard_map/ppermute | solution.py:85
  111.1 5.3 %collective-permute-done.18.refs_5_.refs_15_ = bf16[2,48,1536]{2,1,0:T(8,128)(2,1)S(1)} collective-permute-done((bf16[2,48,1536]{2,1,0:T(8,128)(2,1)S(1)}, bf16[2,48,1536]{2,1,0:T(8,128)(2,1)S(1)}, u32[]{:S(2)}, u32[]{:S(2)}) %collective-permute-start.18) | collective-permute-done | bytes 294944 | tf_op jit(solution)/shard_map/ppermute | solution.py:85
  117.2 3.1 %input_grad.1 = (f32[512,768]{1,0:T(8,128)}, f32[1,768]{1,0:T(1,128)S(1)}) custom-call(bf16[1024,384]{1,0:T(8,128)(2,1)S(1)} %get-tuple-element.140.refs_0_, bf16[1024,384]{1,0:T(8,128)(2,1)S(1)} %get-tuple-element.151.refs_1_, bf16[1024,384]{1,0:T(8,128)(2,1)S(1)} %get-tuple-element.156.refs_2_, bf16[3,768,384]{2,1,0:T(8,128)(2,1)S(1)} %copy-done, ...), custom_call_target="tpu_custom_call" | custom-call | flops 905969664 | bytes 8388608 | tf_op jit(solution)/shard_map/input_grad/pallas_call | solution.py:587
  120.3 6.8 %collective-permute-done.14.refs_9_ = bf16[1,48,3072]{2,1,0:T(8,128)(2,1)S(1)} collective-permute-done((bf16[1,48,3072]{2,1,0:T(8,128)(2,1)S(1)}, bf16[1,48,3072]{2,1,0:T(8,128)(2,1)S(1)}, u32[]{:S(2)}, u32[]{:S(2)}) %collective-permute-start.14) | collective-permute-done | bytes 294944 | tf_op jit(solution)/shard_map/ppermute | solution.py:85
  127.0 3.2 %collective-permute-done.19.refs_16_ = bf16[1,48,1536]{2,1,0:T(8,128)(2,1)S(1)} collective-permute-done((bf16[1,48,1536]{2,1,0:T(8,128)(2,1)S(1)}, bf16[1,48,1536]{2,1,0:T(8,128)(2,1)S(1)}, u32[]{:S(2)}, u32[]{:S(2)}) %collective-permute-start.19) | collective-permute-done | bytes 147488 | tf_op jit(solution)/shard_map/ppermute | solution.py:85
  131.5 1.7 %collective-permute-start.20 = (f32[64,128]{1,0:T(8,128)S(1)}, f32[64,128]{1,0:T(8,128)S(1)}, u32[]{:S(2)}, u32[]{:S(2)}) collective-permute-start(f32[64,128]{1,0:T(8,128)S(1)} %get-tuple-element.171.own_ref), channel_id=1, source_target_pairs={{0,1},{1,0},{2,3},{3,2},{4,5},{5,4},{6,7},{7,6},{8,9},{9,8},{10,11... | collective-permute-start | bytes 98312 | tf_op jit(solution)/shard_map/ppermute | solution.py:89
  134.1 2.4 %collective-permute-start.21 = (f32[8,1024]{1,0:T(8,128)S(1)}, f32[8,1024]{1,0:T(8,128)S(1)}, u32[]{:S(2)}, u32[]{:S(2)}) collective-permute-start(f32[8,1024]{1,0:T(8,128)S(1)} %get-tuple-element.172), channel_id=1, source_target_pairs={{0,2},{1,5},{2,0},{3,7},{4,6},{5,1},{6,4},{7,3},{8,10},{9,13},{10,... | collective-permute-start | bytes 98312 | tf_op jit(solution)/shard_map/ppermute | solution.py:85
  136.5 1.9 %collective-permute-done.21 = f32[8,1024]{1,0:T(8,128)S(1)} collective-permute-done((f32[8,1024]{1,0:T(8,128)S(1)}, f32[8,1024]{1,0:T(8,128)S(1)}, u32[]{:S(2)}, u32[]{:S(2)}) %collective-permute-start.21) | collective-permute-done | bytes 32800 | tf_op jit(solution)/shard_map/ppermute | solution.py:85
  138.4 1.7 %collective-permute-start.22 = (f32[8,1024]{1,0:T(8,128)S(1)}, f32[8,1024]{1,0:T(8,128)S(1)}, u32[]{:S(2)}, u32[]{:S(2)}) collective-permute-start(f32[8,1024]{1,0:T(8,128)S(1)} %add.12), channel_id=1, source_target_pairs={{0,4},{1,9},{2,6},{3,11},{4,0},{5,13},{6,2},{7,15},{8,12},{9,1},{1... | collective-permute-start | bytes 98312 | tf_op jit(solution)/shard_map/ppermute | solution.py:85
  140.1 2.2 %collective-permute-done.22 = f32[8,1024]{1,0:T(8,128)S(1)} collective-permute-done((f32[8,1024]{1,0:T(8,128)S(1)}, f32[8,1024]{1,0:T(8,128)S(1)}, u32[]{:S(2)}, u32[]{:S(2)}) %collective-permute-start.22) | collective-permute-done | bytes 32800 | tf_op jit(solution)/shard_map/ppermute | solution.py:85
  143.6 2.6 %collective-permute-done.23 = f32[8,1024]{1,0:T(8,128)S(1)} collective-permute-done((f32[8,1024]{1,0:T(8,128)S(1)}, f32[8,1024]{1,0:T(8,128)S(1)}, u32[]{:S(2)}, u32[]{:S(2)}) %collective-permute-start.23) | collective-permute-done | bytes 32800 | tf_op jit(solution)/shard_map/ppermute | solution.py:85
  147.0 4.1 %collective-permute-done.24 = f32[8,1024]{1,0:T(8,128)S(1)} collective-permute-done((f32[8,1024]{1,0:T(8,128)S(1)}, f32[8,1024]{1,0:T(8,128)S(1)}, u32[]{:S(2)}, u32[]{:S(2)}) %collective-permute-start.24) | collective-permute-done | bytes 32800 | tf_op jit(solution)/shard_map/ppermute | solution.py:85
  151.1 2.6 %update.1 = (bf16[3,48,384]{2,1,0:T(8,128)(2,1)}, bf16[48,384]{1,0:T(8,128)(2,1)}, bf16[2,48,1024]{2,1,0:T(8,128)(2,1)}, bf16[48,1024]{1,0:T(8,128)(2,1)}, f32[3...) custom-call(f32[128]{0:T(128)S(1)} %compare_select_fusion.refs_0_, ...), custom_call_target="tpu_custom_call" | custom-call | flops 1048576 | bytes 4194304 | tf_op jit(solution)/shard_map/update/pallas_call | solution.py:785
  (85 shorter events, 20.5 us)
Async XLA Ops:
  0.7 4.1 %collective-permute-start = (bf16[512,768]{1,0:T(8,128)(2,1)}, bf16[512,768]{1,0:T(8,128)(2,1)S(1)}, u32[]{:S(2)}, u32[]{:S(2)}) collective-permute-start(bf16[512,768]{1,0:T(8,128)(2,1)} %refs_5_.3), channel_id=1, source_target_pairs={{0,1},{1,0},{2,3},{3,2},{4,5},{5,4},{6,7},{7,6},{8,9},{9,8},{10,11... | collective-permute-start | bytes 2359304 | tf_op jit(solution)/shard_map/ppermute | solution.py:89
  4.8 16.4 %collective-permute-start.3 = (bf16[2,768,1024]{2,1,0:T(8,128)(2,1)}, bf16[2,768,1024]{2,1,0:T(8,128)(2,1)S(1)}, u32[]{:S(2)}, u32[]{:S(2)}) collective-permute-start(bf16[2,768,1024]{2,1,0:T(8,128)(2,1)} %gu_ref), channel_id=1, source_target_pairs={{0,1},{1,0},{2,3},{3,2},{4,5},{5,4},{6,7},{7,6},{8,9},{9,8},{10,11... | collective-permute-start | bytes 9437192 | tf_op jit(solution)/shard_map/ppermute | solution.py:89
  5.0 16.3 %collective-permute-start.4 = (bf16[1024,768]{1,0:T(8,128)(2,1)S(1)}, bf16[1024,768]{1,0:T(8,128)(2,1)S(1)}, u32[]{:S(2)}, u32[]{:S(2)}) collective-permute-start(bf16[1024,768]{1,0:T(8,128)(2,1)S(1)} %copy-done.2), channel_id=1, source_target_pairs={{0,1},{1,0},{2,3},{3,2},{4,5},{5,4},{6,7},{7,6},{8,9},{9,8},{10,11... | collective-permute-start | bytes 4718600 | tf_op jit(solution)/shard_map/ppermute | solution.py:89
  5.4 15.9 %collective-permute-start.2 = (bf16[384,768]{1,0:T(8,128)(2,1)}, bf16[384,768]{1,0:T(8,128)(2,1)S(1)}, u32[]{:S(2)}, u32[]{:S(2)}) collective-permute-start(bf16[384,768]{1,0:T(8,128)(2,1)} %out_ref), channel_id=1, source_target_pairs={{0,1},{1,0},{2,3},{3,2},{4,5},{5,4},{6,7},{7,6},{8,9},{9,8},{10,11... | collective-permute-start | bytes 1769480 | tf_op jit(solution)/shard_map/ppermute | solution.py:89
  7.2 14.0 %copy-start.3 = (bf16[512,768]{1,0:T(8,128)(2,1)S(1)}, bf16[512,768]{1,0:T(8,128)(2,1)}, u32[]{:S(2)}) copy-start(bf16[512,768]{1,0:T(8,128)(2,1)} %refs_5_.3) | copy-start | bytes 2359300
  19.4 1.8 %collective-permute-start.1 = (bf16[512,384]{1,0:T(8,128)(2,1)S(1)}, bf16[512,384]{1,0:T(8,128)(2,1)S(1)}, u32[]{:S(2)}, u32[]{:S(2)}) collective-permute-start(bf16[512,384]{1,0:T(8,128)(2,1)S(1)} %get-tuple-element.110.refs_3_), channel_id=1, source_target_pairs={{0,1},{1,0},{2,3},{3,2},{4,5},{5,4},{6,7},{7,6},{8,9},{9,8},{10,11... | collective-permute-start | bytes 1179656 | tf_op jit(solution)/shard_map/ppermute | solution.py:89
  28.1 6.0 %collective-permute-start.5 = (bf16[16,48,1536]{2,1,0:T(8,128)(2,1)S(1)}, bf16[16,48,1536]{2,1,0:T(8,128)(2,1)S(1)}, u32[]{:S(2)}, u32[]{:S(2)}) collective-permute-start(bf16[16,48,1536]{2,1,0:T(8,128)(2,1)S(1)} %get-tuple-element.122), channel_id=1, source_target_pairs={{0,1},{1,0},{2,3},{3,2},{4,5},{5,4},{6,7},{7,6},{8,9},{9,8},{10,11... | collective-permute-start | bytes 7077896 | tf_op jit(solution)/shard_map/ppermute | solution.py:89
  34.4 16.8 %collective-permute-start.6 = (bf16[8,48,1536]{2,1,0:T(8,128)(2,1)S(1)}, bf16[8,48,1536]{2,1,0:T(8,128)(2,1)S(1)}, u32[]{:S(2)}, u32[]{:S(2)}) collective-permute-start(bf16[8,48,1536]{2,1,0:T(8,128)(2,1)S(1)} %turn.9), channel_id=1, source_target_pairs={{0,2},{1,5},{2,0},{3,7},{4,6},{5,1},{6,4},{7,3},{8,10},{9,13},{10,... | collective-permute-start | bytes 3538952 | tf_op jit(solution)/shard_map/ppermute | solution.py:85
  42.7 12.1 %collective-permute-start.8 = (bf16[16,48,1536]{2,1,0:T(8,128)(2,1)S(1)}, bf16[16,48,1536]{2,1,0:T(8,128)(2,1)S(1)}, u32[]{:S(2)}, u32[]{:S(2)}) collective-permute-start(bf16[16,48,1536]{2,1,0:T(8,128)(2,1)S(1)} %get-tuple-element.134), channel_id=1, source_target_pairs={{0,1},{1,0},{2,3},{3,2},{4,5},{5,4},{6,7},{7,6},{8,9},{9,8},{10,11... | collective-permute-start | bytes 7077896 | tf_op jit(solution)/shard_map/ppermute | solution.py:89
  51.4 2.4 %collective-permute-start.7 = (bf16[512,768]{1,0:T(8,128)(2,1)S(1)}, bf16[512,768]{1,0:T(8,128)(2,1)S(1)}, u32[]{:S(2)}, u32[]{:S(2)}) collective-permute-start(bf16[512,768]{1,0:T(8,128)(2,1)S(1)} %get-tuple-element.131.own_ref), channel_id=1, source_target_pairs={{0,1},{1,0},{2,3},{3,2},{4,5},{5,4},{6,7},{7,6},{8,9},{9,8},{10,11... | collective-permute-start | bytes 2359304 | tf_op jit(solution)/shard_map/ppermute | solution.py:89
  51.5 34.9 %collective-permute-start.11 = (bf16[4,48,1536]{2,1,0:T(8,128)(2,1)S(1)}, bf16[4,48,1536]{2,1,0:T(8,128)(2,1)S(1)}, u32[]{:S(2)}, u32[]{:S(2)}) collective-permute-start(bf16[4,48,1536]{2,1,0:T(8,128)(2,1)S(1)} %turn.10), channel_id=1, source_target_pairs={{0,4},{1,3},{2,6},{3,1},{4,0},{5,7},{6,2},{7,5},{8,12},{9,11},{10,... | collective-permute-start | bytes 1769480 | tf_op jit(solution)/shard_map/ppermute | solution.py:85
  55.1 19.6 %collective-permute-start.9 = (bf16[8,48,1536]{2,1,0:T(8,128)(2,1)S(1)}, bf16[8,48,1536]{2,1,0:T(8,128)(2,1)S(1)}, u32[]{:S(2)}, u32[]{:S(2)}) collective-permute-start(bf16[8,48,1536]{2,1,0:T(8,128)(2,1)S(1)} %turn.11), channel_id=1, source_target_pairs={{0,2},{1,5},{2,0},{3,7},{4,6},{5,1},{6,4},{7,3},{8,10},{9,13},{10,... | collective-permute-start | bytes 3538952 | tf_op jit(solution)/shard_map/ppermute | solution.py:85
  74.9 16.2 %collective-permute-start.12 = (bf16[4,48,1536]{2,1,0:T(8,128)(2,1)S(1)}, bf16[4,48,1536]{2,1,0:T(8,128)(2,1)S(1)}, u32[]{:S(2)}, u32[]{:S(2)}) collective-permute-start(bf16[4,48,1536]{2,1,0:T(8,128)(2,1)S(1)} %turn.12), channel_id=1, source_target_pairs={{0,4},{1,3},{2,6},{3,1},{4,0},{5,7},{6,2},{7,5},{8,12},{9,11},{10,... | collective-permute-start | bytes 1769480 | tf_op jit(solution)/shard_map/ppermute | solution.py:85
  76.5 19.9 %collective-permute-start.15 = (bf16[8,48,1024]{2,1,0:T(8,128)(2,1)S(1)}, bf16[8,48,1024]{2,1,0:T(8,128)(2,1)S(1)}, u32[]{:S(2)}, u32[]{:S(2)}) collective-permute-start(bf16[8,48,1024]{2,1,0:T(8,128)(2,1)S(1)} %get-tuple-element.154), channel_id=1, source_target_pairs={{0,2},{1,5},{2,0},{3,7},{4,6},{5,1},{6,4},{7,3},{8,10},{9,13},{10,... | collective-permute-start | bytes 2359304 | tf_op jit(solution)/shard_map/ppermute | solution.py:85
  85.1 11.3 %collective-permute-start.16 = (bf16[8,48,512]{2,1,0:T(8,128)(2,1)S(1)}, bf16[8,48,512]{2,1,0:T(8,128)(2,1)S(1)}, u32[]{:S(2)}, u32[]{:S(2)}) collective-permute-start(bf16[8,48,512]{2,1,0:T(8,128)(2,1)S(1)} %get-tuple-element.161), channel_id=1, source_target_pairs={{0,2},{1,5},{2,0},{3,7},{4,6},{5,1},{6,4},{7,3},{8,10},{9,13},{10,... | collective-permute-start | bytes 1179656 | tf_op jit(solution)/shard_map/ppermute | solution.py:85
  91.4 14.3 %collective-permute-start.13 = (bf16[2,48,3072]{2,1,0:T(8,128)(2,1)S(1)}, bf16[2,48,3072]{2,1,0:T(8,128)(2,1)S(1)}, u32[]{:S(2)}, u32[]{:S(2)}) collective-permute-start(bf16[2,48,3072]{2,1,0:T(8,128)(2,1)S(1)} %turn.13), channel_id=1, source_target_pairs={{0,8},{1,9},{2,10},{3,11},{4,12},{5,13},{6,14},{7,15},{8,0},{9,1},... | collective-permute-start | bytes 1769480 | tf_op jit(solution)/shard_map/ppermute | solution.py:85
  96.8 9.9 %collective-permute-start.17 = (bf16[4,48,1536]{2,1,0:T(8,128)(2,1)S(1)}, bf16[4,48,1536]{2,1,0:T(8,128)(2,1)S(1)}, u32[]{:S(2)}, u32[]{:S(2)}) collective-permute-start(bf16[4,48,1536]{2,1,0:T(8,128)(2,1)S(1)} %turn.15), channel_id=1, source_target_pairs={{0,4},{1,9},{2,6},{3,11},{4,0},{5,13},{6,2},{7,15},{8,12},{9,1},{1... | collective-permute-start | bytes 1769480 | tf_op jit(solution)/shard_map/ppermute | solution.py:85
  99.7 17.5 %collective-permute-start.10 = (bf16[512,768]{1,0:T(8,128)(2,1)S(1)}, bf16[512,768]{1,0:T(8,128)(2,1)S(1)}, u32[]{:S(2)}, u32[]{:S(2)}) collective-permute-start(bf16[512,768]{1,0:T(8,128)(2,1)S(1)} %input_other.1), channel_id=1, source_target_pairs={{0,1},{1,0},{2,3},{3,2},{4,5},{5,4},{6,7},{7,6},{8,9},{9,8},{10,11... | collective-permute-start | bytes 2359304 | tf_op jit(solution)/shard_map/ppermute | solution.py:89
  106.9 9.6 %collective-permute-start.18 = (bf16[2,48,1536]{2,1,0:T(8,128)(2,1)S(1)}, bf16[2,48,1536]{2,1,0:T(8,128)(2,1)S(1)}, u32[]{:S(2)}, u32[]{:S(2)}) collective-permute-start(bf16[2,48,1536]{2,1,0:T(8,128)(2,1)S(1)} %turn.16), channel_id=1, source_target_pairs={{0,8},{1,3},{2,10},{3,1},{4,12},{5,7},{6,14},{7,5},{8,0},{9,11},{1... | collective-permute-start | bytes 884744 | tf_op jit(solution)/shard_map/ppermute | solution.py:85
  108.6 18.5 %collective-permute-start.14 = (bf16[1,48,3072]{2,1,0:T(8,128)(2,1)S(1)}, bf16[1,48,3072]{2,1,0:T(8,128)(2,1)S(1)}, u32[]{:S(2)}, u32[]{:S(2)}) collective-permute-start(bf16[1,48,3072]{2,1,0:T(8,128)(2,1)S(1)} %turn.14), channel_id=1, source_target_pairs={{0,16},{1,17},{2,18},{3,19},{4,20},{5,21},{6,22},{7,23},{8,24},{9,... | collective-permute-start | bytes 884744 | tf_op jit(solution)/shard_map/ppermute | solution.py:85
  116.6 13.6 %collective-permute-start.19 = (bf16[1,48,1536]{2,1,0:T(8,128)(2,1)S(1)}, bf16[1,48,1536]{2,1,0:T(8,128)(2,1)S(1)}, u32[]{:S(2)}, u32[]{:S(2)}) collective-permute-start(bf16[1,48,1536]{2,1,0:T(8,128)(2,1)S(1)} %turn.17), channel_id=1, source_target_pairs={{0,16},{1,17},{2,18},{3,19},{4,20},{5,21},{6,22},{7,23},{8,24},{9,... | collective-permute-start | bytes 442376 | tf_op jit(solution)/shard_map/ppermute | solution.py:85
  130.2 20.9 %copy-start.7 = (f32[3,768]{1,0:T(4,128)S(1)}, f32[3,768]{1,0:T(4,128)}, u32[]{:S(2)}) copy-start(f32[3,768]{1,0:T(4,128)} %refs_7_.5) | copy-start | bytes 27652
  130.2 20.9 %copy-start.8 = (f32[2,1024]{1,0:T(2,128)S(1)}, f32[2,1024]{1,0:T(2,128)}, u32[]{:S(2)}) copy-start(f32[2,1024]{1,0:T(2,128)} %refs_13_.1) | copy-start | bytes 24580
  130.2 20.9 %copy-start.10 = (f32[2,768]{1,0:T(2,128)S(1)}, f32[2,768]{1,0:T(2,128)}, u32[]{:S(2)}) copy-start(f32[2,768]{1,0:T(2,128)} %refs_9_.3) | copy-start | bytes 18436
  130.2 20.9 %copy-start.11 = (f32[3,384]{1,0:T(4,128)S(1)}, f32[3,384]{1,0:T(4,128)}, u32[]{:S(2)}) copy-start(f32[3,384]{1,0:T(4,128)} %refs_11_.1) | copy-start | bytes 13828
  130.2 20.9 %copy-start.13 = (f32[768]{0:T(1024)S(1)}, f32[768]{0:T(1024)}, u32[]{:S(2)}) copy-start(f32[768]{0:T(1024)} %refs_8_.3) | copy-start | bytes 9220
  130.2 20.9 %copy-start.14 = (f32[768]{0:T(1024)S(1)}, f32[768]{0:T(1024)}, u32[]{:S(2)}) copy-start(f32[768]{0:T(1024)} %refs_10_.1) | copy-start | bytes 9220
  131.5 2.5 %collective-permute-start.20 = (f32[64,128]{1,0:T(8,128)S(1)}, f32[64,128]{1,0:T(8,128)S(1)}, u32[]{:S(2)}, u32[]{:S(2)}) collective-permute-start(f32[64,128]{1,0:T(8,128)S(1)} %get-tuple-element.171.own_ref), channel_id=1, source_target_pairs={{0,1},{1,0},{2,3},{3,2},{4,5},{5,4},{6,7},{7,6},{8,9},{9,8},{10,11... | collective-permute-start | bytes 98312 | tf_op jit(solution)/shard_map/ppermute | solution.py:89
  134.1 4.3 %collective-permute-start.21 = (f32[8,1024]{1,0:T(8,128)S(1)}, f32[8,1024]{1,0:T(8,128)S(1)}, u32[]{:S(2)}, u32[]{:S(2)}) collective-permute-start(f32[8,1024]{1,0:T(8,128)S(1)} %get-tuple-element.172), channel_id=1, source_target_pairs={{0,2},{1,5},{2,0},{3,7},{4,6},{5,1},{6,4},{7,3},{8,10},{9,13},{10,... | collective-permute-start | bytes 98312 | tf_op jit(solution)/shard_map/ppermute | solution.py:85
  138.4 3.9 %collective-permute-start.22 = (f32[8,1024]{1,0:T(8,128)S(1)}, f32[8,1024]{1,0:T(8,128)S(1)}, u32[]{:S(2)}, u32[]{:S(2)}) collective-permute-start(f32[8,1024]{1,0:T(8,128)S(1)} %add.12), channel_id=1, source_target_pairs={{0,4},{1,9},{2,6},{3,11},{4,0},{5,13},{6,2},{7,15},{8,12},{9,1},{1... | collective-permute-start | bytes 98312 | tf_op jit(solution)/shard_map/ppermute | solution.py:85
  142.3 3.9 %collective-permute-start.23 = (f32[8,1024]{1,0:T(8,128)S(1)}, f32[8,1024]{1,0:T(8,128)S(1)}, u32[]{:S(2)}, u32[]{:S(2)}) collective-permute-start(f32[8,1024]{1,0:T(8,128)S(1)} %add.13), channel_id=1, source_target_pairs={{0,8},{1,3},{2,10},{3,1},{4,12},{5,7},{6,14},{7,5},{8,0},{9,11},{1... | collective-permute-start | bytes 98312 | tf_op jit(solution)/shard_map/ppermute | solution.py:85
  146.3 4.8 %collective-permute-start.24 = (f32[8,1024]{1,0:T(8,128)S(1)}, f32[8,1024]{1,0:T(8,128)S(1)}, u32[]{:S(2)}, u32[]{:S(2)}) collective-permute-start(f32[8,1024]{1,0:T(8,128)S(1)} %add.14), channel_id=1, source_target_pairs={{0,16},{1,17},{2,18},{3,19},{4,20},{5,21},{6,22},{7,23},{8,24},{9,... | collective-permute-start | bytes 98312 | tf_op jit(solution)/shard_map/ppermute | solution.py:85
  (11 other events, 84.0 us)
